TPU v7x, 32 devices: a whole 2x2x4 slice. The times are simulated.
32 devices in a mesh: sx: 4 (over z), sy: 4 (over x, core), gz: 2 (over y).
Axes of the slice: x: 2, y: 2, z: 4, core: 2. Of those that a mesh axis runs over, the one named last changes fastest.
Arguments:
- observed: float32 [512, 64, 512], P('gz', 'sx', 'sy'), may hold values from 0.25 to 2
- zone_of_slice: int32 [512], P('gz'), may hold values from 0 to 7
- lateral_x: float32 [8, 7], replicated, may hold values from 0.05 to 1
- lateral_y: float32 [8, 7], replicated, may hold values from 0.05 to 1
- depth_psf: float32 [17], replicated, may hold values from 0.05 to 1
- stitch_width: int32 [4, 4, 2], replicated, may hold values from 1 to 8
Outputs:
- estimate: float32 [512, 64, 512], P('gz', 'sx', 'sy')
All inputs are finite; a program needn't handle non-finite values.
Results may differ from a plain program's by a relative error of at most 0.0001.
Values sent between devices are 32-bit elements; how exact they have to be, the bound alone decides.
No kernel may reach another device: no remote copies, remote signals or barrier semaphores. Data moves between devices by JAX's collectives and lax.ppermute only.
A program may use at most 64 MiB of HBM per device.

v0:
```python
import functools

import jax
import jax.numpy as jnp
from jax import lax
from jax.experimental import pallas as pl
from jax.experimental.pallas import tpu as pltpu
from jax.sharding import PartitionSpec as P

ITERS = 2
LANES = 128
TINY = 1e-30
VMEM = pl.BlockSpec(memory_space=pltpu.VMEM)


def ceil_to(value, unit):
    return -(-value // unit) * unit


def line(axis):
    count = lax.axis_size(axis)
    up = [(i, i + 1) for i in range(count - 1)]
    return up, [(j, i) for i, j in up]


def x_conv(src, dst, taps, reverse, t, width, blocks):
    count = taps.shape[1]
    k = [taps[t, count - 1 - a if reverse else a] for a in range(count)]

    def step(j, carry):
        rows = pl.ds(pl.multiple_of(8 * j, 8), 8)
        v = [src[t, x, rows, :] for x in range(width + count - 1)]
        for x in range(width):
            acc = k[0] * v[x]
            for a in range(1, count):
                acc = acc + k[a] * v[x + a]
            dst[t, x, rows, :] = acc
        return carry

    lax.fori_loop(0, blocks, step, 0)


def y_conv(src, taps, reverse, t, width, blocks, emit):
    count = taps.shape[1]
    k = [taps[t, count - 1 - b if reverse else b] for b in range(count)]

    def step(x, carry):
        for j in range(blocks):
            acc = k[0] * src[t, x, 8 * j : 8 * j + 8, :]
            for b in range(1, count):
                acc = acc + k[b] * src[t, x, 8 * j + b : 8 * j + b + 8, :]
            emit(t, x, j, acc)
        return carry

    lax.fori_loop(0, width, step, 0)


def windows_of(tiles):
    return [(0, tiles)] if tiles <= 2 else [(w, 2) for w in range(tiles - 1)]


def depth_rows(parts, hi_ref, lo_ref):
    tiles = len(parts)
    split = []
    for part in parts:
        hi = part.astype(jnp.bfloat16)
        split.append((hi, (part - hi.astype(jnp.float32)).astype(jnp.bfloat16)))
    out = [None] * tiles
    for index, (first, span) in enumerate(windows_of(tiles)):
        his = jnp.concatenate([split[first + s][0] for s in range(span)], axis=1)
        los = jnp.concatenate([split[first + s][1] for s in range(span)], axis=1)
        dot = functools.partial(jnp.dot, preferred_element_type=jnp.float32)
        res = dot(his, hi_ref[index]) + (dot(los, hi_ref[index]) + dot(his, lo_ref[index]))
        for s in range(span):
            piece = res[:, s * LANES : (s + 1) * LANES]
            out[first + s] = piece if out[first + s] is None else out[first + s] + piece
    return out


def norm_kernel(w_ref, tx_ref, ty_ref, out_ref, mid_ref):
    tiles = tx_ref.shape[0]
    width = out_ref.shape[1]
    blocks = out_ref.shape[2] // 8
    count = tx_ref.shape[1]
    for t in range(tiles):
        k = [tx_ref[t, count - 1 - a] for a in range(count)]

        def step(j, carry, k=k):
            rows = pl.ds(pl.multiple_of(8 * j, 8), 8)
            v = [w_ref[x, rows, :] for x in range(width + count - 1)]
            for x in range(width):
                acc = k[0] * v[x]
                for a in range(1, count):
                    acc = acc + k[a] * v[x + a]
                mid_ref[0, x, rows, :] = acc
            return carry

        lax.fori_loop(0, mid_ref.shape[2] // 8, step, 0)
        ky = [ty_ref[t, count - 1 - b] for b in range(count)]

        def ystep(x, carry, ky=ky, t=t):
            for j in range(blocks):
                acc = ky[0] * mid_ref[0, x, 8 * j : 8 * j + 8, :]
                for b in range(1, count):
                    acc = acc + ky[b] * mid_ref[0, x, 8 * j + b : 8 * j + b + 8, :]
                out_ref[t, x, 8 * j : 8 * j + 8, :] = 1.0 / jnp.maximum(acc, TINY)
            return carry

        lax.fori_loop(0, width, ystep, 0)


def iterate_kernel(dy, need, est_ref, obs_ref, w_ref, inv_ref, tx_ref, ty_ref, fh_ref, fl_ref, bh_ref, bl_ref, out_ref, mid_ref, blur_ref):
    tiles = est_ref.shape[0]
    reach = (tx_ref.shape[1] - 1) // 2
    wide = blur_ref.shape[1]
    rows = blur_ref.shape[2]
    width = out_ref.shape[1]
    blocks = out_ref.shape[2] // 8

    def put(t, x, j, acc):
        blur_ref[t, x, 8 * j : 8 * j + 8, :] = acc

    for t in range(tiles):
        x_conv(est_ref, mid_ref, tx_ref, False, t, wide, -(-need // 8))
        y_conv(mid_ref, ty_ref, False, t, wide, rows // 8, put)

    def depth(i, carry):
        spot = pl.ds(2 * i, 2)
        size = 2 * rows
        parts = [blur_ref[t, spot].reshape(size, LANES) for t in range(tiles)]
        blurred = depth_rows(parts, fh_ref, fl_ref)
        weight = w_ref[spot, dy : dy + rows, :].reshape(size, LANES)
        ratio = []
        for t in range(tiles):
            seen = obs_ref[t, pl.ds(2 * i + reach, 2), dy + reach : dy + reach + rows, :].reshape(size, LANES)
            ratio.append(weight * seen / jnp.maximum(blurred[t], TINY))
        spread = depth_rows(ratio, bh_ref, bl_ref)
        for t in range(tiles):
            blur_ref[t, spot] = spread[t].reshape(2, rows, LANES)
        return carry

    lax.fori_loop(0, wide // 2, depth, 0)

    def finish(t, x, j, acc):
        old = est_ref[t, x + 2 * reach, 8 * j + 2 * reach : 8 * j + 2 * reach + 8, :]
        out_ref[t, x, 8 * j : 8 * j + 8, :] = old * acc * inv_ref[t, x, 8 * j + dy : 8 * j + dy + 8, :]

    for t in range(tiles):
        x_conv(blur_ref, mid_ref, tx_ref, True, t, width, rows // 8)
        y_conv(mid_ref, ty_ref, True, t, width, blocks, finish)


def body(observed, zone_of_slice, lateral_x, lateral_y, depth_psf, stitch_width):
    nz, cx, cy = observed.shape
    taps = lateral_x.shape[1]
    reach = (taps - 1) // 2
    zreach = (depth_psf.shape[0] - 1) // 2
    hz = 2 * zreach * ITERS
    hy = 2 * reach * ITERS
    hx = 2 * reach
    slabs = lax.axis_size("gz")
    tiles = ceil_to(nz + 2 * hz, LANES) // LANES
    f32 = jnp.float32

    zones = zone_of_slice.astype(f32)

    def with_zones(part, ids):
        flat = jnp.pad(ids, (0, cx * cy - ids.shape[0]))
        return jnp.concatenate([part, flat.reshape(1, cx, cy)], axis=0)

    if slabs == 2:
        both = jnp.concatenate([observed[nz - hz :], observed[:hz]], axis=0)
        got = lax.ppermute(with_zones(both, jnp.concatenate([zones[nz - hz :], zones[:hz]])), "gz", [(0, 1), (1, 0)])
        before, after = got[:hz], got[hz : 2 * hz]
        got_ids = got[2 * hz].reshape(-1)
        ids_before, ids_after = got_ids[:hz], got_ids[hz : 2 * hz]
    else:
        up = [(i, (i + 1) % slabs) for i in range(slabs)]
        first = lax.ppermute(with_zones(observed[nz - hz :], zones[nz - hz :]), "gz", up)
        second = lax.ppermute(with_zones(observed[:hz], zones[:hz]), "gz", [(j, i) for i, j in up])
        before, after = first[:hz], second[:hz]
        ids_before, ids_after = first[hz].reshape(-1)[:hz], second[hz].reshape(-1)[:hz]
    pad = tiles * LANES - nz - 2 * hz
    volume = jnp.concatenate([before, observed, after, jnp.zeros((pad, cx, cy), f32)], axis=0)
    ids = jnp.concatenate([ids_before, zones, ids_after, jnp.full((pad,), -1.0, f32)])
    volume = volume.reshape(tiles, LANES, cx, cy).transpose(0, 2, 3, 1)

    match = (ids[None, :] == jnp.arange(lateral_x.shape[0], dtype=f32)[:, None]).astype(f32)

    def lanes_of(kernels):
        table = jnp.sum(match[:, None, :] * kernels[:, :, None], axis=0)
        table = table.reshape(taps, tiles, 1, LANES).transpose(1, 0, 2, 3)
        return jnp.broadcast_to(table, (tiles, taps, 8, LANES))

    tx, ty = lanes_of(lateral_x), lanes_of(lateral_y)

    kernel = depth_psf / jnp.sum(depth_psf)
    wins = windows_of(tiles)
    size = wins[0][1] * LANES
    off = jnp.arange(size)[None, :] - jnp.arange(size)[:, None]
    band = jnp.zeros((size, size), f32)
    flip = jnp.zeros((size, size), f32)
    for j in range(kernel.shape[0]):
        band = band + jnp.where(off == j - zreach, kernel[j], 0.0)
        flip = flip + jnp.where(off == zreach - j, kernel[j], 0.0)

    def halves(matrix):
        cols = jnp.arange(size)
        parts = []
        for index in range(len(wins)):
            low = 0 if index == 0 else LANES // 2
            high = size if index == len(wins) - 1 else LANES + LANES // 2
            parts.append(jnp.where((cols >= low) & (cols < high), matrix, 0.0))
        full = jnp.stack(parts)
        top = lax.reduce_precision(full, 8, 7)
        return top.astype(jnp.bfloat16), (full - top).astype(jnp.bfloat16)

    fh, fl = halves(band)
    bh, bl = halves(flip)

    sx, sy = lax.axis_index("sx"), lax.axis_index("sy")
    stacks_x, stacks_y = stitch_width.shape[:2]
    rows1 = ceil_to(cy + 2 * hy - 2 * reach, 8)
    gx = sx * cx - reach + jnp.arange(cx + 2 * reach)
    gy = sy * cy - (hy - reach) + jnp.arange(rows1)
    near = lax.dynamic_slice(jnp.pad(stitch_width, ((1, 1), (1, 1), (0, 0))), (sx, sy, jnp.int32(0)), (3, 3, 2))
    of_x = gx // cx - sx + 1
    of_y = gy // cy - sy + 1
    bands = jnp.zeros((2, gx.shape[0], rows1), jnp.int32)
    for a in range(3):
        for b in range(3):
            hit = (of_x[:, None] == a) & (of_y[None, :] == b)
            bands = jnp.where(hit[None], near[a, b][:, None, None], bands)
    inside = ((gx >= 0) & (gx < stacks_x * cx))[:, None] & ((gy >= 0) & (gy < stacks_y * cy))[None, :]
    weight = jnp.where((gx % cx)[:, None] < bands[0], 0.5, 1.0) * jnp.where((gy % cy)[None, :] < bands[1], 0.5, 1.0)
    weight = jnp.where(inside, weight, 0.0).astype(f32)
    weight = jnp.broadcast_to(weight[:, :, None], (cx + 2 * reach, rows1, LANES))

    rows_est1 = ceil_to(cy + 2 * hy - 4 * reach, 8)
    rows_mid = ceil_to(rows1 + 2 * reach, 8)
    inv = pl.pallas_call(
        norm_kernel,
        out_shape=jax.ShapeDtypeStruct((tiles, cx, rows_est1, LANES), f32),
        in_specs=[VMEM] * 3,
        out_specs=VMEM,
        scratch_shapes=[pltpu.VMEM((1, cx, rows1, LANES), f32)],
        name="norm",
    )(weight, tx, ty)

    up, down = line("sy")
    low = lax.ppermute(volume[:, :, cy - hy :].reshape(tiles, cx * hy, LANES), "sy", up)
    high = lax.ppermute(volume[:, :, :hy].reshape(tiles, cx * hy, LANES), "sy", down)
    volume = [low.reshape(tiles, cx, hy, LANES), volume, high.reshape(tiles, cx, hy, LANES)]
    spare = ceil_to(rows1 + reach, 8) - cy - 2 * hy
    volume = jnp.concatenate(volume + [jnp.zeros((tiles, cx, spare, LANES), f32)], axis=2)

    def x_halo(value):
        up, down = line("sx")
        low = lax.ppermute(value[:, cx - hx :], "sx", up)
        high = lax.ppermute(value[:, :hx], "sx", down)
        return jnp.concatenate([low, value, high], axis=1)

    estimate = x_halo(volume)
    seen = estimate
    for step in range(ITERS):
        dy = 2 * reach * step
        if step:
            estimate = x_halo(estimate)
        need = cy + 2 * (hy - dy)
        rows_blur = ceil_to(need - 2 * reach, 8)
        rows_out = ceil_to(need - 4 * reach, 8)
        wide = cx + 2 * reach
        estimate = pl.pallas_call(
            functools.partial(iterate_kernel, dy, need),
            out_shape=jax.ShapeDtypeStruct((tiles, cx, rows_out, LANES), f32),
            in_specs=[VMEM] * 10,
            out_specs=VMEM,
            scratch_shapes=[
                pltpu.VMEM((tiles, wide, rows_mid, LANES), f32),
                pltpu.VMEM((tiles, wide, rows_blur, LANES), f32),
            ],
            name="iterate",
        )(estimate, seen, weight, inv, tx, ty, fh, fl, bh, bl)
    result = estimate.transpose(0, 3, 1, 2).reshape(tiles * LANES, cx, cy)
    return result[hz : hz + nz]


def solution(mesh):
    in_specs = (P("gz", "sx", "sy"), P("gz"), P(), P(), P(), P())
    out_specs = P("gz", "sx", "sy")
    return jax.shard_map(body, mesh=mesh, in_specs=in_specs, out_specs=out_specs, check_vma=False)
```

profile of v0, /device:TPU:0, one launch (start us, length us, event | category | flops | bytes accessed | tf_op | source)
XLA Modules:
  0.0 193.9 jit_solution(17021082616886933562)
XLA Ops:
  2.7 3.1 %collective-permute-start = (f32[65,16,128]{2,1,0:T(8,128)S(1)}, f32[65,16,128]{2,1,0:T(8,128)S(1)}, u32[]{:S(2)}, u32[]{:S(2)}) collective-permute-start(f32[65,16,128]{2,1,0:T(8,128)S(1)} %pad_maximum_fusion.6), channel_id=1, source_target_pairs={{0,1},{1,0},{2,3},{3,2},{4,5},{5,4},{6,7},{7,6},{8,9},{9,8},{10,11... | collective-permute-start | bytes 1597448 | tf_op jit(solution)/shard_map/ppermute | solution.py:173
  14.7 1.7 fusion.41
  16.5 12.0 %broadcast_select_fusion = (f32[1,256,256]{2,1,0:T(8,128)S(1)}, f32[1,256,256]{2,1,0:T(8,128)}, f32[1,256,256]{2,1,0:T(8,128)}, f32[1,256,256]{2,1,0:T(8,128)S(1)}) fusion(f32[]{:T(128)} %bitcast.28, f32[]{:T(128)} %bitcast.27, f32[]{:T(128)} %bitcast.26, f32[]{:T(128)} %bitcast.25, f32[]{:T(128)} %bitcast.24, f32[]{:T(128)} %bitcast.23, f32[]{:T(128)} %bitcast.22, ...), kind=kLoop, calls=%fused_computation.52 | loop fusion | flops 5701632 | bytes 1049156 | tf_op jit(solution)/shard_map/jit(_where)/select_n | solution.py:213
  29.4 3.3 %maximum_maximum_fusion = f32[384,16,128]{2,1,0:T(8,128)} fusion(f32[32,16,128]{2,1,0:T(8,128)S(1)} %get-tuple-element.25, f32[256,16,128]{2,1,0:T(8,128)S(1)} %copy-done.1, f32[32,16,128]{2,1,0:T(8,128)S(1)} %get-tuple-element.24, f32[384]{0:T(512)S(1)} %pad.34.clone), kind=kLoop, calls=%fused_computation.2 | loop fusion | flops 2359296 | bytes 5768704 | tf_op jit(solution)/shard_map/concatenate | solution.py:184
  32.6 2.4 %copy.15 = f32[3,128,16,128]{1,3,2,0:T(8,128)S(1)} copy(f32[3,128,16,128]{3,2,1,0:T(8,128)} %bitcast.51) | data formatting | bytes 6291456 | tf_op jit(solution)/shard_map/reshape | solution.py:186
  35.8 1.7 reshape.841
  39.6 3.7 %collective-permute-start.1 = (f32[3,192,128]{2,1,0:T(8,128)}, f32[3,192,128]{2,1,0:T(8,128)}, u32[]{:S(2)}, u32[]{:S(2)}) collective-permute-start(f32[3,192,128]{2,1,0:T(8,128)} %reshape.841), channel_id=1, source_target_pairs={{0,2},{2,4},{4,6},{1,3},{3,5},{5,7},{8,10},{10,12},{12,14},{9,11},... | collective-permute-start | bytes 884744 | tf_op jit(solution)/shard_map/ppermute | solution.py:251
  46.4 1.7 reshape.842
  48.4 3.1 %pad_maximum_fusion.5 = (f32[3,6,160,128]{3,2,1,0:T(8,128)}, f32[3,6,160,128]{3,2,1,0:T(8,128)}) fusion(f32[3,16,8,128]{3,2,1,0:T(8,128)S(1)} %broadcast_in_dim.324, f32[3,16,12,128]{3,2,1,0:T(8,128)S(1)} %reshape.844, f32[3,16,128,128]{3,2,1,0:T(8,128)S(1)} %bitcast.48, f32[3,16,12,128]{3,2,1,0:T(8,128)} %reshape.842), kind=kLoop, calls=%fused_computation.6 | loop fusion | flops 2211840 | bytes 6881280 | tf_op jit(solution)/shard_map/slice | solution.py:259
  51.5 4.6 %collective-permute-start.3 = (f32[3,6,160,128]{3,2,1,0:T(8,128)}, f32[3,6,160,128]{3,2,1,0:T(8,128)}, u32[]{:S(2)}, u32[]{:S(2)}) collective-permute-start(f32[3,6,160,128]{3,2,1,0:T(8,128)} %get-tuple-element.16), channel_id=1, source_target_pairs={{0,8},{8,16},{16,24},{1,9},{9,17},{17,25},{2,10},{10,18},{18,26},{... | collective-permute-start | bytes 4423688 | tf_op jit(solution)/shard_map/ppermute | solution.py:259
  60.9 1.7 broadcast_in_dim.356.w_ref
  62.6 7.4 %norm.1.inv_ref = f32[3,16,144,128]{3,2,1,0:T(8,128)} custom-call(f32[22,152,128]{2,1,0:T(8,128)} %broadcast_in_dim.356.w_ref, f32[3,7,8,128]{3,2,1,0:T(8,128)} %broadcast_in_dim.359.tx_ref, f32[3,7,8,128]{3,2,1,0:T(8,128)} %broadcast_in_dim.361.ty_ref), custom_call_target="tpu_custom_call" | custom-call | tf_op jit(solution)/shard_map/norm/pallas_call | solution.py:241
  70.1 17.5 %collective-permute-done.3 = f32[3,6,160,128]{3,2,1,0:T(8,128)} collective-permute-done((f32[3,6,160,128]{3,2,1,0:T(8,128)}, f32[3,6,160,128]{3,2,1,0:T(8,128)}, u32[]{:S(2)}, u32[]{:S(2)}) %collective-permute-start.3) | collective-permute-done | bytes 1474592 | tf_op jit(solution)/shard_map/ppermute | solution.py:259
  87.5 5.8 %collective-permute-done.4 = f32[3,6,160,128]{3,2,1,0:T(8,128)} collective-permute-done((f32[3,6,160,128]{3,2,1,0:T(8,128)}, f32[3,6,160,128]{3,2,1,0:T(8,128)}, u32[]{:S(2)}, u32[]{:S(2)}) %collective-permute-start.4) | collective-permute-done | bytes 1474592 | tf_op jit(solution)/shard_map/ppermute | solution.py:260
  93.3 5.3 %pad_maximum_fusion.est_ref.obs_ref = f32[3,28,160,128]{3,2,1,0:T(8,128)} fusion(f32[3,6,160,128]{3,2,1,0:T(8,128)} %collective-permute-done.4, f32[3,16,8,128]{3,2,1,0:T(8,128)} %copy-done.2, f32[3,16,12,128]{3,2,1,0:T(8,128)S(1)} %reshape.844, f32[3,16,128,128]{3,2,1,0:T(8,128)S(1)} %bitcast.49, f32[3,16,12,128]{3,2,1,0:T(8,128)} %reshape.842, ...), kind=kLoop, calls=%fused_computation | loop fusion | flops 8601600 | bytes 13762560 | tf_op jit(solution)/shard_map/concatenate | solution.py:261
  98.7 26.5 %iterate.2 = f32[3,16,144,128]{3,2,1,0:T(8,128)} custom-call(f32[3,28,160,128]{3,2,1,0:T(8,128)} %pad_maximum_fusion.est_ref.obs_ref, f32[3,28,160,128]{3,2,1,0:T(8,128)} %pad_maximum_fusion.est_ref.obs_ref, f32[22,152,128]{2,1,0:T(8,128)} %broadcast_in_dim.356.w_ref, f32[3,16,144,128]{3,2,1,0:T(8,128)} %norm.1.inv_ref, ...), custom_call_target="tpu_custom_call" | custom-call | tf_op jit(solution)/shard_map/iterate/pallas_call | solution.py:273
  125.1 2.0 %fusion.49 = (f32[3,6,144,128]{3,2,1,0:T(8,128)S(1)}, f32[3,6,144,128]{3,2,1,0:T(8,128)S(1)}) fusion(f32[3,16,144,128]{3,2,1,0:T(8,128)} %iterate.2), kind=kLoop, calls=%fused_computation.125 | loop fusion | bytes 5308416 | tf_op jit(solution)/shard_map/slice | solution.py:259
  127.2 2.4 %collective-permute-start.5 = (f32[3,6,144,128]{3,2,1,0:T(8,128)S(1)}, f32[3,6,144,128]{3,2,1,0:T(8,128)S(1)}, u32[]{:S(2)}, u32[]{:S(2)}) collective-permute-start(f32[3,6,144,128]{3,2,1,0:T(8,128)S(1)} %get-tuple-element.18), channel_id=1, source_target_pairs={{0,8},{8,16},{16,24},{1,9},{9,17},{17,25},{2,10},{10,18},{18,26},{... | collective-permute-start | bytes 3981320 | tf_op jit(solution)/shard_map/ppermute | solution.py:259
  130.9 27.3 %collective-permute-done.5 = f32[3,6,144,128]{3,2,1,0:T(8,128)S(1)} collective-permute-done((f32[3,6,144,128]{3,2,1,0:T(8,128)S(1)}, f32[3,6,144,128]{3,2,1,0:T(8,128)S(1)}, u32[]{:S(2)}, u32[]{:S(2)}) %collective-permute-start.5) | collective-permute-done | bytes 1327136 | tf_op jit(solution)/shard_map/ppermute | solution.py:259
  158.2 4.2 %collective-permute-done.6 = f32[3,6,144,128]{3,2,1,0:T(8,128)S(1)} collective-permute-done((f32[3,6,144,128]{3,2,1,0:T(8,128)S(1)}, f32[3,6,144,128]{3,2,1,0:T(8,128)S(1)}, u32[]{:S(2)}, u32[]{:S(2)}) %collective-permute-start.6) | collective-permute-done | bytes 1327136 | tf_op jit(solution)/shard_map/ppermute | solution.py:260
  162.4 3.1 %pad_maximum_fusion.1.est_ref = f32[3,28,144,128]{3,2,1,0:T(8,128)} fusion(f32[3,6,144,128]{3,2,1,0:T(8,128)S(1)} %collective-permute-done.6, f32[3,16,144,128]{3,2,1,0:T(8,128)S(1)} %copy-done, f32[3,6,144,128]{3,2,1,0:T(8,128)S(1)} %collective-permute-done.5), kind=kLoop, calls=%fused_computation.1 | loop fusion | flops 3096576 | bytes 12386304 | tf_op jit(solution)/shard_map/concatenate | solution.py:261
  165.4 24.4 %iterate.3 = f32[3,16,128,128]{3,2,1,0:T(8,128)} custom-call(f32[3,28,144,128]{3,2,1,0:T(8,128)} %pad_maximum_fusion.1.est_ref, f32[3,28,160,128]{3,2,1,0:T(8,128)} %pad_maximum_fusion.est_ref.obs_ref, f32[22,152,128]{2,1,0:T(8,128)} %broadcast_in_dim.356.w_ref, f32[3,16,144,128]{3,2,1,0:T(8,128)} %norm.1.inv_ref, ...), custom_call_target="tpu_custom_call" | custom-call | tf_op jit(solution)/shard_map/iterate/pallas_call | solution.py:273
  189.8 2.6 %copy.18 = f32[3,128,16,128]{3,2,1,0:T(8,128)S(1)} copy(f32[3,128,16,128]{1,3,2,0:T(8,128)} %bitcast.50) | data formatting | bytes 6291456 | tf_op jit(solution)/shard_map/transpose | solution.py:284
  192.4 1.5 slice.204
  (104 shorter events, 24.4 us)
Async XLA Ops:
  0.0 29.4 %copy-start.1 = (f32[256,16,128]{2,1,0:T(8,128)S(1)}, f32[256,16,128]{2,1,0:T(8,128)}, u32[]{:S(2)}) copy-start(f32[256,16,128]{2,1,0:T(8,128)} %param.6) | copy-start | bytes 6291460
  2.7 26.6 %collective-permute-start = (f32[65,16,128]{2,1,0:T(8,128)S(1)}, f32[65,16,128]{2,1,0:T(8,128)S(1)}, u32[]{:S(2)}, u32[]{:S(2)}) collective-permute-start(f32[65,16,128]{2,1,0:T(8,128)S(1)} %pad_maximum_fusion.6), channel_id=1, source_target_pairs={{0,1},{1,0},{2,3},{3,2},{4,5},{5,4},{6,7},{7,6},{8,9},{9,8},{10,11... | collective-permute-start | bytes 1597448 | tf_op jit(solution)/shard_map/ppermute | solution.py:173
  38.3 7.0 %collective-permute-start.2 = (f32[3,192,128]{2,1,0:T(8,128)}, f32[3,192,128]{2,1,0:T(8,128)}, u32[]{:S(2)}, u32[]{:S(2)}) collective-permute-start(f32[3,192,128]{2,1,0:T(8,128)} %reshape.843), channel_id=1, source_target_pairs={{2,0},{4,2},{6,4},{3,1},{5,3},{7,5},{10,8},{12,10},{14,12},{11,9},... | collective-permute-start | bytes 884744 | tf_op jit(solution)/shard_map/ppermute | solution.py:252
  39.6 6.7 %collective-permute-start.1 = (f32[3,192,128]{2,1,0:T(8,128)}, f32[3,192,128]{2,1,0:T(8,128)}, u32[]{:S(2)}, u32[]{:S(2)}) collective-permute-start(f32[3,192,128]{2,1,0:T(8,128)} %reshape.841), channel_id=1, source_target_pairs={{0,2},{2,4},{4,6},{1,3},{3,5},{5,7},{8,10},{10,12},{12,14},{9,11},... | collective-permute-start | bytes 884744 | tf_op jit(solution)/shard_map/ppermute | solution.py:251
  48.1 10.2 %copy-start.6 = (pred[22,152]{1,0:T(8,128)(4,1)S(1)}, pred[22,152]{1,0:T(8,128)(4,1)}, u32[]{:S(2)}) copy-start(pred[22,152]{1,0:T(8,128)(4,1)} %get-tuple-element.57) | copy-start | bytes 10036
  48.1 10.1 %copy-start.7 = (pred[22,152]{1,0:T(8,128)(4,1)S(1)}, pred[22,152]{1,0:T(8,128)(4,1)}, u32[]{:S(2)}) copy-start(pred[22,152]{1,0:T(8,128)(4,1)} %get-tuple-element.58) | copy-start | bytes 10036
  48.2 10.1 %copy-start.8 = (pred[22,152]{1,0:T(8,128)(4,1)S(1)}, pred[22,152]{1,0:T(8,128)(4,1)}, u32[]{:S(2)}) copy-start(pred[22,152]{1,0:T(8,128)(4,1)} %get-tuple-element.59) | copy-start | bytes 10036
  48.2 10.1 %copy-start.9 = (pred[22,152]{1,0:T(8,128)(4,1)S(1)}, pred[22,152]{1,0:T(8,128)(4,1)}, u32[]{:S(2)}) copy-start(pred[22,152]{1,0:T(8,128)(4,1)} %get-tuple-element.60) | copy-start | bytes 10036
  48.2 10.1 %copy-start.10 = (pred[22,152]{1,0:T(8,128)(4,1)S(1)}, pred[22,152]{1,0:T(8,128)(4,1)}, u32[]{:S(2)}) copy-start(pred[22,152]{1,0:T(8,128)(4,1)} %get-tuple-element.61) | copy-start | bytes 10036
  48.2 10.1 %copy-start.11 = (pred[22,152]{1,0:T(8,128)(4,1)S(1)}, pred[22,152]{1,0:T(8,128)(4,1)}, u32[]{:S(2)}) copy-start(pred[22,152]{1,0:T(8,128)(4,1)} %get-tuple-element.62) | copy-start | bytes 10036
  48.2 10.1 %copy-start.12 = (pred[22,152]{1,0:T(8,128)(4,1)S(1)}, pred[22,152]{1,0:T(8,128)(4,1)}, u32[]{:S(2)}) copy-start(pred[22,152]{1,0:T(8,128)(4,1)} %get-tuple-element.63) | copy-start | bytes 10036
  48.2 10.1 %copy-start.17 = (s32[2]{0:T(128)S(1)}, s32[2]{0:T(128)}, u32[]{:S(2)}) copy-start(s32[2]{0:T(128)} %get-tuple-element.7) | copy-start | bytes 28
  48.3 10.2 %copy-start.26 = (pred[22]{0:T(512)(128)(4,1)S(1)}, pred[22]{0:T(512)(128)(4,1)}, u32[]{:S(2)}) copy-start(pred[22]{0:T(512)(128)(4,1)} %get-tuple-element.66) | copy-start | bytes 70
  48.3 10.2 %copy-start.27 = (pred[152]{0:T(512)(128)(4,1)S(1)}, pred[152]{0:T(512)(128)(4,1)}, u32[]{:S(2)}) copy-start(pred[152]{0:T(512)(128)(4,1)} %get-tuple-element.64) | copy-start | bytes 460
  48.3 10.2 %copy-start.28 = (s32[152]{0:T(256)S(1)}, s32[152]{0:T(256)}, u32[]{:S(2)}) copy-start(s32[152]{0:T(256)} %and_select_fusion) | copy-start | bytes 1828
  48.3 10.2 %copy-start.29 = (s32[22]{0:T(128)S(1)}, s32[22]{0:T(128)}, u32[]{:S(2)}) copy-start(s32[22]{0:T(128)} %and_select_fusion.3) | copy-start | bytes 268
  48.3 11.1 %copy-start.16 = (f32[256]{0:T(256)S(1)}, f32[256]{0:T(256)}, u32[]{:S(2)}) copy-start(f32[256]{0:T(256)} %copy-done.15) | copy-start | bytes 3076
  48.3 11.2 %copy-start.13 = (f32[8,7]{0,1:T(8,128)S(1)}, f32[8,7]{0,1:T(8,128)}, u32[]{:S(2)}) copy-start(f32[8,7]{0,1:T(8,128)} %copy.16) | copy-start | bytes 676
  48.4 11.2 %copy-start.14 = (f32[8,7]{0,1:T(8,128)S(1)}, f32[8,7]{0,1:T(8,128)}, u32[]{:S(2)}) copy-start(f32[8,7]{0,1:T(8,128)} %copy.17) | copy-start | bytes 676
  51.5 36.1 %collective-permute-start.3 = (f32[3,6,160,128]{3,2,1,0:T(8,128)}, f32[3,6,160,128]{3,2,1,0:T(8,128)}, u32[]{:S(2)}, u32[]{:S(2)}) collective-permute-start(f32[3,6,160,128]{3,2,1,0:T(8,128)} %get-tuple-element.16), channel_id=1, source_target_pairs={{0,8},{8,16},{16,24},{1,9},{9,17},{17,25},{2,10},{10,18},{18,26},{... | collective-permute-start | bytes 4423688 | tf_op jit(solution)/shard_map/ppermute | solution.py:259
  56.1 37.2 %collective-permute-start.4 = (f32[3,6,160,128]{3,2,1,0:T(8,128)}, f32[3,6,160,128]{3,2,1,0:T(8,128)}, u32[]{:S(2)}, u32[]{:S(2)}) collective-permute-start(f32[3,6,160,128]{3,2,1,0:T(8,128)} %get-tuple-element.17), channel_id=1, source_target_pairs={{8,0},{16,8},{24,16},{9,1},{17,9},{25,17},{10,2},{18,10},{26,18},{... | collective-permute-start | bytes 4423688 | tf_op jit(solution)/shard_map/ppermute | solution.py:260
  125.1 37.2 %copy-start = (f32[3,16,144,128]{3,2,1,0:T(8,128)S(1)}, f32[3,16,144,128]{3,2,1,0:T(8,128)}, u32[]{:S(2)}) copy-start(f32[3,16,144,128]{3,2,1,0:T(8,128)} %iterate.2) | copy-start | bytes 10616836
  127.2 31.0 %collective-permute-start.5 = (f32[3,6,144,128]{3,2,1,0:T(8,128)S(1)}, f32[3,6,144,128]{3,2,1,0:T(8,128)S(1)}, u32[]{:S(2)}, u32[]{:S(2)}) collective-permute-start(f32[3,6,144,128]{3,2,1,0:T(8,128)S(1)} %get-tuple-element.18), channel_id=1, source_target_pairs={{0,8},{8,16},{16,24},{1,9},{9,17},{17,25},{2,10},{10,18},{18,26},{... | collective-permute-start | bytes 3981320 | tf_op jit(solution)/shard_map/ppermute | solution.py:259
  129.6 32.8 %collective-permute-start.6 = (f32[3,6,144,128]{3,2,1,0:T(8,128)S(1)}, f32[3,6,144,128]{3,2,1,0:T(8,128)S(1)}, u32[]{:S(2)}, u32[]{:S(2)}) collective-permute-start(f32[3,6,144,128]{3,2,1,0:T(8,128)S(1)} %get-tuple-element.19), channel_id=1, source_target_pairs={{8,0},{16,8},{24,16},{9,1},{17,9},{25,17},{10,2},{18,10},{26,18},{... | collective-permute-start | bytes 3981320 | tf_op jit(solution)/shard_map/ppermute | solution.py:260
  (13 other events, 106.9 us)
where the time goes:
time: 195 us; the launch traced here: 194 us
  Pallas kernels  58.3 us (30%)
  waiting for transfers between devices  54.8 us (28%)
  other arithmetic  37.2 us (19%)
  local copies, waits for them, and re-layouts  25.4 us (13%)
  starting transfers between devices  17.7 us (9%)
    pallas_call x2, Pallas kernels, body(): pl.pallas_call(functools.partial(iterate_kernel, dy, need), out_shape=jax...  50.8 us
    ppermute x2, waiting for transfers between devices, x_halo(): low = lax.ppermute(value[:, cx - hx:], 'sx', up)  44.7 us
    select_n x1, other arithmetic, halves(): parts.append(jnp.where((cols >= low) & (cols < high), matrix, 0.0))  12 us
    ppermute x2, waiting for transfers between devices, x_halo(): high = lax.ppermute(value[:, :hx], 'sx', down)  10 us
    concatenate x2, other arithmetic, x_halo(): return jnp.concatenate([low, value, high], axis=1)  8.39 us
    pallas_call x1, Pallas kernels, body(): pl.pallas_call(norm_kernel, out_shape=jax.ShapeDtypeStruct((tiles, cx, ro...  7.44 us
    ppermute x2, starting transfers between devices, x_halo(): low = lax.ppermute(value[:, cx - hx:], 'sx', up)  7.06 us
  transfers between devices with their start and end apart: 7, of which 4 were waited for; matrix products, arithmetic and copies ran while one was open for 16% of the time, Pallas kernels for 4%

commit v1 on v0

--- a/solution.py
+++ b/solution.py
@@ -23,21 +23,47 @@
     return up, [(j, i) for i, j in up]
 
 
-def x_conv(src, dst, taps, reverse, t, width, blocks):
-    count = taps.shape[1]
-    k = [taps[t, count - 1 - a if reverse else a] for a in range(count)]
+def lane_is_low():
+    return lax.broadcasted_iota(jnp.int32, (8, LANES), 1) < LANES // 2
+
+
+def halo_row(ref, tiles, packed, hx, t, p, rows):
+    if not packed or t < tiles - 1:
+        return ref[hx * t + p, rows, :]
+    half = hx // 2
+    value = ref[hx * t + p % half, rows, :]
+    if p >= half:
+        value = pltpu.roll(value, LANES // 2, 1)
+    return jnp.where(lane_is_low(), value, 0.0)
+
+
+def pack_rows(src, pay, packed, hx, x0, blocks, src_block, pay_block):
+    tiles = src.shape[0]
 
     def step(j, carry):
-        rows = pl.ds(pl.multiple_of(8 * j, 8), 8)
-        v = [src[t, x, rows, :] for x in range(width + count - 1)]
-        for x in range(width):
-            acc = k[0] * v[x]
-            for a in range(1, count):
-                acc = acc + k[a] * v[x + a]
-            dst[t, x, rows, :] = acc
+        here = pl.ds(pl.multiple_of(8 * (j + src_block), 8), 8)
+        there = pl.ds(pl.multiple_of(8 * (j + pay_block), 8), 8)
+        for t in range(tiles - 1 if packed else tiles):
+            for p in range(hx):
+                pay[hx * t + p, there, :] = src[t, x0 + p, here, :]
+        if packed:
+            half = hx // 2
+            for p in range(half):
+                other = pltpu.roll(src[tiles - 1, x0 + p + half, here, :], LANES // 2, 1)
+                pay[hx * (tiles - 1) + p, there, :] = jnp.where(lane_is_low(), src[tiles - 1, x0 + p, here, :], other)
         return carry
 
     lax.fori_loop(0, blocks, step, 0)
+
+
+def conv_rows(k, v, width):
+    out = []
+    for x in range(width):
+        acc = k[0] * v[x]
+        for a in range(1, len(k)):
+            acc = acc + k[a] * v[x + a]
+        out.append(acc)
+    return out
 
 
 def y_conv(src, taps, reverse, t, width, blocks, emit):
@@ -78,20 +104,16 @@
 
 
 def norm_kernel(w_ref, tx_ref, ty_ref, out_ref, mid_ref):
-    tiles = tx_ref.shape[0]
+    tiles, count = tx_ref.shape[:2]
+    reach = (count - 1) // 2
     width = out_ref.shape[1]
-    blocks = out_ref.shape[2] // 8
-    count = tx_ref.shape[1]
     for t in range(tiles):
         k = [tx_ref[t, count - 1 - a] for a in range(count)]
 
         def step(j, carry, k=k):
             rows = pl.ds(pl.multiple_of(8 * j, 8), 8)
             v = [w_ref[x, rows, :] for x in range(width + count - 1)]
-            for x in range(width):
-                acc = k[0] * v[x]
-                for a in range(1, count):
-                    acc = acc + k[a] * v[x + a]
+            for x, acc in enumerate(conv_rows(k, v, width)):
                 mid_ref[0, x, rows, :] = acc
             return carry
 
@@ -99,41 +121,111 @@
         ky = [ty_ref[t, count - 1 - b] for b in range(count)]
 
         def ystep(x, carry, ky=ky, t=t):
-            for j in range(blocks):
-                acc = ky[0] * mid_ref[0, x, 8 * j : 8 * j + 8, :]
+            for j in range(out_ref.shape[2] // 8):
+                at = 8 * j + reach
+                acc = ky[0] * mid_ref[0, x, at : at + 8, :]
                 for b in range(1, count):
-                    acc = acc + ky[b] * mid_ref[0, x, 8 * j + b : 8 * j + b + 8, :]
+                    acc = acc + ky[b] * mid_ref[0, x, at + b : at + b + 8, :]
                 out_ref[t, x, 8 * j : 8 * j + 8, :] = 1.0 / jnp.maximum(acc, TINY)
             return carry
 
         lax.fori_loop(0, width, ystep, 0)
 
 
-def iterate_kernel(dy, need, est_ref, obs_ref, w_ref, inv_ref, tx_ref, ty_ref, fh_ref, fl_ref, bh_ref, bl_ref, out_ref, mid_ref, blur_ref):
-    tiles = est_ref.shape[0]
-    reach = (tx_ref.shape[1] - 1) // 2
-    wide = blur_ref.shape[1]
+def assemble_kernel(packed, hx, cut, vol_ref, low_ref, high_ref, ext_ref, *pays):
+    tiles, cx, cy = vol_ref.shape[:3]
+    hy = low_ref.shape[1] // cx
+    end = cy + 2 * hy
+    for t in range(tiles):
+        for x in range(cx):
+            ext_ref[t, x, 0:hy, :] = low_ref[t, hy * x : hy * x + hy, :]
+            ext_ref[t, x, hy : hy + cy, :] = vol_ref[t, x]
+            ext_ref[t, x, hy + cy : end, :] = high_ref[t, hy * x : hy * x + hy, :]
+            ext_ref[t, x, end:, :] = jnp.zeros((ext_ref.shape[2] - end, LANES), jnp.float32)
+    for n, (pay_up, pay_down) in enumerate((pays[:2], pays[2:])):
+        first, last = (0, cut) if n == 0 else (cut, end)
+        blocks = -(-(last - first) // 8)
+        pack_rows(ext_ref, pay_up, packed, hx, cx - hx, blocks, first // 8, 0)
+        pack_rows(ext_ref, pay_down, packed, hx, 0, blocks, first // 8, 0)
+
+
+def iterate_kernel(plan, *refs):
+    refs = list(refs)
+    take = refs.pop
+    est_ref = take(0)
+    halos = [(take(0), take(0), first, last) for first, last in plan["halos"]]
+    w_ref = take(0) if plan["make_data"] else None
+    data_in = None if plan["make_data"] else take(0)
+    tail_ref = take(0) if plan["tail"] else None
+    inv_ref, tx_ref, ty_ref, fh_ref, fl_ref, bh_ref, bl_ref = [take(0) for _ in range(7)]
+    out_ref = take(0)
+    data_ref = take(0) if plan["make_data"] else data_in
+    pays = [take(0), take(0)] if plan["pay"] else None
+    mid_ref, blur_ref = refs
+    packed, hx, low, high = plan["packed"], plan["hx"], plan["low"], plan["high"]
+    est_base, data_base, data_off, inv_off = plan["est_base"], plan["data_base"], plan["data_off"], plan["inv_off"]
+    tiles, cx = est_ref.shape[:2]
+    count = tx_ref.shape[1]
+    reach = (count - 1) // 2
+    wide = cx + 2 * reach
     rows = blur_ref.shape[2]
-    width = out_ref.shape[1]
-    blocks = out_ref.shape[2] // 8
-
-    def put(t, x, j, acc):
-        blur_ref[t, x, 8 * j : 8 * j + 8, :] = acc
+    last_block = -(-(high + 4 * reach) // 8)
+    data_first = data_base // 8 if plan["make_data"] else low // 8
+    half = (hx - 2 * reach) // 2
 
     for t in range(tiles):
-        x_conv(est_ref, mid_ref, tx_ref, False, t, wide, -(-need // 8))
+        k = [tx_ref[t, a] for a in range(count)]
+        for lo_ref, hi_ref, first, last in halos:
+
+            def gather(j, t=t, lo_ref=lo_ref, hi_ref=hi_ref, first=first):
+                here = pl.ds(pl.multiple_of(8 * j - est_base, 8), 8)
+                there = pl.ds(pl.multiple_of(8 * j - first, 8), 8)
+                v = [halo_row(lo_ref, tiles, packed, hx, t, p, there) for p in range(hx)]
+                v += [est_ref[t, x, here, :] for x in range(cx)]
+                return v + [halo_row(hi_ref, tiles, packed, hx, t, p, there) for p in range(hx)]
+
+            def keep(j, v, t=t):
+                here = pl.ds(pl.multiple_of(8 * j, 8), 8)
+                there = pl.ds(pl.multiple_of(8 * j - data_base, 8), 8)
+                for x in range(wide):
+                    data_ref[t, x, there, :] = w_ref[x, here, :] * v[x + reach]
+
+            def only_data(j, carry, gather=gather, keep=keep):
+                keep(j, gather(j))
+                return carry
+
+            def step(j, carry, gather=gather, keep=keep, k=k, t=t):
+                v = gather(j)
+                if plan["make_data"]:
+                    keep(j, v)
+                mid = pl.ds(pl.multiple_of(8 * j - low, 8), 8)
+                for x, acc in enumerate(conv_rows(k, v, wide)):
+                    mid_ref[t, x, mid, :] = acc
+                return carry
+
+            a, b = max(first // 8, data_first), min(last // 8, low // 8)
+            if plan["make_data"] and a < b:
+                lax.fori_loop(a, b, only_data, 0)
+            a, b = max(first // 8, low // 8), min(-(-last // 8), last_block)
+            if a < b:
+                lax.fori_loop(a, b, step, 0)
+
+        def put(t, x, j, acc):
+            blur_ref[t, x, 8 * j : 8 * j + 8, :] = acc
+
         y_conv(mid_ref, ty_ref, False, t, wide, rows // 8, put)
+
+    spot0 = low + data_off + reach - data_base
 
     def depth(i, carry):
         spot = pl.ds(2 * i, 2)
         size = 2 * rows
         parts = [blur_ref[t, spot].reshape(size, LANES) for t in range(tiles)]
         blurred = depth_rows(parts, fh_ref, fl_ref)
-        weight = w_ref[spot, dy : dy + rows, :].reshape(size, LANES)
         ratio = []
         for t in range(tiles):
-            seen = obs_ref[t, pl.ds(2 * i + reach, 2), dy + reach : dy + reach + rows, :].reshape(size, LANES)
-            ratio.append(weight * seen / jnp.maximum(blurred[t], TINY))
+            seen = data_ref[t, spot, spot0 : spot0 + rows, :].reshape(size, LANES)
+            ratio.append(seen / jnp.maximum(blurred[t], TINY))
         spread = depth_rows(ratio, bh_ref, bl_ref)
         for t in range(tiles):
             blur_ref[t, spot] = spread[t].reshape(2, rows, LANES)
@@ -141,13 +233,40 @@
 
     lax.fori_loop(0, wide // 2, depth, 0)
 
-    def finish(t, x, j, acc):
-        old = est_ref[t, x + 2 * reach, 8 * j + 2 * reach : 8 * j + 2 * reach + 8, :]
-        out_ref[t, x, 8 * j : 8 * j + 8, :] = old * acc * inv_ref[t, x, 8 * j + dy : 8 * j + dy + 8, :]
-
+    out_skip = plan["tail"]
+    blocks = -(-(high - low) // 8)
     for t in range(tiles):
-        x_conv(blur_ref, mid_ref, tx_ref, True, t, width, rows // 8)
-        y_conv(mid_ref, ty_ref, True, t, width, blocks, finish)
+        k = [tx_ref[t, count - 1 - a] for a in range(count)]
+
+        def back(j, carry, k=k, t=t):
+            here = pl.ds(pl.multiple_of(8 * j, 8), 8)
+            v = [blur_ref[t, x, here, :] for x in range(wide)]
+            for x, acc in enumerate(conv_rows(k, v, cx)):
+                mid_ref[t, x, here, :] = acc
+            return carry
+
+        lax.fori_loop(0, rows // 8, back, 0)
+
+        def finish(t, x, j, acc):
+            at = 8 * j + low + 2 * reach - est_base
+            to = 8 * j + out_skip
+            scale = 8 * j + low + inv_off
+            out_ref[t, x, to : to + 8, :] = est_ref[t, x, at : at + 8, :] * acc * inv_ref[t, x, scale : scale + 8, :]
+
+        y_conv(mid_ref, ty_ref, True, t, cx, blocks, finish)
+
+    if out_skip:
+        have = tail_ref.shape[2]
+        for t in range(tiles):
+
+            def copy(x, carry, t=t):
+                out_ref[t, x, 0:out_skip, :] = tail_ref[t, x, have - out_skip : have, :]
+                return carry
+
+            lax.fori_loop(0, cx, copy, 0)
+    if pays:
+        pack_rows(out_ref, pays[0], packed, hx, cx - hx, blocks, out_skip // 8, 0)
+        pack_rows(out_ref, pays[1], packed, hx, 0, blocks, out_skip // 8, 0)
 
 
 def body(observed, zone_of_slice, lateral_x, lateral_y, depth_psf, stitch_width):
@@ -220,13 +339,13 @@
 
     sx, sy = lax.axis_index("sx"), lax.axis_index("sy")
     stacks_x, stacks_y = stitch_width.shape[:2]
-    rows1 = ceil_to(cy + 2 * hy - 2 * reach, 8)
+    full = ceil_to(cy + 2 * hy + reach, 8)
     gx = sx * cx - reach + jnp.arange(cx + 2 * reach)
-    gy = sy * cy - (hy - reach) + jnp.arange(rows1)
+    gy = sy * cy - hy + jnp.arange(full)
     near = lax.dynamic_slice(jnp.pad(stitch_width, ((1, 1), (1, 1), (0, 0))), (sx, sy, jnp.int32(0)), (3, 3, 2))
     of_x = gx // cx - sx + 1
     of_y = gy // cy - sy + 1
-    bands = jnp.zeros((2, gx.shape[0], rows1), jnp.int32)
+    bands = jnp.zeros((2, gx.shape[0], full), jnp.int32)
     for a in range(3):
         for b in range(3):
             hit = (of_x[:, None] == a) & (of_y[None, :] == b)
@@ -234,53 +353,89 @@
     inside = ((gx >= 0) & (gx < stacks_x * cx))[:, None] & ((gy >= 0) & (gy < stacks_y * cy))[None, :]
     weight = jnp.where((gx % cx)[:, None] < bands[0], 0.5, 1.0) * jnp.where((gy % cy)[None, :] < bands[1], 0.5, 1.0)
     weight = jnp.where(inside, weight, 0.0).astype(f32)
-    weight = jnp.broadcast_to(weight[:, :, None], (cx + 2 * reach, rows1, LANES))
-
-    rows_est1 = ceil_to(cy + 2 * hy - 4 * reach, 8)
-    rows_mid = ceil_to(rows1 + 2 * reach, 8)
-    inv = pl.pallas_call(
-        norm_kernel,
-        out_shape=jax.ShapeDtypeStruct((tiles, cx, rows_est1, LANES), f32),
-        in_specs=[VMEM] * 3,
-        out_specs=VMEM,
-        scratch_shapes=[pltpu.VMEM((1, cx, rows1, LANES), f32)],
-        name="norm",
-    )(weight, tx, ty)
+    weight = jnp.broadcast_to(weight[:, :, None], (cx + 2 * reach, full, LANES))
 
     up, down = line("sy")
     low = lax.ppermute(volume[:, :, cy - hy :].reshape(tiles, cx * hy, LANES), "sy", up)
     high = lax.ppermute(volume[:, :, :hy].reshape(tiles, cx * hy, LANES), "sy", down)
-    volume = [low.reshape(tiles, cx, hy, LANES), volume, high.reshape(tiles, cx, hy, LANES)]
-    spare = ceil_to(rows1 + reach, 8) - cy - 2 * hy
-    volume = jnp.concatenate(volume + [jnp.zeros((tiles, cx, spare, LANES), f32)], axis=2)
-
-    def x_halo(value):
-        up, down = line("sx")
-        low = lax.ppermute(value[:, cx - hx :], "sx", up)
-        high = lax.ppermute(value[:, :hx], "sx", down)
-        return jnp.concatenate([low, value, high], axis=1)
-
-    estimate = x_halo(volume)
-    seen = estimate
-    for step in range(ITERS):
-        dy = 2 * reach * step
-        if step:
-            estimate = x_halo(estimate)
-        need = cy + 2 * (hy - dy)
-        rows_blur = ceil_to(need - 2 * reach, 8)
-        rows_out = ceil_to(need - 4 * reach, 8)
-        wide = cx + 2 * reach
-        estimate = pl.pallas_call(
-            functools.partial(iterate_kernel, dy, need),
-            out_shape=jax.ShapeDtypeStruct((tiles, cx, rows_out, LANES), f32),
-            in_specs=[VMEM] * 10,
-            out_specs=VMEM,
-            scratch_shapes=[
-                pltpu.VMEM((tiles, wide, rows_mid, LANES), f32),
-                pltpu.VMEM((tiles, wide, rows_blur, LANES), f32),
-            ],
-            name="iterate",
-        )(estimate, seen, weight, inv, tx, ty, fh, fl, bh, bl)
+
+    wide = cx + 2 * reach
+    packed = nz + 2 * hz - (tiles - 1) * LANES <= LANES // 2
+    planes = hx * (tiles - 1) + hx // 2 if packed else hx * tiles
+    end0, end1, end2 = cy + 2 * hy, cy + 2 * hy - 4 * reach, cy
+    mid1 = ceil_to(end1 // 2, 8) + 8
+    mid2 = mid1 - ceil_to(4 * reach, 8)
+    cut = ceil_to(mid1 + 4 * reach, 8)
+    up, down = line("sx")
+
+    def shape(*dims):
+        return jax.ShapeDtypeStruct(dims, f32)
+
+    def pay_shapes(rows):
+        return [shape(planes, ceil_to(rows, 8), LANES)] * 2
+
+    def swap(pays):
+        return lax.ppermute(pays[0], "sx", up), lax.ppermute(pays[1], "sx", down)
+
+    def call(kernel, out_shape, args, scratch, name, limit, flops):
+        moved = sum(a.size * 4 for a in args) + sum(o.size * 4 for o in out_shape)
+        return pl.pallas_call(
+            kernel,
+            out_shape=out_shape,
+            in_specs=[VMEM] * len(args),
+            out_specs=[VMEM] * len(out_shape),
+            scratch_shapes=[pltpu.VMEM(dims, f32) for dims in scratch],
+            compiler_params=pltpu.CompilerParams(vmem_limit_bytes=limit << 20),
+            cost_estimate=pl.CostEstimate(flops=flops, bytes_accessed=moved, transcendentals=0),
+            name=name,
+        )(*args)
+
+    ext, *pays = call(
+        functools.partial(assemble_kernel, packed, hx, cut),
+        [shape(tiles, cx, full, LANES)] + pay_shapes(cut) + pay_shapes(end0 - cut),
+        (volume, low, high), [], "assemble", 8, 1,
+    )
+    halo_a = swap(pays[:2])
+    halo_b = swap(pays[2:])
+    (inv,) = call(
+        norm_kernel, [shape(tiles, cx, ceil_to(end1, 8), LANES)], (weight, tx, ty),
+        [(1, cx, full, LANES)], "norm", 8, 1,
+    )
+    tables = (inv, tx, ty, fh, fl, bh, bl)
+
+    def iterate(name, est, halos, extra, plan, outs):
+        rows = ceil_to(plan["high"] - plan["low"] + 2 * reach, 8)
+        args = (est,) + tuple(h for _, pair in halos for h in pair) + extra + tables
+        plan = dict(plan, hx=hx, packed=packed, halos=[rng for rng, _ in halos])
+        scratch = [(tiles, wide, rows + 16, LANES), (tiles, wide, rows, LANES)]
+        return call(functools.partial(iterate_kernel, plan), outs, args, scratch, name, 16, 1)
+
+    data_at = mid2 + 8
+    est_a, data_a, *pays = iterate(
+        "first_a", ext, [((0, cut), halo_a)], (weight,),
+        dict(low=0, high=mid1, est_base=0, data_base=0, data_off=0, inv_off=0, make_data=True, tail=0, pay=True),
+        [shape(tiles, cx, mid1, LANES), shape(tiles, wide, cut, LANES)] + pay_shapes(mid1),
+    )
+    halo_c = swap(pays)
+    tail = mid1 - mid2
+    est_b, data_b, *pays = iterate(
+        "first_b", ext, [((0, cut), halo_a), ((cut, end0), halo_b)], (weight, est_a),
+        dict(low=mid1, high=end1, est_base=0, data_base=data_at, data_off=0, inv_off=0, make_data=True, tail=tail, pay=True),
+        [shape(tiles, cx, ceil_to(end1, 8) - mid2, LANES), shape(tiles, wide, full - data_at, LANES)] + pay_shapes(end1 - mid1),
+    )
+    halo_d = swap(pays)
+    shift = 2 * reach
+    (out_a,) = iterate(
+        "second_a", est_a, [((0, mid1), halo_c)], (data_a,),
+        dict(low=0, high=mid2, est_base=0, data_base=0, data_off=shift, inv_off=shift, make_data=False, tail=0, pay=False),
+        [shape(tiles, cx, mid2, LANES)],
+    )
+    (out_b,) = iterate(
+        "second_b", est_b, [((0, mid1), halo_c), ((mid1, end1), halo_d)], (data_b,),
+        dict(low=mid2, high=end2, est_base=mid2, data_base=data_at, data_off=shift, inv_off=shift, make_data=False, tail=0, pay=False),
+        [shape(tiles, cx, end2 - mid2, LANES)],
+    )
+    estimate = jnp.concatenate([out_a, out_b], axis=2)
     result = estimate.transpose(0, 3, 1, 2).reshape(tiles * LANES, cx, cy)
     return result[hz : hz + nz]
 

time: 195 us -> 139 us (0.71)
  the two profiles are of different devices: /device:TPU:0 before, /device:TPU:10 now
where the time goes in v1:
time: 139 us; the launch traced here: 137 us
  Pallas kernels  58.1 us (42%)
  starting transfers between devices  30.6 us (22%)
  other arithmetic  20.1 us (14%)
  local copies, waits for them, and re-layouts  17.5 us (13%)
  waiting for transfers between devices  10.5 us (8%)
    pallas_call x6, Pallas kernels, call(): pl.pallas_call(kernel, out_shape=out_shape, in_specs=[VMEM] * len(args),...  58.1 us
    ppermute x8, starting transfers between devices, swap(): return (lax.ppermute(pays[0], 'sx', up), lax.ppermute(pays[1], 'sx', down))  23.5 us
    select_n x1, other arithmetic, halves(): parts.append(jnp.where((cols >= low) & (cols < high), matrix, 0.0))  10.9 us
    ppermute x8, waiting for transfers between devices, swap(): return (lax.ppermute(pays[0], 'sx', up), lax.ppermute(pays[1], 'sx', down))  6.04 us
    ppermute x1, starting transfers between devices, body(): lax.ppermute(volume[:, :, :hy].reshape(tiles, cx * hy, LANES), 'sy', down)  3.63 us
    ppermute x1, waiting for transfers between devices, body(): lax.ppermute(volume[:, :, :hy].reshape(tiles, cx * hy, LANES), 'sy', down)  3.47 us
    concatenate x1, other arithmetic, body(): jnp.concatenate([before, observed, after, jnp.zeros((pad, cx, cy), f32)],...  3.29 us
    slice x1, local copies, waits for them, and re-layouts, body(): return result[hz:hz + nz]  3.04 us
  transfers between devices with their start and end apart: 11, of which 4 were waited for; matrix products, arithmetic and copies ran while one was open for 16% of the time, Pallas kernels for 31%

profile of v1, /device:TPU:10, one launch (start us, length us, event | category | flops | bytes accessed | tf_op | source)
XLA Modules:
  0.0 137.1 jit_solution(8813574415373253409)
XLA Ops:
  8.6 10.9 %broadcast_select_fusion = (f32[1,256,256]{2,1,0:T(8,128)S(1)}, f32[1,256,256]{2,1,0:T(8,128)S(1)}, f32[1,256,256]{2,1,0:T(8,128)S(1)}, f32[1,256,256]{2,1,0:T(8,128)S(1)}) fusion(f32[]{:T(128)} %bitcast.28, f32[]{:T(128)} %bitcast.27, f32[]{:T(128)} %bitcast.26, f32[]{:T(128)} %bitcast.25, f32[]{:T(128)} %bitcast.24, f32[]{:T(128)} %bitcast.23, ...), kind=kLoop, calls=%fused_computation.47 | loop fusion | flops 5701632 | bytes 1049156 | tf_op jit(solution)/shard_map/jit(_where)/select_n | solution.py:332
  21.9 3.3 %maximum_maximum_fusion = f32[384,16,128]{2,1,0:T(8,128)} fusion(f32[32,16,128]{2,1,0:T(8,128)S(1)} %get-tuple-element.47, f32[256,16,128]{2,1,0:T(8,128)S(1)} %copy-done.3, f32[32,16,128]{2,1,0:T(8,128)S(1)} %get-tuple-element.46, f32[384]{0:T(512)S(1)} %pad.23.clone), kind=kLoop, calls=%fused_computation | loop fusion | flops 2359296 | bytes 5768704 | tf_op jit(solution)/shard_map/concatenate | solution.py:303
  25.2 2.4 %copy.15 = f32[3,128,16,128]{1,3,2,0:T(8,128)S(1)} copy(f32[3,128,16,128]{3,2,1,0:T(8,128)} %bitcast.50) | data formatting | bytes 6291456 | tf_op jit(solution)/shard_map/reshape | solution.py:305
  30.3 1.9 %collective-permute-start.1 = (f32[3,192,128]{2,1,0:T(8,128)}, f32[3,192,128]{2,1,0:T(8,128)}, u32[]{:S(2)}, u32[]{:S(2)}) collective-permute-start(f32[3,192,128]{2,1,0:T(8,128)} %reshape.835), channel_id=1, source_target_pairs={{0,2},{2,4},{4,6},{1,3},{3,5},{5,7},{8,10},{10,12},{12,14},{9,11},... | collective-permute-start | bytes 884744 | tf_op jit(solution)/shard_map/ppermute | solution.py:359
  33.9 3.6 %collective-permute-start.2 = (f32[3,192,128]{2,1,0:T(8,128)}, f32[3,192,128]{2,1,0:T(8,128)S(1)}, u32[]{:S(2)}, u32[]{:S(2)}) collective-permute-start(f32[3,192,128]{2,1,0:T(8,128)} %reshape.836), channel_id=1, source_target_pairs={{2,0},{4,2},{6,4},{3,1},{5,3},{7,5},{10,8},{12,10},{14,12},{11,9},... | collective-permute-start | bytes 884744 | tf_op jit(solution)/shard_map/ppermute | solution.py:360
  38.6 3.5 %collective-permute-done.2.high_ref = f32[3,192,128]{2,1,0:T(8,128)S(1)} collective-permute-done((f32[3,192,128]{2,1,0:T(8,128)}, f32[3,192,128]{2,1,0:T(8,128)S(1)}, u32[]{:S(2)}, u32[]{:S(2)}) %collective-permute-start.2) | collective-permute-done | bytes 294944 | tf_op jit(solution)/shard_map/ppermute | solution.py:360
  42.1 4.0 %assemble.1 = (f32[3,16,160,128]{3,2,1,0:T(8,128)S(1)}, f32[15,96,128]{2,1,0:T(8,128)S(1)}, f32[15,96,128]{2,1,0:T(8,128)S(1)}, f32[15,56,128]{2,1,0:T(8,128)S(1)}, f32[15,56,128]{2,1,0:T(8,128)S(1)}) custom-call(f32[3,16,128,128]{3,2,1,0:T(8,128)S(1)} %bitcast.49, f32[3,192,128]{2,1,0:T(8,128)} %collective-permute-done.1.low_ref, ...), custom_call_target="tpu_custom_call" | custom-call | flops 1 | bytes 10002432 | tf_op jit(solution)/shard_map/assemble/pallas_call | solution.py:382
  46.1 3.5 %collective-permute-start.3 = (f32[15,96,128]{2,1,0:T(8,128)S(1)}, f32[15,96,128]{2,1,0:T(8,128)S(1)}, u32[]{:S(2)}, u32[]{:S(2)}) collective-permute-start(f32[15,96,128]{2,1,0:T(8,128)S(1)} %get-tuple-element.19), channel_id=1, source_target_pairs={{0,8},{8,16},{16,24},{1,9},{9,17},{17,25},{2,10},{10,18},{18,26},{... | collective-permute-start | bytes 2211848 | tf_op jit(solution)/shard_map/ppermute | solution.py:378
  49.6 2.4 %collective-permute-start.4 = (f32[15,96,128]{2,1,0:T(8,128)S(1)}, f32[15,96,128]{2,1,0:T(8,128)S(1)}, u32[]{:S(2)}, u32[]{:S(2)}) collective-permute-start(f32[15,96,128]{2,1,0:T(8,128)S(1)} %get-tuple-element.20), channel_id=1, source_target_pairs={{8,0},{16,8},{24,16},{9,1},{17,9},{25,17},{10,2},{18,10},{26,18},{... | collective-permute-start | bytes 2211848 | tf_op jit(solution)/shard_map/ppermute | solution.py:378
  52.8 3.4 %collective-permute-start.7 = (f32[15,56,128]{2,1,0:T(8,128)S(1)}, f32[15,56,128]{2,1,0:T(8,128)S(1)}, u32[]{:S(2)}, u32[]{:S(2)}) collective-permute-start(f32[15,56,128]{2,1,0:T(8,128)S(1)} %get-tuple-element.25), channel_id=1, source_target_pairs={{0,8},{8,16},{16,24},{1,9},{9,17},{17,25},{2,10},{10,18},{18,26},{... | collective-permute-start | bytes 1290248 | tf_op jit(solution)/shard_map/ppermute | solution.py:378
  56.3 2.4 %collective-permute-start.8 = (f32[15,56,128]{2,1,0:T(8,128)S(1)}, f32[15,56,128]{2,1,0:T(8,128)S(1)}, u32[]{:S(2)}, u32[]{:S(2)}) collective-permute-start(f32[15,56,128]{2,1,0:T(8,128)S(1)} %get-tuple-element.26), channel_id=1, source_target_pairs={{8,0},{16,8},{24,16},{9,1},{17,9},{25,17},{10,2},{18,10},{26,18},{... | collective-permute-start | bytes 1290248 | tf_op jit(solution)/shard_map/ppermute | solution.py:378
  59.4 4.4 %norm.1.refs_4_.refs_7_.refs_6_ = f32[3,16,144,128]{3,2,1,0:T(8,128)S(1)} custom-call(f32[22,160,128]{2,1,0:T(8,128)S(1)} %broadcast_in_dim.352.w_ref.refs_3_.refs_5_, f32[3,7,8,128]{3,2,1,0:T(8,128)S(1)} %broadcast_in_dim.355.tx_ref.refs_5_.refs_8_.refs_7_, f32[3,7,8,128]{3,2,1,0:T(8,128)S(1)} %broadcast_in_dim.357.ty_ref.refs_6_.refs_9_.refs_8_), custom_call_target="tpu_custom_call" | custom-call | flops 1 | bytes 5513216 | tf_op jit(solution)/shard_map/norm/pallas_call | solution.py:382
  63.8 2.8 %collective-permute-done.3.refs_1_ = f32[15,96,128]{2,1,0:T(8,128)S(1)} collective-permute-done((f32[15,96,128]{2,1,0:T(8,128)S(1)}, f32[15,96,128]{2,1,0:T(8,128)S(1)}, u32[]{:S(2)}, u32[]{:S(2)}) %collective-permute-start.3) | collective-permute-done | bytes 737312 | tf_op jit(solution)/shard_map/ppermute | solution.py:378
  66.6 3.2 %collective-permute-done.4.refs_2_ = f32[15,96,128]{2,1,0:T(8,128)S(1)} collective-permute-done((f32[15,96,128]{2,1,0:T(8,128)S(1)}, f32[15,96,128]{2,1,0:T(8,128)S(1)}, u32[]{:S(2)}, u32[]{:S(2)}) %collective-permute-start.4) | collective-permute-done | bytes 737312 | tf_op jit(solution)/shard_map/ppermute | solution.py:378
  69.8 14.8 %first_a.1 = (f32[3,16,80,128]{3,2,1,0:T(8,128)S(1)}, f32[3,22,96,128]{3,2,1,0:T(8,128)S(1)}, f32[15,80,128]{2,1,0:T(8,128)S(1)}, f32[15,80,128]{2,1,0:T(8,128)S(1)}) custom-call(f32[3,16,160,128]{3,2,1,0:T(8,128)S(1)} %get-tuple-element.18.refs_0_, f32[15,96,128]{2,1,0:T(8,128)S(1)} %collective-permute-done.3.refs_1_, ...), custom_call_target="tpu_custom_call" | custom-call | flops 1 | bytes 19456000 | tf_op jit(solution)/shard_map/first_a/pallas_call | solution.py:382
  84.6 3.5 %collective-permute-start.5 = (f32[15,80,128]{2,1,0:T(8,128)S(1)}, f32[15,80,128]{2,1,0:T(8,128)S(1)}, u32[]{:S(2)}, u32[]{:S(2)}) collective-permute-start(f32[15,80,128]{2,1,0:T(8,128)S(1)} %get-tuple-element.22), channel_id=1, source_target_pairs={{0,8},{8,16},{16,24},{1,9},{9,17},{17,25},{2,10},{10,18},{18,26},{... | collective-permute-start | bytes 1843208 | tf_op jit(solution)/shard_map/ppermute | solution.py:378
  88.1 2.4 %collective-permute-start.6 = (f32[15,80,128]{2,1,0:T(8,128)S(1)}, f32[15,80,128]{2,1,0:T(8,128)S(1)}, u32[]{:S(2)}, u32[]{:S(2)}) collective-permute-start(f32[15,80,128]{2,1,0:T(8,128)S(1)} %get-tuple-element.23), channel_id=1, source_target_pairs={{8,0},{16,8},{24,16},{9,1},{17,9},{25,17},{10,2},{18,10},{26,18},{... | collective-permute-start | bytes 1843208 | tf_op jit(solution)/shard_map/ppermute | solution.py:378
  90.5 12.8 %first_b.1 = (f32[3,16,80,128]{3,2,1,0:T(8,128)S(1)}, f32[3,22,88,128]{3,2,1,0:T(8,128)S(1)}, f32[15,64,128]{2,1,0:T(8,128)S(1)}, f32[15,64,128]{2,1,0:T(8,128)S(1)}) custom-call(f32[3,16,160,128]{3,2,1,0:T(8,128)S(1)} %get-tuple-element.18.refs_0_, f32[15,96,128]{2,1,0:T(8,128)S(1)} %collective-permute-done.3.refs_1_, ...), custom_call_target="tpu_custom_call" | custom-call | flops 1 | bytes 21766144 | tf_op jit(solution)/shard_map/first_b/pallas_call | solution.py:382
  103.3 1.9 %collective-permute-start.10 = (f32[15,64,128]{2,1,0:T(8,128)S(1)}, f32[15,64,128]{2,1,0:T(8,128)S(1)}, u32[]{:S(2)}, u32[]{:S(2)}) collective-permute-start(f32[15,64,128]{2,1,0:T(8,128)S(1)} %get-tuple-element.29), channel_id=1, source_target_pairs={{8,0},{16,8},{24,16},{9,1},{17,9},{25,17},{10,2},{18,10},{26,18},{... | collective-permute-start | bytes 1474568 | tf_op jit(solution)/shard_map/ppermute | solution.py:378
  105.2 3.9 %collective-permute-start.9 = (f32[15,64,128]{2,1,0:T(8,128)S(1)}, f32[15,64,128]{2,1,0:T(8,128)S(1)}, u32[]{:S(2)}, u32[]{:S(2)}) collective-permute-start(f32[15,64,128]{2,1,0:T(8,128)S(1)} %get-tuple-element.28), channel_id=1, source_target_pairs={{0,8},{8,16},{16,24},{1,9},{9,17},{17,25},{2,10},{10,18},{18,26},{... | collective-permute-start | bytes 1474568 | tf_op jit(solution)/shard_map/ppermute | solution.py:378
  109.2 11.2 %second_a.1 = f32[3,16,64,128]{3,2,1,0:T(8,128)S(1)} custom-call(f32[3,16,80,128]{3,2,1,0:T(8,128)S(1)} %get-tuple-element.21.refs_0_.refs_6_, f32[15,80,128]{2,1,0:T(8,128)S(1)} %collective-permute-done.5.refs_1_, f32[15,80,128]{2,1,0:T(8,128)S(1)} %collective-permute-done.6.refs_2_, f32[3,22,96,128]{3,2,1,0:T(8,128)S(1)} %get-tuple-element.24.refs_3_, ...), custom_call_target="tpu_custom_call" | custom-call | flops 1 | bytes 13819904 | tf_op jit(solution)/shard_map/second_a/pallas_call | solution.py:382
  120.3 11.1 %second_b.1 = f32[3,16,64,128]{3,2,1,0:T(8,128)S(1)} custom-call(f32[3,16,80,128]{3,2,1,0:T(8,128)S(1)} %get-tuple-element.27.refs_0_, f32[15,80,128]{2,1,0:T(8,128)S(1)} %collective-permute-done.5.refs_1_, f32[15,80,128]{2,1,0:T(8,128)S(1)} %collective-permute-done.6.refs_2_, f32[15,64,128]{2,1,0:T(8,128)S(1)} %collective-permute-done.9.refs_3_, ...), custom_call_target="tpu_custom_call" | custom-call | flops 1 | bytes 14532608 | tf_op jit(solution)/shard_map/second_b/pallas_call | solution.py:382
  131.7 2.3 %copy.18 = f32[3,128,16,128]{3,2,1,0:T(8,128)} copy(f32[3,128,16,128]{1,3,2,0:T(8,128)S(1)} %maximum_bitcast_fusion) | data formatting | bytes 6291456 | tf_op jit(solution)/shard_map/transpose | solution.py:439
  134.1 3.0 %slice.186 = f32[256,16,128]{2,1,0:T(8,128)} slice(f32[384,16,128]{2,1,0:T(8,128)} %bitcast.51), slice={[32:288], [0:16], [0:128]} | slice | bytes 4194304 | tf_op jit(solution)/shard_map/slice | solution.py:440
  (61 shorter events, 18.2 us)
Async XLA Ops:
  0.0 21.3 %copy-start.5 = (s32[4,4,2]{1,2,0:T(2,128)S(1)}, s32[4,4,2]{1,2,0:T(2,128)}, u32[]{:S(2)}) copy-start(s32[4,4,2]{1,2,0:T(2,128)} %param.11) | copy-start | bytes 388
  0.8 21.2 %copy-start.3 = (f32[256,16,128]{2,1,0:T(8,128)S(1)}, f32[256,16,128]{2,1,0:T(8,128)}, u32[]{:S(2)}) copy-start(f32[256,16,128]{2,1,0:T(8,128)} %param.6) | copy-start | bytes 6291460
  2.1 19.8 %collective-permute-start = (f32[65,16,128]{2,1,0:T(8,128)S(1)}, f32[65,16,128]{2,1,0:T(8,128)S(1)}, u32[]{:S(2)}, u32[]{:S(2)}) collective-permute-start(f32[65,16,128]{2,1,0:T(8,128)S(1)} %pad_maximum_fusion), channel_id=1, source_target_pairs={{0,1},{1,0},{2,3},{3,2},{4,5},{5,4},{6,7},{7,6},{8,9},{9,8},{10,11... | collective-permute-start | bytes 1597448 | tf_op jit(solution)/shard_map/ppermute | solution.py:292
  21.9 3.4 %copy-start.4 = (f32[65,16,128]{2,1,0:T(8,128)}, f32[65,16,128]{2,1,0:T(8,128)S(1)}, u32[]{:S(2)}) copy-start(f32[65,16,128]{2,1,0:T(8,128)S(1)} %collective-permute-done) | copy-start | bytes 1597444
  30.3 8.3 %collective-permute-start.1 = (f32[3,192,128]{2,1,0:T(8,128)}, f32[3,192,128]{2,1,0:T(8,128)}, u32[]{:S(2)}, u32[]{:S(2)}) collective-permute-start(f32[3,192,128]{2,1,0:T(8,128)} %reshape.835), channel_id=1, source_target_pairs={{0,2},{2,4},{4,6},{1,3},{3,5},{5,7},{8,10},{10,12},{12,14},{9,11},... | collective-permute-start | bytes 884744 | tf_op jit(solution)/shard_map/ppermute | solution.py:359
  33.9 8.2 %collective-permute-start.2 = (f32[3,192,128]{2,1,0:T(8,128)}, f32[3,192,128]{2,1,0:T(8,128)S(1)}, u32[]{:S(2)}, u32[]{:S(2)}) collective-permute-start(f32[3,192,128]{2,1,0:T(8,128)} %reshape.836), channel_id=1, source_target_pairs={{2,0},{4,2},{6,4},{3,1},{5,3},{7,5},{10,8},{12,10},{14,12},{11,9},... | collective-permute-start | bytes 884744 | tf_op jit(solution)/shard_map/ppermute | solution.py:360
  46.1 20.5 %collective-permute-start.3 = (f32[15,96,128]{2,1,0:T(8,128)S(1)}, f32[15,96,128]{2,1,0:T(8,128)S(1)}, u32[]{:S(2)}, u32[]{:S(2)}) collective-permute-start(f32[15,96,128]{2,1,0:T(8,128)S(1)} %get-tuple-element.19), channel_id=1, source_target_pairs={{0,8},{8,16},{16,24},{1,9},{9,17},{17,25},{2,10},{10,18},{18,26},{... | collective-permute-start | bytes 2211848 | tf_op jit(solution)/shard_map/ppermute | solution.py:378
  49.6 20.3 %collective-permute-start.4 = (f32[15,96,128]{2,1,0:T(8,128)S(1)}, f32[15,96,128]{2,1,0:T(8,128)S(1)}, u32[]{:S(2)}, u32[]{:S(2)}) collective-permute-start(f32[15,96,128]{2,1,0:T(8,128)S(1)} %get-tuple-element.20), channel_id=1, source_target_pairs={{8,0},{16,8},{24,16},{9,1},{17,9},{25,17},{10,2},{18,10},{26,18},{... | collective-permute-start | bytes 2211848 | tf_op jit(solution)/shard_map/ppermute | solution.py:378
  52.8 37.6 %collective-permute-start.7 = (f32[15,56,128]{2,1,0:T(8,128)S(1)}, f32[15,56,128]{2,1,0:T(8,128)S(1)}, u32[]{:S(2)}, u32[]{:S(2)}) collective-permute-start(f32[15,56,128]{2,1,0:T(8,128)S(1)} %get-tuple-element.25), channel_id=1, source_target_pairs={{0,8},{8,16},{16,24},{1,9},{9,17},{17,25},{2,10},{10,18},{18,26},{... | collective-permute-start | bytes 1290248 | tf_op jit(solution)/shard_map/ppermute | solution.py:378
  56.3 34.2 %collective-permute-start.8 = (f32[15,56,128]{2,1,0:T(8,128)S(1)}, f32[15,56,128]{2,1,0:T(8,128)S(1)}, u32[]{:S(2)}, u32[]{:S(2)}) collective-permute-start(f32[15,56,128]{2,1,0:T(8,128)S(1)} %get-tuple-element.26), channel_id=1, source_target_pairs={{8,0},{16,8},{24,16},{9,1},{17,9},{25,17},{10,2},{18,10},{26,18},{... | collective-permute-start | bytes 1290248 | tf_op jit(solution)/shard_map/ppermute | solution.py:378
  59.4 10.5 %copy-start = (bf16[2,256,256]{2,1,0:T(8,128)(2,1)S(1)}, bf16[2,256,256]{2,1,0:T(8,128)(2,1)}, u32[]{:S(2)}) copy-start(bf16[2,256,256]{2,1,0:T(8,128)(2,1)} %get-tuple-element.49.refs_9_.refs_12_.refs_11_) | copy-start | bytes 786436
  59.4 10.4 %copy-start.1 = (bf16[2,256,256]{2,1,0:T(8,128)(2,1)S(1)}, bf16[2,256,256]{2,1,0:T(8,128)(2,1)}, u32[]{:S(2)}) copy-start(bf16[2,256,256]{2,1,0:T(8,128)(2,1)} %get-tuple-element.50.refs_8_.refs_11_.refs_10_) | copy-start | bytes 786436
  59.4 10.4 %copy-start.2 = (bf16[2,256,256]{2,1,0:T(8,128)(2,1)S(1)}, bf16[2,256,256]{2,1,0:T(8,128)(2,1)}, u32[]{:S(2)}) copy-start(bf16[2,256,256]{2,1,0:T(8,128)(2,1)} %get-tuple-element.51.refs_7_.refs_10_.refs_9_) | copy-start | bytes 786436
  84.6 24.5 %collective-permute-start.5 = (f32[15,80,128]{2,1,0:T(8,128)S(1)}, f32[15,80,128]{2,1,0:T(8,128)S(1)}, u32[]{:S(2)}, u32[]{:S(2)}) collective-permute-start(f32[15,80,128]{2,1,0:T(8,128)S(1)} %get-tuple-element.22), channel_id=1, source_target_pairs={{0,8},{8,16},{16,24},{1,9},{9,17},{17,25},{2,10},{10,18},{18,26},{... | collective-permute-start | bytes 1843208 | tf_op jit(solution)/shard_map/ppermute | solution.py:378
  88.1 21.1 %collective-permute-start.6 = (f32[15,80,128]{2,1,0:T(8,128)S(1)}, f32[15,80,128]{2,1,0:T(8,128)S(1)}, u32[]{:S(2)}, u32[]{:S(2)}) collective-permute-start(f32[15,80,128]{2,1,0:T(8,128)S(1)} %get-tuple-element.23), channel_id=1, source_target_pairs={{8,0},{16,8},{24,16},{9,1},{17,9},{25,17},{10,2},{18,10},{26,18},{... | collective-permute-start | bytes 1843208 | tf_op jit(solution)/shard_map/ppermute | solution.py:378
  103.3 17.1 %collective-permute-start.10 = (f32[15,64,128]{2,1,0:T(8,128)S(1)}, f32[15,64,128]{2,1,0:T(8,128)S(1)}, u32[]{:S(2)}, u32[]{:S(2)}) collective-permute-start(f32[15,64,128]{2,1,0:T(8,128)S(1)} %get-tuple-element.29), channel_id=1, source_target_pairs={{8,0},{16,8},{24,16},{9,1},{17,9},{25,17},{10,2},{18,10},{26,18},{... | collective-permute-start | bytes 1474568 | tf_op jit(solution)/shard_map/ppermute | solution.py:378
  105.2 15.1 %collective-permute-start.9 = (f32[15,64,128]{2,1,0:T(8,128)S(1)}, f32[15,64,128]{2,1,0:T(8,128)S(1)}, u32[]{:S(2)}, u32[]{:S(2)}) collective-permute-start(f32[15,64,128]{2,1,0:T(8,128)S(1)} %get-tuple-element.28), channel_id=1, source_target_pairs={{0,8},{8,16},{16,24},{1,9},{9,17},{17,25},{2,10},{10,18},{18,26},{... | collective-permute-start | bytes 1474568 | tf_op jit(solution)/shard_map/ppermute | solution.py:378

commit v2 on v1

--- a/solution.py
+++ b/solution.py
@@ -132,15 +132,65 @@
         lax.fori_loop(0, width, ystep, 0)
 
 
-def assemble_kernel(packed, hx, cut, vol_ref, low_ref, high_ref, ext_ref, *pays):
+def band_kernel(psf_ref, fh_ref, fl_ref, bh_ref, bl_ref):
+    windows, size = fh_ref.shape[:2]
+    taps = psf_ref.shape[0]
+    total = psf_ref[0]
+    for j in range(1, taps):
+        total = total + psf_ref[j]
+    step = LANES // 2
+    for r in range(0, size, step):
+        shape = (step, size)
+        cols = lax.broadcasted_iota(jnp.int32, shape, 1)
+        off = cols - lax.broadcasted_iota(jnp.int32, shape, 0) - r + (taps - 1) // 2
+        band, flip = jnp.zeros(shape, jnp.float32), jnp.zeros(shape, jnp.float32)
+        for j in range(taps):
+            band = jnp.where(off == j, psf_ref[j], band)
+            flip = jnp.where(off == taps - 1 - j, psf_ref[j], flip)
+        for matrix, hi_ref, lo_ref in ((band, fh_ref, fl_ref), (flip, bh_ref, bl_ref)):
+            matrix = matrix / jnp.full(shape, total, jnp.float32)
+            for w in range(windows):
+                first = 0 if w == 0 else LANES // 2
+                last = size if w == windows - 1 else LANES + LANES // 2
+                part = jnp.where((cols >= first) & (cols < last), matrix, 0.0)
+                hi = part.astype(jnp.bfloat16)
+                hi_ref[w, r : r + step, :] = hi
+                lo_ref[w, r : r + step, :] = (part - hi.astype(jnp.float32)).astype(jnp.bfloat16)
+
+
+def edges_kernel(hy, after, vol_ref, low_ref, high_ref, *diags):
+    tiles, cx, cy = vol_ref.shape[:3]
+    for x in range(cx):
+        to = slice(hy * x, hy * x + hy)
+        for ref, rows, diag in ((low_ref, slice(cy - hy, cy), 0), (high_ref, slice(0, hy), 1)):
+            for t in range(tiles):
+                ref[t, to, :] = vol_ref[t, x, rows, :]
+            if diags:
+                lane = lax.broadcasted_iota(jnp.int32, (hy, LANES), 1)
+                diags[diag][to, :] = jnp.where(lane < after, vol_ref[tiles - 1, x, rows, :], vol_ref[0, x, rows, :])
+
+
+def assemble_kernel(packed, hx, cut, after, refs_in, *refs):
+    vol_ref, low_ref, high_ref = refs[:3]
+    halo_ref, low_z, high_z = refs[3:6] if refs_in == 6 else (None,) * 3
+    ext_ref, *pays = refs[refs_in:]
     tiles, cx, cy = vol_ref.shape[:3]
     hy = low_ref.shape[1] // cx
     end = cy + 2 * hy
+
+    def merge(t, value, halo, rows):
+        if halo is None or 0 < t < tiles - 1:
+            return value
+        lane = lax.broadcasted_iota(jnp.int32, value.shape, 1)
+        use = lane < after if t == 0 else (lane >= after) & (lane < 2 * after)
+        return jnp.where(use, halo[rows], value)
+
     for t in range(tiles):
         for x in range(cx):
-            ext_ref[t, x, 0:hy, :] = low_ref[t, hy * x : hy * x + hy, :]
-            ext_ref[t, x, hy : hy + cy, :] = vol_ref[t, x]
-            ext_ref[t, x, hy + cy : end, :] = high_ref[t, hy * x : hy * x + hy, :]
+            edge = slice(hy * x, hy * x + hy)
+            ext_ref[t, x, 0:hy, :] = merge(t, low_ref[t, edge, :], low_z, edge)
+            ext_ref[t, x, hy : hy + cy, :] = merge(t, vol_ref[t, x], halo_ref, x)
+            ext_ref[t, x, hy + cy : end, :] = merge(t, high_ref[t, edge, :], high_z, edge)
             ext_ref[t, x, end:, :] = jnp.zeros((ext_ref.shape[2] - end, LANES), jnp.float32)
     for n, (pay_up, pay_down) in enumerate((pays[:2], pays[2:])):
         first, last = (0, cut) if n == 0 else (cut, end)
@@ -300,8 +350,13 @@
         before, after = first[:hz], second[:hz]
         ids_before, ids_after = first[hz].reshape(-1)[:hz], second[hz].reshape(-1)[:hz]
     pad = tiles * LANES - nz - 2 * hz
-    volume = jnp.concatenate([before, observed, after, jnp.zeros((pad, cx, cy), f32)], axis=0)
     ids = jnp.concatenate([ids_before, zones, ids_after, jnp.full((pad,), -1.0, f32)])
+    direct = slabs == 2 and nz % LANES == 0 and 2 * hz <= LANES
+    if direct:
+        volume = jnp.pad(observed, ((hz, hz + pad), (0, 0), (0, 0)))
+        halo = jnp.pad(got[: 2 * hz], ((0, LANES - 2 * hz), (0, 0), (0, 0))).transpose(1, 2, 0)
+    else:
+        volume = jnp.concatenate([before, observed, after, jnp.zeros((pad, cx, cy), f32)], axis=0)
     volume = volume.reshape(tiles, LANES, cx, cy).transpose(0, 2, 3, 1)
 
     match = (ids[None, :] == jnp.arange(lateral_x.shape[0], dtype=f32)[:, None]).astype(f32)
@@ -312,30 +367,6 @@
         return jnp.broadcast_to(table, (tiles, taps, 8, LANES))
 
     tx, ty = lanes_of(lateral_x), lanes_of(lateral_y)
-
-    kernel = depth_psf / jnp.sum(depth_psf)
-    wins = windows_of(tiles)
-    size = wins[0][1] * LANES
-    off = jnp.arange(size)[None, :] - jnp.arange(size)[:, None]
-    band = jnp.zeros((size, size), f32)
-    flip = jnp.zeros((size, size), f32)
-    for j in range(kernel.shape[0]):
-        band = band + jnp.where(off == j - zreach, kernel[j], 0.0)
-        flip = flip + jnp.where(off == zreach - j, kernel[j], 0.0)
-
-    def halves(matrix):
-        cols = jnp.arange(size)
-        parts = []
-        for index in range(len(wins)):
-            low = 0 if index == 0 else LANES // 2
-            high = size if index == len(wins) - 1 else LANES + LANES // 2
-            parts.append(jnp.where((cols >= low) & (cols < high), matrix, 0.0))
-        full = jnp.stack(parts)
-        top = lax.reduce_precision(full, 8, 7)
-        return top.astype(jnp.bfloat16), (full - top).astype(jnp.bfloat16)
-
-    fh, fl = halves(band)
-    bh, bl = halves(flip)
 
     sx, sy = lax.axis_index("sx"), lax.axis_index("sy")
     stacks_x, stacks_y = stitch_width.shape[:2]
@@ -355,10 +386,6 @@
     weight = jnp.where(inside, weight, 0.0).astype(f32)
     weight = jnp.broadcast_to(weight[:, :, None], (cx + 2 * reach, full, LANES))
 
-    up, down = line("sy")
-    low = lax.ppermute(volume[:, :, cy - hy :].reshape(tiles, cx * hy, LANES), "sy", up)
-    high = lax.ppermute(volume[:, :, :hy].reshape(tiles, cx * hy, LANES), "sy", down)
-
     wide = cx + 2 * reach
     packed = nz + 2 * hz - (tiles - 1) * LANES <= LANES // 2
     planes = hx * (tiles - 1) + hx // 2 if packed else hx * tiles
@@ -377,12 +404,12 @@
     def swap(pays):
         return lax.ppermute(pays[0], "sx", up), lax.ppermute(pays[1], "sx", down)
 
-    def call(kernel, out_shape, args, scratch, name, limit, flops):
+    def call(kernel, out_shape, args, scratch, name, limit, flops, specs=VMEM):
         moved = sum(a.size * 4 for a in args) + sum(o.size * 4 for o in out_shape)
         return pl.pallas_call(
             kernel,
             out_shape=out_shape,
-            in_specs=[VMEM] * len(args),
+            in_specs=[specs] * len(args),
             out_specs=[VMEM] * len(out_shape),
             scratch_shapes=[pltpu.VMEM(dims, f32) for dims in scratch],
             compiler_params=pltpu.CompilerParams(vmem_limit_bytes=limit << 20),
@@ -390,10 +417,29 @@
             name=name,
         )(*args)
 
+    wins = windows_of(tiles)
+    size = wins[0][1] * LANES
+    fh, fl, bh, bl = call(
+        band_kernel, [jax.ShapeDtypeStruct((len(wins), size, size), jnp.bfloat16)] * 4, (depth_psf,), [], "band", 8, 1,
+        specs=pl.BlockSpec(memory_space=pltpu.SMEM),
+    )
+
+    stacks = lax.axis_size("sy")
+    edge = shape(tiles, cx * hy, LANES)
+    diag = [shape(cx * hy, LANES)] * 2 if direct else []
+    low, high, *corner = call(functools.partial(edges_kernel, hy, hz), [edge, edge] + diag, (volume,), [], "edges", 8, 1)
+    yup, ydown = line("sy")
+    parts = [volume, lax.ppermute(low, "sy", yup), lax.ppermute(high, "sy", ydown)]
+    if direct:
+        cross = [(2 * i + g, 2 * i + 2 + (1 - g)) for i in range(stacks - 1) for g in range(2)]
+        parts.append(halo)
+        parts.append(lax.ppermute(corner[0], ("sy", "gz"), cross))
+        parts.append(lax.ppermute(corner[1], ("sy", "gz"), [(j, i) for i, j in cross]))
+
     ext, *pays = call(
-        functools.partial(assemble_kernel, packed, hx, cut),
+        functools.partial(assemble_kernel, packed, hx, cut, hz, len(parts)),
         [shape(tiles, cx, full, LANES)] + pay_shapes(cut) + pay_shapes(end0 - cut),
-        (volume, low, high), [], "assemble", 8, 1,
+        tuple(parts), [], "assemble", 8, 1,
     )
     halo_a = swap(pays[:2])
     halo_b = swap(pays[2:])

time: 139 us -> 132 us (0.950)
  other arithmetic: 20.1 us -> 6.15 us
  starting transfers between devices: 30.6 us -> 37 us
  waiting for transfers between devices: 10.5 us -> 7.07 us
  local copies, waits for them, and re-layouts: 17.5 us -> 20.3 us
  Pallas kernels: 58.1 us -> 60.4 us
    select_n x1 -> x0, other arithmetic: 10.9 us -> none  [halves(): parts.append(jnp.where((cols >= low) & (cols < high), matrix, 0.0))]
    ppermute x2 -> x4, starting transfers between devices: 5.54 us -> 12 us  [the longest x1 4.54 us: body(): lax.ppermute(corner[1], ('sy', 'gz'), [(j, i) for i, j in cross])]
    ppermute x2 -> x4, waiting for transfers between devices: 4.44 us -> 0.01 us  [the longest x1 0.01 us: body(): parts.append(lax.ppermute(corner[0], ('sy', 'gz'), cross))]
    reshape x2 -> x0, local copies, waits for them, and re-layouts: 3.46 us -> none  [the longest x1 1.73 us: body(): volume[:, :, cy - hy:].reshape(tiles, cx * hy, LANES)]
    concatenate x1 -> x0, other arithmetic: 3.29 us -> none  [body(): jnp.concatenate([before, observed, after, jnp.zeros((pad, cx, cy), f32)],...]
    unnamed x14 -> x25, local copies, waits for them, and re-layouts: 1.56 us -> 4.7 us
    pallas_call x6 -> x8, Pallas kernels: 58.1 us -> 60.4 us  [call(): pl.pallas_call(kernel, out_shape=out_shape, in_specs=[specs] * len(args),...]
    pad x0 -> x1, local copies, waits for them, and re-layouts: none -> 1.85 us  [body(): volume = jnp.pad(observed, ((hz, hz + pad), (0, 0), (0, 0)))]
  transfers between devices with their start and end apart: 11 -> 13, of which waited for: 4 -> 2; matrix products, arithmetic and copies ran while one was open for 16% -> 12% of each run, Pallas kernels for 31% -> 34%
where the time goes in v2:
time: 132 us; the launch traced here: 131 us
  Pallas kernels  60.4 us (46%)
  starting transfers between devices  37 us (28%)
  local copies, waits for them, and re-layouts  20.3 us (15%)
  waiting for transfers between devices  7.07 us (5%)
  other arithmetic  6.15 us (5%)
    pallas_call x8, Pallas kernels, call(): pl.pallas_call(kernel, out_shape=out_shape, in_specs=[specs] * len(args),...  60.4 us
    ppermute x8, starting transfers between devices, swap(): return (lax.ppermute(pays[0], 'sx', up), lax.ppermute(pays[1], 'sx', down))  23.5 us
    ppermute x8, waiting for transfers between devices, swap(): return (lax.ppermute(pays[0], 'sx', up), lax.ppermute(pays[1], 'sx', down))  7.06 us
    unnamed x25, local copies, waits for them, and re-layouts  4.7 us
    ppermute x1, starting transfers between devices, body(): lax.ppermute(corner[1], ('sy', 'gz'), [(j, i) for i, j in cross])  4.54 us
    ppermute x1, starting transfers between devices, body(): lax.ppermute(high, 'sy', ydown)  3.64 us
    slice x1, local copies, waits for them, and re-layouts, body(): return result[hz:hz + nz]  3.04 us
  transfers between devices with their start and end apart: 13, of which 2 were waited for; matrix products, arithmetic and copies ran while one was open for 12% of the time, Pallas kernels for 34%

profile of v2, /device:TPU:10, one launch (start us, length us, event | category | flops | bytes accessed | tf_op | source)
XLA Modules:
  0.0 131.3 jit_solution(14690395767915236501)
XLA Ops:
  6.3 2.4 %copy.24 = f32[3,128,16,128]{1,3,2,0:T(8,128)S(1)} copy(f32[3,128,16,128]{3,2,1,0:T(8,128)} %bitcast.35) | data formatting | bytes 6291456 | tf_op jit(solution)/shard_map/reshape | solution.py:360
  9.6 1.9 %collective-permute-start = (f32[3,192,128]{2,1,0:T(8,128)}, f32[3,192,128]{2,1,0:T(8,128)}, u32[]{:S(2)}, u32[]{:S(2)}) collective-permute-start(f32[3,192,128]{2,1,0:T(8,128)} %get-tuple-element.26), channel_id=1, source_target_pairs={{0,2},{2,4},{4,6},{1,3},{3,5},{5,7},{8,10},{10,12},{12,14},{9,11},... | collective-permute-start | bytes 884744 | tf_op jit(solution)/shard_map/ppermute | solution.py:432
  11.5 3.6 %collective-permute-start.1 = (f32[3,192,128]{2,1,0:T(8,128)}, f32[3,192,128]{2,1,0:T(8,128)}, u32[]{:S(2)}, u32[]{:S(2)}) collective-permute-start(f32[3,192,128]{2,1,0:T(8,128)} %get-tuple-element.27), channel_id=1, source_target_pairs={{2,0},{4,2},{6,4},{3,1},{5,3},{7,5},{10,8},{12,10},{14,12},{11,9},... | collective-permute-start | bytes 884744 | tf_op jit(solution)/shard_map/ppermute | solution.py:432
  15.2 1.9 %collective-permute-start.3 = (f32[192,128]{1,0:T(8,128)}, f32[192,128]{1,0:T(8,128)S(1)}, u32[]{:S(2)}, u32[]{:S(2)}) collective-permute-start(f32[192,128]{1,0:T(8,128)} %get-tuple-element.28), channel_id=1, source_target_pairs={{0,3},{1,2},{2,5},{3,4},{4,7},{5,6},{8,11},{9,10},{10,13},{11,12},... | collective-permute-start | bytes 294920 | tf_op jit(solution)/shard_map/ppermute | solution.py:436
  17.1 4.5 %collective-permute-start.4 = (f32[192,128]{1,0:T(8,128)}, f32[192,128]{1,0:T(8,128)}, u32[]{:S(2)}, u32[]{:S(2)}) collective-permute-start(f32[192,128]{1,0:T(8,128)} %get-tuple-element.29), channel_id=1, source_target_pairs={{3,0},{2,1},{5,2},{4,3},{7,4},{6,5},{11,8},{10,9},{13,10},{12,11},... | collective-permute-start | bytes 294920 | tf_op jit(solution)/shard_map/ppermute | solution.py:437
  31.4 2.4 %copy.29 = f32[64,16,128]{0,2,1:T(8,128)} copy(f32[64,16,128]{2,1,0:T(8,128)} %slice.80) | data formatting | bytes 1048576
  35.1 4.1 %assemble.1 = (f32[3,16,160,128]{3,2,1,0:T(8,128)S(1)}, f32[15,96,128]{2,1,0:T(8,128)S(1)}, f32[15,96,128]{2,1,0:T(8,128)S(1)}, f32[15,56,128]{2,1,0:T(8,128)S(1)}, f32[15,56,128]{2,1,0:T(8,128)S(1)}) custom-call(f32[3,16,128,128]{3,2,1,0:T(8,128)S(1)} %bitcast.34, f32[3,192,128]{2,1,0:T(8,128)} %collective-permute-done.refs_1_, ...), custom_call_target="tpu_custom_call" | custom-call | flops 1 | bytes 11247616 | tf_op jit(solution)/shard_map/assemble/pallas_call | solution.py:409
  39.3 3.5 %collective-permute-start.5 = (f32[15,96,128]{2,1,0:T(8,128)S(1)}, f32[15,96,128]{2,1,0:T(8,128)S(1)}, u32[]{:S(2)}, u32[]{:S(2)}) collective-permute-start(f32[15,96,128]{2,1,0:T(8,128)S(1)} %get-tuple-element.31), channel_id=1, source_target_pairs={{0,8},{8,16},{16,24},{1,9},{9,17},{17,25},{2,10},{10,18},{18,26},{... | collective-permute-start | bytes 2211848 | tf_op jit(solution)/shard_map/ppermute | solution.py:405
  42.7 2.4 %collective-permute-start.6 = (f32[15,96,128]{2,1,0:T(8,128)S(1)}, f32[15,96,128]{2,1,0:T(8,128)S(1)}, u32[]{:S(2)}, u32[]{:S(2)}) collective-permute-start(f32[15,96,128]{2,1,0:T(8,128)S(1)} %get-tuple-element.32), channel_id=1, source_target_pairs={{8,0},{16,8},{24,16},{9,1},{17,9},{25,17},{10,2},{18,10},{26,18},{... | collective-permute-start | bytes 2211848 | tf_op jit(solution)/shard_map/ppermute | solution.py:405
  45.1 1.9 %collective-permute-start.10 = (f32[15,56,128]{2,1,0:T(8,128)S(1)}, f32[15,56,128]{2,1,0:T(8,128)S(1)}, u32[]{:S(2)}, u32[]{:S(2)}) collective-permute-start(f32[15,56,128]{2,1,0:T(8,128)S(1)} %get-tuple-element.42), channel_id=1, source_target_pairs={{8,0},{16,8},{24,16},{9,1},{17,9},{25,17},{10,2},{18,10},{26,18},{... | collective-permute-start | bytes 1290248 | tf_op jit(solution)/shard_map/ppermute | solution.py:405
  47.1 3.9 %collective-permute-start.9 = (f32[15,56,128]{2,1,0:T(8,128)S(1)}, f32[15,56,128]{2,1,0:T(8,128)S(1)}, u32[]{:S(2)}, u32[]{:S(2)}) collective-permute-start(f32[15,56,128]{2,1,0:T(8,128)S(1)} %get-tuple-element.41), channel_id=1, source_target_pairs={{0,8},{8,16},{16,24},{1,9},{9,17},{17,25},{2,10},{10,18},{18,26},{... | collective-permute-start | bytes 1290248 | tf_op jit(solution)/shard_map/ppermute | solution.py:405
  52.6 4.4 %norm.1.refs_4_.refs_7_.refs_6_ = f32[3,16,144,128]{3,2,1,0:T(8,128)S(1)} custom-call(f32[22,160,128]{2,1,0:T(8,128)S(1)} %broadcast_in_dim.222.w_ref.refs_3_.refs_5_, f32[3,7,8,128]{3,2,1,0:T(8,128)S(1)} %broadcast_in_dim.225.tx_ref.refs_5_.refs_8_.refs_7_, f32[3,7,8,128]{3,2,1,0:T(8,128)S(1)} %broadcast_in_dim.227.ty_ref.refs_6_.refs_9_.refs_8_), custom_call_target="tpu_custom_call" | custom-call | flops 1 | bytes 5513216 | tf_op jit(solution)/shard_map/norm/pallas_call | solution.py:409
  57.0 3.5 %collective-permute-done.5.refs_1_ = f32[15,96,128]{2,1,0:T(8,128)S(1)} collective-permute-done((f32[15,96,128]{2,1,0:T(8,128)S(1)}, f32[15,96,128]{2,1,0:T(8,128)S(1)}, u32[]{:S(2)}, u32[]{:S(2)}) %collective-permute-start.5) | collective-permute-done | bytes 737312 | tf_op jit(solution)/shard_map/ppermute | solution.py:405
  60.5 3.5 %collective-permute-done.6.refs_2_ = f32[15,96,128]{2,1,0:T(8,128)S(1)} collective-permute-done((f32[15,96,128]{2,1,0:T(8,128)S(1)}, f32[15,96,128]{2,1,0:T(8,128)S(1)}, u32[]{:S(2)}, u32[]{:S(2)}) %collective-permute-start.6) | collective-permute-done | bytes 737312 | tf_op jit(solution)/shard_map/ppermute | solution.py:405
  64.0 14.6 %first_a.1 = (f32[3,16,80,128]{3,2,1,0:T(8,128)S(1)}, f32[3,22,96,128]{3,2,1,0:T(8,128)S(1)}, f32[15,80,128]{2,1,0:T(8,128)S(1)}, f32[15,80,128]{2,1,0:T(8,128)S(1)}) custom-call(f32[3,16,160,128]{3,2,1,0:T(8,128)S(1)} %get-tuple-element.30.refs_0_, f32[15,96,128]{2,1,0:T(8,128)S(1)} %collective-permute-done.5.refs_1_, ...), custom_call_target="tpu_custom_call" | custom-call | flops 1 | bytes 19456000 | tf_op jit(solution)/shard_map/first_a/pallas_call | solution.py:409
  78.6 3.5 %collective-permute-start.7 = (f32[15,80,128]{2,1,0:T(8,128)S(1)}, f32[15,80,128]{2,1,0:T(8,128)S(1)}, u32[]{:S(2)}, u32[]{:S(2)}) collective-permute-start(f32[15,80,128]{2,1,0:T(8,128)S(1)} %get-tuple-element.38), channel_id=1, source_target_pairs={{0,8},{8,16},{16,24},{1,9},{9,17},{17,25},{2,10},{10,18},{18,26},{... | collective-permute-start | bytes 1843208 | tf_op jit(solution)/shard_map/ppermute | solution.py:405
  82.1 2.4 %collective-permute-start.8 = (f32[15,80,128]{2,1,0:T(8,128)S(1)}, f32[15,80,128]{2,1,0:T(8,128)S(1)}, u32[]{:S(2)}, u32[]{:S(2)}) collective-permute-start(f32[15,80,128]{2,1,0:T(8,128)S(1)} %get-tuple-element.39), channel_id=1, source_target_pairs={{8,0},{16,8},{24,16},{9,1},{17,9},{25,17},{10,2},{18,10},{26,18},{... | collective-permute-start | bytes 1843208 | tf_op jit(solution)/shard_map/ppermute | solution.py:405
  84.6 12.8 %first_b.1 = (f32[3,16,80,128]{3,2,1,0:T(8,128)S(1)}, f32[3,22,88,128]{3,2,1,0:T(8,128)S(1)}, f32[15,64,128]{2,1,0:T(8,128)S(1)}, f32[15,64,128]{2,1,0:T(8,128)S(1)}) custom-call(f32[3,16,160,128]{3,2,1,0:T(8,128)S(1)} %get-tuple-element.30.refs_0_, f32[15,96,128]{2,1,0:T(8,128)S(1)} %collective-permute-done.5.refs_1_, ...), custom_call_target="tpu_custom_call" | custom-call | flops 1 | bytes 21766144 | tf_op jit(solution)/shard_map/first_b/pallas_call | solution.py:409
  97.4 3.4 %collective-permute-start.11 = (f32[15,64,128]{2,1,0:T(8,128)S(1)}, f32[15,64,128]{2,1,0:T(8,128)S(1)}, u32[]{:S(2)}, u32[]{:S(2)}) collective-permute-start(f32[15,64,128]{2,1,0:T(8,128)S(1)} %get-tuple-element.44), channel_id=1, source_target_pairs={{0,8},{8,16},{16,24},{1,9},{9,17},{17,25},{2,10},{10,18},{18,26},{... | collective-permute-start | bytes 1474568 | tf_op jit(solution)/shard_map/ppermute | solution.py:405
  100.8 2.5 %collective-permute-start.12 = (f32[15,64,128]{2,1,0:T(8,128)S(1)}, f32[15,64,128]{2,1,0:T(8,128)S(1)}, u32[]{:S(2)}, u32[]{:S(2)}) collective-permute-start(f32[15,64,128]{2,1,0:T(8,128)S(1)} %get-tuple-element.45), channel_id=1, source_target_pairs={{8,0},{16,8},{24,16},{9,1},{17,9},{25,17},{10,2},{18,10},{26,18},{... | collective-permute-start | bytes 1474568 | tf_op jit(solution)/shard_map/ppermute | solution.py:405
  103.3 11.2 %second_a.1 = f32[3,16,64,128]{3,2,1,0:T(8,128)S(1)} custom-call(f32[3,16,80,128]{3,2,1,0:T(8,128)S(1)} %get-tuple-element.37.refs_0_.refs_6_, f32[15,80,128]{2,1,0:T(8,128)S(1)} %collective-permute-done.7.refs_1_, f32[15,80,128]{2,1,0:T(8,128)S(1)} %collective-permute-done.8.refs_2_, f32[3,22,96,128]{3,2,1,0:T(8,128)S(1)} %get-tuple-element.40.refs_3_, ...), custom_call_target="tpu_custom_call" | custom-call | flops 1 | bytes 13819904 | tf_op jit(solution)/shard_map/second_a/pallas_call | solution.py:409
  114.5 11.1 %second_b.1 = f32[3,16,64,128]{3,2,1,0:T(8,128)S(1)} custom-call(f32[3,16,80,128]{3,2,1,0:T(8,128)S(1)} %get-tuple-element.43.refs_0_, f32[15,80,128]{2,1,0:T(8,128)S(1)} %collective-permute-done.7.refs_1_, f32[15,80,128]{2,1,0:T(8,128)S(1)} %collective-permute-done.8.refs_2_, f32[15,64,128]{2,1,0:T(8,128)S(1)} %collective-permute-done.11.refs_3_, ...), custom_call_target="tpu_custom_call" | custom-call | flops 1 | bytes 14532608 | tf_op jit(solution)/shard_map/second_b/pallas_call | solution.py:409
  125.9 2.4 %copy.28 = f32[3,128,16,128]{3,2,1,0:T(8,128)} copy(f32[3,128,16,128]{1,3,2,0:T(8,128)S(1)} %maximum_bitcast_fusion) | data formatting | bytes 6291456 | tf_op jit(solution)/shard_map/transpose | solution.py:485
  128.3 3.0 %slice.86 = f32[256,16,128]{2,1,0:T(8,128)} slice(f32[384,16,128]{2,1,0:T(8,128)} %bitcast.36), slice={[32:288], [0:16], [0:128]} | slice | bytes 4194304 | tf_op jit(solution)/shard_map/slice | solution.py:486
  (66 shorter events, 20.0 us)
Async XLA Ops:
  0.0 4.4 %copy-start.7 = (f32[256,16,128]{2,1,0:T(8,128)S(1)}, f32[256,16,128]{2,1,0:T(8,128)}, u32[]{:S(2)}) copy-start(f32[256,16,128]{2,1,0:T(8,128)} %param.6) | copy-start | bytes 6291460
  2.9 26.6 %collective-permute-start.2 = (f32[65,16,128]{2,1,0:T(8,128)}, f32[65,16,128]{2,1,0:T(8,128)}, u32[]{:S(2)}, u32[]{:S(2)}) collective-permute-start(f32[65,16,128]{2,1,0:T(8,128)} %pad_maximum_fusion), channel_id=1, source_target_pairs={{0,1},{1,0},{2,3},{3,2},{4,5},{5,4},{6,7},{7,6},{8,9},{9,8},{10,11... | collective-permute-start | bytes 1597448 | tf_op jit(solution)/shard_map/ppermute | solution.py:342
  8.6 15.4 %copy-start.9 = (f32[8,7]{1,0:T(8,128)S(1)}, f32[8,7]{1,0:T(8,128)}, u32[]{:S(2)}) copy-start(f32[8,7]{1,0:T(8,128)} %param.8) | copy-start | bytes 676
  8.7 15.4 %copy-start.10 = (f32[8,7]{1,0:T(8,128)S(1)}, f32[8,7]{1,0:T(8,128)}, u32[]{:S(2)}) copy-start(f32[8,7]{1,0:T(8,128)} %param.9) | copy-start | bytes 676
  8.7 15.5 %copy-start.6 = (f32[17]{0:T(128)S(1)}, f32[17]{0:T(128)}, u32[]{:S(2)}) copy-start(f32[17]{0:T(128)} %psf_ref.1) | copy-start | bytes 208
  8.7 18.8 %copy-start.8 = (s32[4,4,2]{1,2,0:T(2,128)S(1)}, s32[4,4,2]{1,2,0:T(2,128)}, u32[]{:S(2)}) copy-start(s32[4,4,2]{1,2,0:T(2,128)} %param.11) | copy-start | bytes 388
  9.6 25.5 %collective-permute-start = (f32[3,192,128]{2,1,0:T(8,128)}, f32[3,192,128]{2,1,0:T(8,128)}, u32[]{:S(2)}, u32[]{:S(2)}) collective-permute-start(f32[3,192,128]{2,1,0:T(8,128)} %get-tuple-element.26), channel_id=1, source_target_pairs={{0,2},{2,4},{4,6},{1,3},{3,5},{5,7},{8,10},{10,12},{12,14},{9,11},... | collective-permute-start | bytes 884744 | tf_op jit(solution)/shard_map/ppermute | solution.py:432
  11.5 23.6 %collective-permute-start.1 = (f32[3,192,128]{2,1,0:T(8,128)}, f32[3,192,128]{2,1,0:T(8,128)}, u32[]{:S(2)}, u32[]{:S(2)}) collective-permute-start(f32[3,192,128]{2,1,0:T(8,128)} %get-tuple-element.27), channel_id=1, source_target_pairs={{2,0},{4,2},{6,4},{3,1},{5,3},{7,5},{10,8},{12,10},{14,12},{11,9},... | collective-permute-start | bytes 884744 | tf_op jit(solution)/shard_map/ppermute | solution.py:432
  15.2 19.9 %collective-permute-start.3 = (f32[192,128]{1,0:T(8,128)}, f32[192,128]{1,0:T(8,128)S(1)}, u32[]{:S(2)}, u32[]{:S(2)}) collective-permute-start(f32[192,128]{1,0:T(8,128)} %get-tuple-element.28), channel_id=1, source_target_pairs={{0,3},{1,2},{2,5},{3,4},{4,7},{5,6},{8,11},{9,10},{10,13},{11,12},... | collective-permute-start | bytes 294920 | tf_op jit(solution)/shard_map/ppermute | solution.py:436
  17.1 18.0 %collective-permute-start.4 = (f32[192,128]{1,0:T(8,128)}, f32[192,128]{1,0:T(8,128)}, u32[]{:S(2)}, u32[]{:S(2)}) collective-permute-start(f32[192,128]{1,0:T(8,128)} %get-tuple-element.29), channel_id=1, source_target_pairs={{3,0},{2,1},{5,2},{4,3},{7,4},{6,5},{11,8},{10,9},{13,10},{12,11},... | collective-permute-start | bytes 294920 | tf_op jit(solution)/shard_map/ppermute | solution.py:437
  25.4 0.7 copy-start
  26.1 0.7 copy-start.2
  26.8 0.7 copy-start.4
  39.3 21.2 %collective-permute-start.5 = (f32[15,96,128]{2,1,0:T(8,128)S(1)}, f32[15,96,128]{2,1,0:T(8,128)S(1)}, u32[]{:S(2)}, u32[]{:S(2)}) collective-permute-start(f32[15,96,128]{2,1,0:T(8,128)S(1)} %get-tuple-element.31), channel_id=1, source_target_pairs={{0,8},{8,16},{16,24},{1,9},{9,17},{17,25},{2,10},{10,18},{18,26},{... | collective-permute-start | bytes 2211848 | tf_op jit(solution)/shard_map/ppermute | solution.py:405
  42.7 21.3 %collective-permute-start.6 = (f32[15,96,128]{2,1,0:T(8,128)S(1)}, f32[15,96,128]{2,1,0:T(8,128)S(1)}, u32[]{:S(2)}, u32[]{:S(2)}) collective-permute-start(f32[15,96,128]{2,1,0:T(8,128)S(1)} %get-tuple-element.32), channel_id=1, source_target_pairs={{8,0},{16,8},{24,16},{9,1},{17,9},{25,17},{10,2},{18,10},{26,18},{... | collective-permute-start | bytes 2211848 | tf_op jit(solution)/shard_map/ppermute | solution.py:405
  45.1 39.4 %collective-permute-start.10 = (f32[15,56,128]{2,1,0:T(8,128)S(1)}, f32[15,56,128]{2,1,0:T(8,128)S(1)}, u32[]{:S(2)}, u32[]{:S(2)}) collective-permute-start(f32[15,56,128]{2,1,0:T(8,128)S(1)} %get-tuple-element.42), channel_id=1, source_target_pairs={{8,0},{16,8},{24,16},{9,1},{17,9},{25,17},{10,2},{18,10},{26,18},{... | collective-permute-start | bytes 1290248 | tf_op jit(solution)/shard_map/ppermute | solution.py:405
  47.1 37.5 %collective-permute-start.9 = (f32[15,56,128]{2,1,0:T(8,128)S(1)}, f32[15,56,128]{2,1,0:T(8,128)S(1)}, u32[]{:S(2)}, u32[]{:S(2)}) collective-permute-start(f32[15,56,128]{2,1,0:T(8,128)S(1)} %get-tuple-element.41), channel_id=1, source_target_pairs={{0,8},{8,16},{16,24},{1,9},{9,17},{17,25},{2,10},{10,18},{18,26},{... | collective-permute-start | bytes 1290248 | tf_op jit(solution)/shard_map/ppermute | solution.py:405
  52.5 11.5 %copy-start.1 = (bf16[2,256,256]{2,1,0:T(8,128)(2,1)S(1)}, bf16[2,256,256]{2,1,0:T(8,128)(2,1)}, u32[]{:S(2)}) copy-start(bf16[2,256,256]{2,1,0:T(8,128)(2,1)} %copy-done) | copy-start | bytes 786436
  52.5 11.5 %copy-start.3 = (bf16[2,256,256]{2,1,0:T(8,128)(2,1)S(1)}, bf16[2,256,256]{2,1,0:T(8,128)(2,1)}, u32[]{:S(2)}) copy-start(bf16[2,256,256]{2,1,0:T(8,128)(2,1)} %copy-done.2) | copy-start | bytes 786436
  52.5 11.5 %copy-start.5 = (bf16[2,256,256]{2,1,0:T(8,128)(2,1)S(1)}, bf16[2,256,256]{2,1,0:T(8,128)(2,1)}, u32[]{:S(2)}) copy-start(bf16[2,256,256]{2,1,0:T(8,128)(2,1)} %copy-done.4) | copy-start | bytes 786436
  78.6 24.6 %collective-permute-start.7 = (f32[15,80,128]{2,1,0:T(8,128)S(1)}, f32[15,80,128]{2,1,0:T(8,128)S(1)}, u32[]{:S(2)}, u32[]{:S(2)}) collective-permute-start(f32[15,80,128]{2,1,0:T(8,128)S(1)} %get-tuple-element.38), channel_id=1, source_target_pairs={{0,8},{8,16},{16,24},{1,9},{9,17},{17,25},{2,10},{10,18},{18,26},{... | collective-permute-start | bytes 1843208 | tf_op jit(solution)/shard_map/ppermute | solution.py:405
  82.1 21.2 %collective-permute-start.8 = (f32[15,80,128]{2,1,0:T(8,128)S(1)}, f32[15,80,128]{2,1,0:T(8,128)S(1)}, u32[]{:S(2)}, u32[]{:S(2)}) collective-permute-start(f32[15,80,128]{2,1,0:T(8,128)S(1)} %get-tuple-element.39), channel_id=1, source_target_pairs={{8,0},{16,8},{24,16},{9,1},{17,9},{25,17},{10,2},{18,10},{26,18},{... | collective-permute-start | bytes 1843208 | tf_op jit(solution)/shard_map/ppermute | solution.py:405
  97.4 17.1 %collective-permute-start.11 = (f32[15,64,128]{2,1,0:T(8,128)S(1)}, f32[15,64,128]{2,1,0:T(8,128)S(1)}, u32[]{:S(2)}, u32[]{:S(2)}) collective-permute-start(f32[15,64,128]{2,1,0:T(8,128)S(1)} %get-tuple-element.44), channel_id=1, source_target_pairs={{0,8},{8,16},{16,24},{1,9},{9,17},{17,25},{2,10},{10,18},{18,26},{... | collective-permute-start | bytes 1474568 | tf_op jit(solution)/shard_map/ppermute | solution.py:405
  100.8 13.7 %collective-permute-start.12 = (f32[15,64,128]{2,1,0:T(8,128)S(1)}, f32[15,64,128]{2,1,0:T(8,128)S(1)}, u32[]{:S(2)}, u32[]{:S(2)}) collective-permute-start(f32[15,64,128]{2,1,0:T(8,128)S(1)} %get-tuple-element.45), channel_id=1, source_target_pairs={{8,0},{16,8},{24,16},{9,1},{17,9},{25,17},{10,2},{18,10},{26,18},{... | collective-permute-start | bytes 1474568 | tf_op jit(solution)/shard_map/ppermute | solution.py:405

commit v3 on v2

--- a/solution.py
+++ b/solution.py
@@ -85,22 +85,88 @@
     return [(0, tiles)] if tiles <= 2 else [(w, 2) for w in range(tiles - 1)]
 
 
-def depth_rows(parts, hi_ref, lo_ref):
-    tiles = len(parts)
+def depth_rows(parts, hi_ref, lo_ref, shifted=False):
     split = []
     for part in parts:
         hi = part.astype(jnp.bfloat16)
         split.append((hi, (part - hi.astype(jnp.float32)).astype(jnp.bfloat16)))
-    out = [None] * tiles
-    for index, (first, span) in enumerate(windows_of(tiles)):
+    dot = functools.partial(jnp.dot, preferred_element_type=jnp.float32)
+    out = {}
+    for index, (first, span) in enumerate(windows_of(len(parts))):
         his = jnp.concatenate([split[first + s][0] for s in range(span)], axis=1)
         los = jnp.concatenate([split[first + s][1] for s in range(span)], axis=1)
-        dot = functools.partial(jnp.dot, preferred_element_type=jnp.float32)
         res = dot(his, hi_ref[index]) + (dot(los, hi_ref[index]) + dot(his, lo_ref[index]))
-        for s in range(span):
+        for s in range(res.shape[1] // LANES):
+            to = s if shifted else first + s
             piece = res[:, s * LANES : (s + 1) * LANES]
-            out[first + s] = piece if out[first + s] is None else out[first + s] + piece
-    return out
+            out[to] = out[to] + piece if to in out else piece
+    return [out[t] for t in range(len(out))]
+
+
+def x_loop(taps, reverse, first, last, rows_in, rows_out):
+    tiles, count = taps.shape[:2]
+
+    def step(j, carry):
+        for t in range(tiles):
+            k = [taps[t, count - 1 - a if reverse else a] for a in range(count)]
+            for n, v in enumerate(rows_in(t, j)):
+                rows_out(t, j, n, conv_rows(k, v, len(v) - count + 1))
+        return carry
+
+    if first < last:
+        lax.fori_loop(first, last, step, 0)
+
+
+def y_pair(mid_ref, taps, t, i, blocks):
+    count = taps.shape[1]
+    k = [taps[t, b] for b in range(count)]
+    out = []
+    for x in (2 * i, 2 * i + 1):
+        for j in range(blocks):
+            acc = k[0] * mid_ref[t, x, 8 * j : 8 * j + 8, :]
+            for b in range(1, count):
+                acc = acc + k[b] * mid_ref[t, x, 8 * j + b : 8 * j + b + 8, :]
+            out.append(acc)
+    return jnp.concatenate(out, axis=0)
+
+
+def correct(mid_ref, ty_ref, mats, shifted, pairs, rows, data_of, spread_ref, at=lambda i: 2 * i):
+    fh_ref, fl_ref, bh_ref, bl_ref = mats
+    tiles = mid_ref.shape[0]
+
+    def depth(i, carry):
+        blurred = depth_rows([y_pair(mid_ref, ty_ref, t, i, rows // 8) for t in range(tiles)], fh_ref, fl_ref)
+        ratio = [data_of(t, i) / jnp.maximum(blurred[t], TINY) for t in range(tiles)]
+        for t, value in enumerate(depth_rows(ratio, bh_ref, bl_ref, shifted)):
+            spread_ref[t, pl.ds(2 * i, 2), 0:rows, :] = value.reshape(2, rows, LANES)
+        return carry
+
+    lax.fori_loop(0, pairs, depth, 0)
+
+
+def inner_kernel(plan, est_ref, obs_ref, w_ref, tx_ref, ty_ref, fh_ref, fl_ref, bh_ref, bl_ref, spread_ref, mid_ref):
+    tiles, cx = est_ref.shape[:2]
+    reach = (tx_ref.shape[1] - 1) // 2
+    rows = spread_ref.shape[2]
+    first = plan["data_off"] + reach
+    count = cx - 2 * reach
+
+    def rows_in(t, j):
+        here = pl.ds(pl.multiple_of(8 * j, 8), 8)
+        return [[est_ref[t, x, here, :] for x in range(cx)]]
+
+    def rows_out(t, j, n, values):
+        here = pl.ds(pl.multiple_of(8 * j, 8), 8)
+        for x, value in enumerate(values):
+            mid_ref[t, x, here, :] = value
+
+    x_loop(tx_ref, False, 0, -(-plan["need"] // 8), rows_in, rows_out)
+
+    def data_of(t, i):
+        seen = obs_ref[t, pl.ds(2 * i + reach, 2), first : first + rows, :]
+        return (seen * w_ref[pl.ds(2 * i + 2 * reach, 2), first : first + rows, :]).reshape(2 * rows, LANES)
+
+    correct(mid_ref, ty_ref, (fh_ref, fl_ref, bh_ref, bl_ref), plan["shifted"], count // 2, rows, data_of, spread_ref)
 
 
 def norm_kernel(w_ref, tx_ref, ty_ref, out_ref, mid_ref):
@@ -132,7 +198,7 @@
         lax.fori_loop(0, width, ystep, 0)
 
 
-def band_kernel(psf_ref, fh_ref, fl_ref, bh_ref, bl_ref):
+def band_kernel(lane0, psf_ref, fh_ref, fl_ref, bh_ref, bl_ref, sh_ref, sl_ref):
     windows, size = fh_ref.shape[:2]
     taps = psf_ref.shape[0]
     total = psf_ref[0]
@@ -156,6 +222,20 @@
                 hi = part.astype(jnp.bfloat16)
                 hi_ref[w, r : r + step, :] = hi
                 lo_ref[w, r : r + step, :] = (part - hi.astype(jnp.float32)).astype(jnp.bfloat16)
+        shape = (step, sh_ref.shape[2])
+        for w in range(windows):
+            ext = lax.broadcasted_iota(jnp.int32, shape, 0) + r + w * LANES
+            off = ext - lax.broadcasted_iota(jnp.int32, shape, 1) - lane0 + (taps - 1) // 2
+            part = jnp.zeros(shape, jnp.float32)
+            first = 0 if w == 0 else LANES // 2
+            last = size if w == windows - 1 else LANES + LANES // 2
+            if first <= r < last:
+                for j in range(taps):
+                    part = jnp.where(off == j, psf_ref[j], part)
+                part = part / jnp.full(shape, total, jnp.float32)
+            hi = part.astype(jnp.bfloat16)
+            sh_ref[w, r : r + step, :] = hi
+            sl_ref[w, r : r + step, :] = (part - hi.astype(jnp.float32)).astype(jnp.bfloat16)
 
 
 def edges_kernel(hy, after, vol_ref, low_ref, high_ref, *diags):
@@ -199,124 +279,121 @@
         pack_rows(ext_ref, pay_down, packed, hx, 0, blocks, first // 8, 0)
 
 
-def iterate_kernel(plan, *refs):
+def outer_kernel(plan, *refs):
     refs = list(refs)
     take = refs.pop
     est_ref = take(0)
     halos = [(take(0), take(0), first, last) for first, last in plan["halos"]]
-    w_ref = take(0) if plan["make_data"] else None
-    data_in = None if plan["make_data"] else take(0)
-    tail_ref = take(0) if plan["tail"] else None
-    inv_ref, tx_ref, ty_ref, fh_ref, fl_ref, bh_ref, bl_ref = [take(0) for _ in range(7)]
+    make = plan["make_data"]
+    w_ref = take(0) if make else None
+    data_in = None if make else take(0)
+    prior_ref = take(0) if plan["prior"] else None
+    inner_ref, inv_ref, tx_ref, ty_ref, bx_ref, by_ref = [take(0) for _ in range(6)]
+    mats = [take(0) for _ in range(4)]
     out_ref = take(0)
-    data_ref = take(0) if plan["make_data"] else data_in
+    data_ref = take(0) if make else data_in
     pays = [take(0), take(0)] if plan["pay"] else None
-    mid_ref, blur_ref = refs
+    mid_ref, edge_ref = refs
     packed, hx, low, high = plan["packed"], plan["hx"], plan["low"], plan["high"]
-    est_base, data_base, data_off, inv_off = plan["est_base"], plan["data_base"], plan["data_off"], plan["inv_off"]
+    data_base, off, lane0 = plan["data_base"], plan["data_off"], plan["lane0"]
     tiles, cx = est_ref.shape[:2]
+    outs = out_ref.shape[0]
     count = tx_ref.shape[1]
     reach = (count - 1) // 2
-    wide = cx + 2 * reach
-    rows = blur_ref.shape[2]
+    rows = edge_ref.shape[2]
     last_block = -(-(high + 4 * reach) // 8)
-    data_first = data_base // 8 if plan["make_data"] else low // 8
-    half = (hx - 2 * reach) // 2
-
-    for t in range(tiles):
-        k = [tx_ref[t, a] for a in range(count)]
-        for lo_ref, hi_ref, first, last in halos:
-
-            def gather(j, t=t, lo_ref=lo_ref, hi_ref=hi_ref, first=first):
-                here = pl.ds(pl.multiple_of(8 * j - est_base, 8), 8)
-                there = pl.ds(pl.multiple_of(8 * j - first, 8), 8)
-                v = [halo_row(lo_ref, tiles, packed, hx, t, p, there) for p in range(hx)]
-                v += [est_ref[t, x, here, :] for x in range(cx)]
-                return v + [halo_row(hi_ref, tiles, packed, hx, t, p, there) for p in range(hx)]
-
-            def keep(j, v, t=t):
-                here = pl.ds(pl.multiple_of(8 * j, 8), 8)
-                there = pl.ds(pl.multiple_of(8 * j - data_base, 8), 8)
-                for x in range(wide):
-                    data_ref[t, x, there, :] = w_ref[x, here, :] * v[x + reach]
-
-            def only_data(j, carry, gather=gather, keep=keep):
-                keep(j, gather(j))
-                return carry
-
-            def step(j, carry, gather=gather, keep=keep, k=k, t=t):
-                v = gather(j)
-                if plan["make_data"]:
-                    keep(j, v)
-                mid = pl.ds(pl.multiple_of(8 * j - low, 8), 8)
-                for x, acc in enumerate(conv_rows(k, v, wide)):
-                    mid_ref[t, x, mid, :] = acc
-                return carry
-
-            a, b = max(first // 8, data_first), min(last // 8, low // 8)
-            if plan["make_data"] and a < b:
-                lax.fori_loop(a, b, only_data, 0)
-            a, b = max(first // 8, low // 8), min(-(-last // 8), last_block)
-            if a < b:
-                lax.fori_loop(a, b, step, 0)
-
-        def put(t, x, j, acc):
-            blur_ref[t, x, 8 * j : 8 * j + 8, :] = acc
-
-        y_conv(mid_ref, ty_ref, False, t, wide, rows // 8, put)
-
-    spot0 = low + data_off + reach - data_base
-
-    def depth(i, carry):
-        spot = pl.ds(2 * i, 2)
-        size = 2 * rows
-        parts = [blur_ref[t, spot].reshape(size, LANES) for t in range(tiles)]
-        blurred = depth_rows(parts, fh_ref, fl_ref)
-        ratio = []
-        for t in range(tiles):
-            seen = data_ref[t, spot, spot0 : spot0 + rows, :].reshape(size, LANES)
-            ratio.append(seen / jnp.maximum(blurred[t], TINY))
-        spread = depth_rows(ratio, bh_ref, bl_ref)
-        for t in range(tiles):
-            blur_ref[t, spot] = spread[t].reshape(2, rows, LANES)
-        return carry
-
-    lax.fori_loop(0, wide // 2, depth, 0)
-
-    out_skip = plan["tail"]
+    data_first = data_base // 8 if make else low // 8
+
+    for lo_ref, hi_ref, first, last in halos:
+
+        def rows_in(t, j, lo_ref=lo_ref, hi_ref=hi_ref, first=first):
+            here = pl.ds(pl.multiple_of(8 * j, 8), 8)
+            there = pl.ds(pl.multiple_of(8 * j - first, 8), 8)
+            one = [halo_row(lo_ref, tiles, packed, hx, t, p, there) for p in range(hx)]
+            one += [est_ref[t, x, here, :] for x in range(hx)]
+            two = [est_ref[t, x, here, :] for x in range(cx - hx, cx)]
+            two += [halo_row(hi_ref, tiles, packed, hx, t, p, there) for p in range(hx)]
+            return [one, two]
+
+        def keep(t, j, pair):
+            here = pl.ds(pl.multiple_of(8 * j, 8), 8)
+            there = pl.ds(pl.multiple_of(8 * j - data_base, 8), 8)
+            for n, v in enumerate(pair):
+                for x in range(hx):
+                    data_ref[t, hx * n + x, there, :] = w_ref[x + cx * n, here, :] * v[x + reach]
+
+        def rows_in_keep(t, j, rows_in=rows_in, keep=keep):
+            pair = rows_in(t, j)
+            if make:
+                keep(t, j, pair)
+            return pair
+
+        def rows_out(t, j, n, values):
+            mid = pl.ds(pl.multiple_of(8 * j - low, 8), 8)
+            for x, value in enumerate(values):
+                mid_ref[t, hx * n + x, mid, :] = value
+
+        def only_data(j, carry, rows_in=rows_in, keep=keep):
+            for t in range(tiles):
+                keep(t, j, rows_in(t, j))
+            return carry
+
+        a, b = max(first // 8, data_first), min(last // 8, low // 8)
+        if make and a < b:
+            lax.fori_loop(a, b, only_data, 0)
+        x_loop(tx_ref, False, max(first // 8, low // 8), min(-(-last // 8), last_block), rows_in_keep, rows_out)
+
+    spot0 = low + off + reach - data_base
+
+    def data_of(t, i):
+        return data_ref[t, pl.ds(2 * i, 2), spot0 : spot0 + rows, :].reshape(2 * rows, LANES)
+
+    correct(mid_ref, ty_ref, mats, plan["shifted"], hx, rows, data_of, edge_ref)
+
     blocks = -(-(high - low) // 8)
-    for t in range(tiles):
-        k = [tx_ref[t, count - 1 - a] for a in range(count)]
-
-        def back(j, carry, k=k, t=t):
-            here = pl.ds(pl.multiple_of(8 * j, 8), 8)
-            v = [blur_ref[t, x, here, :] for x in range(wide)]
-            for x, acc in enumerate(conv_rows(k, v, cx)):
-                mid_ref[t, x, here, :] = acc
-            return carry
-
-        lax.fori_loop(0, rows // 8, back, 0)
-
-        def finish(t, x, j, acc):
-            at = 8 * j + low + 2 * reach - est_base
-            to = 8 * j + out_skip
-            scale = 8 * j + low + inv_off
-            out_ref[t, x, to : to + 8, :] = est_ref[t, x, at : at + 8, :] * acc * inv_ref[t, x, scale : scale + 8, :]
-
-        y_conv(mid_ref, ty_ref, True, t, cx, blocks, finish)
-
-    if out_skip:
-        have = tail_ref.shape[2]
-        for t in range(tiles):
+
+    def back_in(t, j):
+        here = pl.ds(pl.multiple_of(8 * j, 8), 8)
+        there = pl.ds(pl.multiple_of(8 * j + low, 8), 8)
+        v = [edge_ref[t, x, here, :] for x in range(hx)]
+        v += [inner_ref[t, x, there, :] for x in range(cx - 2 * reach)]
+        return [v + [edge_ref[t, x, here, :] for x in range(hx, 2 * hx)]]
+
+    def back_out(t, j, n, values):
+        here = pl.ds(pl.multiple_of(8 * j, 8), 8)
+        for x, value in enumerate(values):
+            mid_ref[t, x, here, :] = value
+
+    x_loop(bx_ref, True, 0, rows // 8, back_in, back_out)
+    base = low if prior_ref is not None else 0
+
+    def finish(t, x, j, acc):
+        at = 8 * j + low + 2 * reach
+        scale = 8 * j + low + off
+        old = est_ref[t, x, at : at + 8, :] * inv_ref[t, x, scale : scale + 8, :]
+        if lane0:
+            if t + 1 < tiles:
+                more = est_ref[t + 1, x, at : at + 8, :] * inv_ref[t + 1, x, scale : scale + 8, :]
+                lane = lax.broadcasted_iota(jnp.int32, (8, LANES), 1)
+                old = jnp.where(lane >= lane0, old, more)
+            old = pltpu.roll(old, LANES - lane0, 1)
+        to = 8 * j + base
+        out_ref[t, x, to : to + 8, :] = old * acc
+
+    for t in range(outs):
+        y_conv(mid_ref, by_ref, True, t, cx, blocks, finish)
+
+    if prior_ref is not None:
+        for t in range(outs):
 
             def copy(x, carry, t=t):
-                out_ref[t, x, 0:out_skip, :] = tail_ref[t, x, have - out_skip : have, :]
+                out_ref[t, x, 0:low, :] = prior_ref[t, x, 0:low, :]
                 return carry
 
             lax.fori_loop(0, cx, copy, 0)
     if pays:
-        pack_rows(out_ref, pays[0], packed, hx, cx - hx, blocks, out_skip // 8, 0)
-        pack_rows(out_ref, pays[1], packed, hx, 0, blocks, out_skip // 8, 0)
+        pack_rows(out_ref, pays[0], packed, hx, cx - hx, blocks, base // 8, 0)
+        pack_rows(out_ref, pays[1], packed, hx, 0, blocks, base // 8, 0)
 
 
 def body(observed, zone_of_slice, lateral_x, lateral_y, depth_psf, stitch_width):
@@ -359,14 +436,16 @@
         volume = jnp.concatenate([before, observed, after, jnp.zeros((pad, cx, cy), f32)], axis=0)
     volume = volume.reshape(tiles, LANES, cx, cy).transpose(0, 2, 3, 1)
 
-    match = (ids[None, :] == jnp.arange(lateral_x.shape[0], dtype=f32)[:, None]).astype(f32)
-
-    def lanes_of(kernels):
+    def lanes_of(kernels, names):
+        match = (names[None, :] == jnp.arange(lateral_x.shape[0], dtype=f32)[:, None]).astype(f32)
         table = jnp.sum(match[:, None, :] * kernels[:, :, None], axis=0)
-        table = table.reshape(taps, tiles, 1, LANES).transpose(1, 0, 2, 3)
-        return jnp.broadcast_to(table, (tiles, taps, 8, LANES))
-
-    tx, ty = lanes_of(lateral_x), lanes_of(lateral_y)
+        table = table.reshape(taps, -1, 1, LANES).transpose(1, 0, 2, 3)
+        return jnp.broadcast_to(table, (table.shape[0], taps, 8, LANES))
+
+    tx, ty = lanes_of(lateral_x, ids), lanes_of(lateral_y, ids)
+    own = ceil_to(nz, LANES) // LANES
+    own_ids = jnp.concatenate([zones, jnp.full((own * LANES - nz,), -1.0, f32)])
+    tx_own, ty_own = lanes_of(lateral_x, own_ids), lanes_of(lateral_y, own_ids)
 
     sx, sy = lax.axis_index("sx"), lax.axis_index("sy")
     stacks_x, stacks_y = stitch_width.shape[:2]
@@ -419,8 +498,11 @@
 
     wins = windows_of(tiles)
     size = wins[0][1] * LANES
-    fh, fl, bh, bl = call(
-        band_kernel, [jax.ShapeDtypeStruct((len(wins), size, size), jnp.bfloat16)] * 4, (depth_psf,), [], "band", 8, 1,
+    fh, fl, bh, bl, sh, sl = call(
+        functools.partial(band_kernel, hz),
+        [jax.ShapeDtypeStruct((len(wins), size, size), jnp.bfloat16)] * 4
+        + [jax.ShapeDtypeStruct((len(wins), size, own * LANES), jnp.bfloat16)] * 2,
+        (depth_psf,), [], "band", 8, 1,
         specs=pl.BlockSpec(memory_space=pltpu.SMEM),
     )
 
@@ -447,43 +529,55 @@
         norm_kernel, [shape(tiles, cx, ceil_to(end1, 8), LANES)], (weight, tx, ty),
         [(1, cx, full, LANES)], "norm", 8, 1,
     )
-    tables = (inv, tx, ty, fh, fl, bh, bl)
-
-    def iterate(name, est, halos, extra, plan, outs):
+    shift = 2 * reach
+
+    def inner(name, est, data_off, shifted, rows, need, back):
+        plan = dict(data_off=data_off, shifted=shifted, need=need)
+        args = (est, ext, weight, tx, ty, fh, fl) + back
+        rows = ceil_to(rows, 8)
+        return call(
+            functools.partial(inner_kernel, plan),
+            [shape(own if shifted else tiles, cx - shift, rows, LANES)], args,
+            [(tiles, cx - shift, rows + 16, LANES)], name, 24, 1,
+        )[0]
+
+    def outer(name, est, halos, extra, inner_part, last, plan, outs):
         rows = ceil_to(plan["high"] - plan["low"] + 2 * reach, 8)
-        args = (est,) + tuple(h for _, pair in halos for h in pair) + extra + tables
-        plan = dict(plan, hx=hx, packed=packed, halos=[rng for rng, _ in halos])
-        scratch = [(tiles, wide, rows + 16, LANES), (tiles, wide, rows, LANES)]
-        return call(functools.partial(iterate_kernel, plan), outs, args, scratch, name, 16, 1)
+        back, lateral = ((sh, sl), (tx_own, ty_own)) if last else ((bh, bl), (tx, ty))
+        args = (est,) + tuple(h for _, pair in halos for h in pair) + extra
+        args += (inner_part, inv, tx, ty) + lateral + (fh, fl) + back
+        plan = dict(
+            plan, hx=hx, packed=packed, halos=[rng for rng, _ in halos], make_data=not last, pay=not last,
+            shifted=last, data_off=shift if last else 0, lane0=hz if last else 0,
+        )
+        scratch = [(tiles, cx, rows + 16, LANES), (own if last else tiles, 2 * hx, rows, LANES)]
+        return call(functools.partial(outer_kernel, plan), outs, args, scratch, name, 16, 1)
 
     data_at = mid2 + 8
-    est_a, data_a, *pays = iterate(
-        "first_a", ext, [((0, cut), halo_a)], (weight,),
-        dict(low=0, high=mid1, est_base=0, data_base=0, data_off=0, inv_off=0, make_data=True, tail=0, pay=True),
-        [shape(tiles, cx, mid1, LANES), shape(tiles, wide, cut, LANES)] + pay_shapes(mid1),
+    spread1 = inner("inner_1", ext, 0, False, end1 + shift, end0, (bh, bl))
+    est_a, data_a, *pays = outer(
+        "outer_1a", ext, [((0, cut), halo_a)], (weight,), spread1, False,
+        dict(low=0, high=mid1, data_base=0, prior=False),
+        [shape(tiles, cx, mid1, LANES), shape(tiles, 2 * hx, cut, LANES)] + pay_shapes(mid1),
     )
     halo_c = swap(pays)
-    tail = mid1 - mid2
-    est_b, data_b, *pays = iterate(
-        "first_b", ext, [((0, cut), halo_a), ((cut, end0), halo_b)], (weight, est_a),
-        dict(low=mid1, high=end1, est_base=0, data_base=data_at, data_off=0, inv_off=0, make_data=True, tail=tail, pay=True),
-        [shape(tiles, cx, ceil_to(end1, 8) - mid2, LANES), shape(tiles, wide, full - data_at, LANES)] + pay_shapes(end1 - mid1),
+    est, data_b, *pays = outer(
+        "outer_1b", ext, [((0, cut), halo_a), ((cut, end0), halo_b)], (weight, est_a), spread1, False,
+        dict(low=mid1, high=end1, data_base=data_at, prior=True),
+        [shape(tiles, cx, ceil_to(end1, 8), LANES), shape(tiles, 2 * hx, full - data_at, LANES)] + pay_shapes(end1 - mid1),
     )
     halo_d = swap(pays)
-    shift = 2 * reach
-    (out_a,) = iterate(
-        "second_a", est_a, [((0, mid1), halo_c)], (data_a,),
-        dict(low=0, high=mid2, est_base=0, data_base=0, data_off=shift, inv_off=shift, make_data=False, tail=0, pay=False),
-        [shape(tiles, cx, mid2, LANES)],
-    )
-    (out_b,) = iterate(
-        "second_b", est_b, [((0, mid1), halo_c), ((mid1, end1), halo_d)], (data_b,),
-        dict(low=mid2, high=end2, est_base=mid2, data_base=data_at, data_off=shift, inv_off=shift, make_data=False, tail=0, pay=False),
-        [shape(tiles, cx, end2 - mid2, LANES)],
+    spread2 = inner("inner_2", est, shift, True, end2 + shift, end1, (sh, sl))
+    (out_a,) = outer(
+        "outer_2a", est, [((0, mid1), halo_c)], (data_a,), spread2, True,
+        dict(low=0, high=mid2, data_base=0, prior=False), [shape(own, cx, mid2, LANES)],
+    )
+    (out_b,) = outer(
+        "outer_2b", est, [((0, mid1), halo_c), ((mid1, end1), halo_d)], (data_b,), spread2, True,
+        dict(low=mid2, high=end2, data_base=data_at, prior=False), [shape(own, cx, end2 - mid2, LANES)],
     )
     estimate = jnp.concatenate([out_a, out_b], axis=2)
-    result = estimate.transpose(0, 3, 1, 2).reshape(tiles * LANES, cx, cy)
-    return result[hz : hz + nz]
+    return estimate.transpose(0, 3, 1, 2).reshape(own * LANES, cx, cy)[:nz]
 
 
 def solution(mesh):

time: 132 us -> 122 us (0.924)
  waiting for transfers between devices: 7.07 us -> 1.28 us
  Pallas kernels: 60.4 us -> 57.9 us
  local copies, waits for them, and re-layouts: 20.3 us -> 18.4 us
    ppermute x8, waiting for transfers between devices: 7.06 us -> 1.27 us  [swap(): return (lax.ppermute(pays[0], 'sx', up), lax.ppermute(pays[1], 'sx', down))]
    slice x1 -> x0, local copies, waits for them, and re-layouts: 3.04 us -> none  [body(): return result[hz:hz + nz]]
    pallas_call x8 -> x10, Pallas kernels: 60.4 us -> 57.9 us  [call(): pl.pallas_call(kernel, out_shape=out_shape, in_specs=[specs] * len(args),...]
    unnamed x25 -> x33, local copies, waits for them, and re-layouts: 4.7 us -> 6.17 us
  transfers between devices with their start and end apart: 13 -> 13, of which waited for: 2 -> 1; matrix products, arithmetic and copies ran while one was open for 12% -> 13% of each run, Pallas kernels for 34% -> 37%
where the time goes in v3:
time: 122 us; the launch traced here: 121 us
  Pallas kernels  57.9 us (47%)
  starting transfers between devices  37 us (30%)
  local copies, waits for them, and re-layouts  18.4 us (15%)
  other arithmetic  6.3 us (5%)
  waiting for transfers between devices  1.28 us (1%)
    pallas_call x10, Pallas kernels, call(): pl.pallas_call(kernel, out_shape=out_shape, in_specs=[specs] * len(args),...  57.9 us
    ppermute x8, starting transfers between devices, swap(): return (lax.ppermute(pays[0], 'sx', up), lax.ppermute(pays[1], 'sx', down))  23.4 us
    unnamed x33, local copies, waits for them, and re-layouts  6.17 us
    ppermute x1, starting transfers between devices, body(): lax.ppermute(corner[1], ('sy', 'gz'), [(j, i) for i, j in cross])  4.54 us
    ppermute x1, starting transfers between devices, body(): lax.ppermute(high, 'sy', ydown)  3.64 us
  transfers between devices with their start and end apart: 13, of which 1 were waited for; matrix products, arithmetic and copies ran while one was open for 13% of the time, Pallas kernels for 37%

profile of v3, /device:TPU:10, one launch (start us, length us, event | category | flops | bytes accessed | tf_op | source)
XLA Modules:
  0.0 121.2 jit_solution(16204912092097727195)
XLA Ops:
  6.2 2.4 %copy.28 = f32[3,128,16,128]{1,3,2,0:T(8,128)S(1)} copy(f32[3,128,16,128]{3,2,1,0:T(8,128)} %bitcast.45) | data formatting | bytes 6291456 | tf_op jit(solution)/shard_map/reshape | solution.py:437
  9.6 1.9 %collective-permute-start = (f32[3,192,128]{2,1,0:T(8,128)}, f32[3,192,128]{2,1,0:T(8,128)}, u32[]{:S(2)}, u32[]{:S(2)}) collective-permute-start(f32[3,192,128]{2,1,0:T(8,128)} %get-tuple-element.28), channel_id=1, source_target_pairs={{0,2},{2,4},{4,6},{1,3},{3,5},{5,7},{8,10},{10,12},{12,14},{9,11},... | collective-permute-start | bytes 884744 | tf_op jit(solution)/shard_map/ppermute | solution.py:514
  11.5 3.6 %collective-permute-start.1 = (f32[3,192,128]{2,1,0:T(8,128)}, f32[3,192,128]{2,1,0:T(8,128)}, u32[]{:S(2)}, u32[]{:S(2)}) collective-permute-start(f32[3,192,128]{2,1,0:T(8,128)} %get-tuple-element.29), channel_id=1, source_target_pairs={{2,0},{4,2},{6,4},{3,1},{5,3},{7,5},{10,8},{12,10},{14,12},{11,9},... | collective-permute-start | bytes 884744 | tf_op jit(solution)/shard_map/ppermute | solution.py:514
  15.2 1.9 %collective-permute-start.3 = (f32[192,128]{1,0:T(8,128)}, f32[192,128]{1,0:T(8,128)S(1)}, u32[]{:S(2)}, u32[]{:S(2)}) collective-permute-start(f32[192,128]{1,0:T(8,128)} %get-tuple-element.30), channel_id=1, source_target_pairs={{0,3},{1,2},{2,5},{3,4},{4,7},{5,6},{8,11},{9,10},{10,13},{11,12},... | collective-permute-start | bytes 294920 | tf_op jit(solution)/shard_map/ppermute | solution.py:518
  17.1 4.5 %collective-permute-start.4 = (f32[192,128]{1,0:T(8,128)}, f32[192,128]{1,0:T(8,128)}, u32[]{:S(2)}, u32[]{:S(2)}) collective-permute-start(f32[192,128]{1,0:T(8,128)} %get-tuple-element.31), channel_id=1, source_target_pairs={{3,0},{2,1},{5,2},{4,3},{7,4},{6,5},{11,8},{10,9},{13,10},{12,11},... | collective-permute-start | bytes 294920 | tf_op jit(solution)/shard_map/ppermute | solution.py:519
  31.7 1.9 %slice.76 = f32[64,16,128]{2,1,0:T(8,128)} slice(f32[65,16,128]{2,1,0:T(8,128)} %collective-permute-done.2), slice={[0:64], [0:16], [0:128]} | slice | bytes 1048576 | tf_op jit(solution)/shard_map/slice | solution.py:434
  33.5 2.4 %copy.37 = f32[64,16,128]{0,2,1:T(8,128)} copy(f32[64,16,128]{2,1,0:T(8,128)} %slice.76) | data formatting | bytes 1048576
  37.3 4.1 %assemble.1 = (f32[3,16,160,128]{3,2,1,0:T(8,128)S(1)}, f32[15,96,128]{2,1,0:T(8,128)S(1)}, f32[15,96,128]{2,1,0:T(8,128)S(1)}, f32[15,56,128]{2,1,0:T(8,128)S(1)}, f32[15,56,128]{2,1,0:T(8,128)S(1)}) custom-call(f32[3,16,128,128]{3,2,1,0:T(8,128)S(1)} %bitcast.44, f32[3,192,128]{2,1,0:T(8,128)} %collective-permute-done.refs_1_, ...), custom_call_target="tpu_custom_call" | custom-call | flops 1 | bytes 11247616 | tf_op jit(solution)/shard_map/assemble/pallas_call | solution.py:488
  41.4 3.5 %collective-permute-start.5 = (f32[15,96,128]{2,1,0:T(8,128)S(1)}, f32[15,96,128]{2,1,0:T(8,128)S(1)}, u32[]{:S(2)}, u32[]{:S(2)}) collective-permute-start(f32[15,96,128]{2,1,0:T(8,128)S(1)} %get-tuple-element.33), channel_id=1, source_target_pairs={{0,8},{8,16},{16,24},{1,9},{9,17},{17,25},{2,10},{10,18},{18,26},{... | collective-permute-start | bytes 2211848 | tf_op jit(solution)/shard_map/ppermute | solution.py:484
  44.9 2.4 %collective-permute-start.6 = (f32[15,96,128]{2,1,0:T(8,128)S(1)}, f32[15,96,128]{2,1,0:T(8,128)S(1)}, u32[]{:S(2)}, u32[]{:S(2)}) collective-permute-start(f32[15,96,128]{2,1,0:T(8,128)S(1)} %get-tuple-element.34), channel_id=1, source_target_pairs={{8,0},{16,8},{24,16},{9,1},{17,9},{25,17},{10,2},{18,10},{26,18},{... | collective-permute-start | bytes 2211848 | tf_op jit(solution)/shard_map/ppermute | solution.py:484
  47.3 3.4 %collective-permute-start.7 = (f32[15,56,128]{2,1,0:T(8,128)S(1)}, f32[15,56,128]{2,1,0:T(8,128)S(1)}, u32[]{:S(2)}, u32[]{:S(2)}) collective-permute-start(f32[15,56,128]{2,1,0:T(8,128)S(1)} %get-tuple-element.35), channel_id=1, source_target_pairs={{0,8},{8,16},{16,24},{1,9},{9,17},{17,25},{2,10},{10,18},{18,26},{... | collective-permute-start | bytes 1290248 | tf_op jit(solution)/shard_map/ppermute | solution.py:484
  50.7 2.4 %collective-permute-start.8 = (f32[15,56,128]{2,1,0:T(8,128)S(1)}, f32[15,56,128]{2,1,0:T(8,128)S(1)}, u32[]{:S(2)}, u32[]{:S(2)}) collective-permute-start(f32[15,56,128]{2,1,0:T(8,128)S(1)} %get-tuple-element.36), channel_id=1, source_target_pairs={{8,0},{16,8},{24,16},{9,1},{17,9},{25,17},{10,2},{18,10},{26,18},{... | collective-permute-start | bytes 1290248 | tf_op jit(solution)/shard_map/ppermute | solution.py:484
  54.8 4.4 %norm.1.refs_5_.refs_8_.refs_7_ = f32[3,16,144,128]{3,2,1,0:T(8,128)S(1)} custom-call(f32[22,160,128]{2,1,0:T(8,128)S(1)} %broadcast_in_dim.246.w_ref.refs_3_.refs_5_, f32[3,7,8,128]{3,2,1,0:T(8,128)S(1)} %broadcast_in_dim.249.tx_ref.refs_6_.refs_8_.refs_9_.refs_11_, f32[3,7,8,128]{3,2,1,0:T(8,128)S(1)} %broadcast_in_dim.251.ty_ref.refs_7_.refs_9_.refs_10_.refs_12_), custom_call_target="tpu_custom_call" | custom-call | flops 1 | bytes 5513216 | tf_op jit(solution)/shard_map/norm/pallas_call | solution.py:488
  59.1 5.7 %inner_1.1.refs_4_.refs_7_ = f32[3,10,152,128]{3,2,1,0:T(8,128)S(1)} custom-call(f32[3,16,160,128]{3,2,1,0:T(8,128)S(1)} %get-tuple-element.32.est_ref.obs_ref.refs_0_, f32[3,16,160,128]{3,2,1,0:T(8,128)S(1)} %get-tuple-element.32.est_ref.obs_ref.refs_0_, f32[22,160,128]{2,1,0:T(8,128)S(1)} %broadcast_in_dim.246.w_ref.refs_3_.refs_5_, ...), custom_call_target="tpu_custom_call" | custom-call | flops 1 | bytes 14270464 | tf_op jit(solution)/shard_map/inner_1/pallas_call | solution.py:488
  66.1 9.1 %outer_1a.1 = (f32[3,16,80,128]{3,2,1,0:T(8,128)S(1)}, f32[3,12,96,128]{3,2,1,0:T(8,128)S(1)}, f32[15,80,128]{2,1,0:T(8,128)S(1)}, f32[15,80,128]{2,1,0:T(8,128)S(1)}) custom-call(f32[3,16,160,128]{3,2,1,0:T(8,128)S(1)} %get-tuple-element.32.est_ref.obs_ref.refs_0_, f32[15,96,128]{2,1,0:T(8,128)S(1)} %collective-permute-done.5.refs_1_, ...), custom_call_target="tpu_custom_call" | custom-call | flops 1 | bytes 20488192 | tf_op jit(solution)/shard_map/outer_1a/pallas_call | solution.py:488
  75.2 2.4 %collective-permute-start.10 = (f32[15,80,128]{2,1,0:T(8,128)S(1)}, f32[15,80,128]{2,1,0:T(8,128)S(1)}, u32[]{:S(2)}, u32[]{:S(2)}) collective-permute-start(f32[15,80,128]{2,1,0:T(8,128)S(1)} %get-tuple-element.44), channel_id=1, source_target_pairs={{8,0},{16,8},{24,16},{9,1},{17,9},{25,17},{10,2},{18,10},{26,18},{... | collective-permute-start | bytes 1843208 | tf_op jit(solution)/shard_map/ppermute | solution.py:484
  77.6 3.4 %collective-permute-start.9 = (f32[15,80,128]{2,1,0:T(8,128)S(1)}, f32[15,80,128]{2,1,0:T(8,128)S(1)}, u32[]{:S(2)}, u32[]{:S(2)}) collective-permute-start(f32[15,80,128]{2,1,0:T(8,128)S(1)} %get-tuple-element.43), channel_id=1, source_target_pairs={{0,8},{8,16},{16,24},{1,9},{9,17},{17,25},{2,10},{10,18},{18,26},{... | collective-permute-start | bytes 1843208 | tf_op jit(solution)/shard_map/ppermute | solution.py:484
  81.1 8.1 %outer_1b.1 = (f32[3,16,144,128]{3,2,1,0:T(8,128)S(1)}, f32[3,12,88,128]{3,2,1,0:T(8,128)S(1)}, f32[15,64,128]{2,1,0:T(8,128)S(1)}, f32[15,64,128]{2,1,0:T(8,128)S(1)}) custom-call(f32[3,16,160,128]{3,2,1,0:T(8,128)S(1)} %get-tuple-element.32.est_ref.obs_ref.refs_0_, f32[15,96,128]{2,1,0:T(8,128)S(1)} %collective-permute-done.5.refs_1_, ...), custom_call_target="tpu_custom_call" | custom-call | flops 1 | bytes 24494080 | tf_op jit(solution)/shard_map/outer_1b/pallas_call | solution.py:488
  89.2 3.5 %collective-permute-start.11 = (f32[15,64,128]{2,1,0:T(8,128)S(1)}, f32[15,64,128]{2,1,0:T(8,128)S(1)}, u32[]{:S(2)}, u32[]{:S(2)}) collective-permute-start(f32[15,64,128]{2,1,0:T(8,128)S(1)} %get-tuple-element.48), channel_id=1, source_target_pairs={{0,8},{8,16},{16,24},{1,9},{9,17},{17,25},{2,10},{10,18},{18,26},{... | collective-permute-start | bytes 1474568 | tf_op jit(solution)/shard_map/ppermute | solution.py:484
  92.7 2.4 %collective-permute-start.12 = (f32[15,64,128]{2,1,0:T(8,128)S(1)}, f32[15,64,128]{2,1,0:T(8,128)S(1)}, u32[]{:S(2)}, u32[]{:S(2)}) collective-permute-start(f32[15,64,128]{2,1,0:T(8,128)S(1)} %get-tuple-element.49), channel_id=1, source_target_pairs={{8,0},{16,8},{24,16},{9,1},{17,9},{25,17},{10,2},{18,10},{26,18},{... | collective-permute-start | bytes 1474568 | tf_op jit(solution)/shard_map/ppermute | solution.py:484
  95.2 6.8 %inner_2.1.refs_4_.refs_6_ = f32[2,10,136,128]{3,2,1,0:T(8,128)S(1)} custom-call(f32[3,16,144,128]{3,2,1,0:T(8,128)S(1)} %get-tuple-element.42.est_ref.refs_0_, f32[3,16,160,128]{3,2,1,0:T(8,128)S(1)} %get-tuple-element.32.est_ref.obs_ref.refs_0_, f32[22,160,128]{2,1,0:T(8,128)S(1)} %broadcast_in_dim.246.w_ref.refs_3_.refs_5_, ...), custom_call_target="tpu_custom_call" | custom-call | flops 1 | bytes 12935168 | tf_op jit(solution)/shard_map/inner_2/pallas_call | solution.py:488
  102.1 8.5 %outer_2a.1 = f32[2,16,64,128]{3,2,1,0:T(8,128)S(1)} custom-call(f32[3,16,144,128]{3,2,1,0:T(8,128)S(1)} %get-tuple-element.42.est_ref.refs_0_, f32[15,80,128]{2,1,0:T(8,128)S(1)} %collective-permute-done.9.refs_1_, f32[15,80,128]{2,1,0:T(8,128)S(1)} %collective-permute-done.10.refs_2_, f32[3,12,96,128]{3,2,1,0:T(8,128)S(1)} %get-tuple-element.45.refs_3_, ...), custom_call_target="tpu_custom_call" | custom-call | flops 1 | bytes 14901248 | tf_op jit(solution)/shard_map/outer_2a/pallas_call | solution.py:488
  110.6 8.5 %outer_2b.1 = f32[2,16,64,128]{3,2,1,0:T(8,128)S(1)} custom-call(f32[3,16,144,128]{3,2,1,0:T(8,128)S(1)} %get-tuple-element.42.est_ref.refs_0_, f32[15,80,128]{2,1,0:T(8,128)S(1)} %collective-permute-done.9.refs_1_, f32[15,80,128]{2,1,0:T(8,128)S(1)} %collective-permute-done.10.refs_2_, f32[15,64,128]{2,1,0:T(8,128)S(1)} %collective-permute-done.11.refs_3_, ...), custom_call_target="tpu_custom_call" | custom-call | flops 1 | bytes 15736832 | tf_op jit(solution)/shard_map/outer_2b/pallas_call | solution.py:488
  119.3 2.0 %copy.36 = f32[2,128,16,128]{3,2,1,0:T(8,128)} copy(f32[2,128,16,128]{1,3,2,0:T(8,128)S(1)} %maximum_bitcast_fusion) | data formatting | bytes 4194304 | tf_op jit(solution)/shard_map/transpose | solution.py:580
  (79 shorter events, 21.6 us)
Async XLA Ops:
  0.0 4.4 %copy-start.11 = (f32[256,16,128]{2,1,0:T(8,128)S(1)}, f32[256,16,128]{2,1,0:T(8,128)}, u32[]{:S(2)}) copy-start(f32[256,16,128]{2,1,0:T(8,128)} %param.6) | copy-start | bytes 6291460
  2.9 28.8 %collective-permute-start.2 = (f32[65,16,128]{2,1,0:T(8,128)}, f32[65,16,128]{2,1,0:T(8,128)}, u32[]{:S(2)}, u32[]{:S(2)}) collective-permute-start(f32[65,16,128]{2,1,0:T(8,128)} %pad_maximum_fusion), channel_id=1, source_target_pairs={{0,1},{1,0},{2,3},{3,2},{4,5},{5,4},{6,7},{7,6},{8,9},{9,8},{10,11... | collective-permute-start | bytes 1597448 | tf_op jit(solution)/shard_map/ppermute | solution.py:419
  8.6 15.5 %copy-start.13 = (f32[8,7]{1,0:T(8,128)S(1)}, f32[8,7]{1,0:T(8,128)}, u32[]{:S(2)}) copy-start(f32[8,7]{1,0:T(8,128)} %param.8) | copy-start | bytes 676
  8.6 15.5 %copy-start.14 = (f32[8,7]{1,0:T(8,128)S(1)}, f32[8,7]{1,0:T(8,128)}, u32[]{:S(2)}) copy-start(f32[8,7]{1,0:T(8,128)} %param.9) | copy-start | bytes 676
  8.7 15.6 %copy-start.10 = (f32[17]{0:T(128)S(1)}, f32[17]{0:T(128)}, u32[]{:S(2)}) copy-start(f32[17]{0:T(128)} %psf_ref.1) | copy-start | bytes 208
  8.7 21.0 %copy-start.12 = (s32[4,4,2]{1,2,0:T(2,128)S(1)}, s32[4,4,2]{1,2,0:T(2,128)}, u32[]{:S(2)}) copy-start(s32[4,4,2]{1,2,0:T(2,128)} %param.11) | copy-start | bytes 388
  9.6 27.6 %collective-permute-start = (f32[3,192,128]{2,1,0:T(8,128)}, f32[3,192,128]{2,1,0:T(8,128)}, u32[]{:S(2)}, u32[]{:S(2)}) collective-permute-start(f32[3,192,128]{2,1,0:T(8,128)} %get-tuple-element.28), channel_id=1, source_target_pairs={{0,2},{2,4},{4,6},{1,3},{3,5},{5,7},{8,10},{10,12},{12,14},{9,11},... | collective-permute-start | bytes 884744 | tf_op jit(solution)/shard_map/ppermute | solution.py:514
  11.5 25.7 %collective-permute-start.1 = (f32[3,192,128]{2,1,0:T(8,128)}, f32[3,192,128]{2,1,0:T(8,128)}, u32[]{:S(2)}, u32[]{:S(2)}) collective-permute-start(f32[3,192,128]{2,1,0:T(8,128)} %get-tuple-element.29), channel_id=1, source_target_pairs={{2,0},{4,2},{6,4},{3,1},{5,3},{7,5},{10,8},{12,10},{14,12},{11,9},... | collective-permute-start | bytes 884744 | tf_op jit(solution)/shard_map/ppermute | solution.py:514
  15.2 22.0 %collective-permute-start.3 = (f32[192,128]{1,0:T(8,128)}, f32[192,128]{1,0:T(8,128)S(1)}, u32[]{:S(2)}, u32[]{:S(2)}) collective-permute-start(f32[192,128]{1,0:T(8,128)} %get-tuple-element.30), channel_id=1, source_target_pairs={{0,3},{1,2},{2,5},{3,4},{4,7},{5,6},{8,11},{9,10},{10,13},{11,12},... | collective-permute-start | bytes 294920 | tf_op jit(solution)/shard_map/ppermute | solution.py:518
  17.1 20.1 %collective-permute-start.4 = (f32[192,128]{1,0:T(8,128)}, f32[192,128]{1,0:T(8,128)}, u32[]{:S(2)}, u32[]{:S(2)}) collective-permute-start(f32[192,128]{1,0:T(8,128)} %get-tuple-element.31), channel_id=1, source_target_pairs={{3,0},{2,1},{5,2},{4,3},{7,4},{6,5},{11,8},{10,9},{13,10},{12,11},... | collective-permute-start | bytes 294920 | tf_op jit(solution)/shard_map/ppermute | solution.py:519
  26.0 0.7 copy-start
  41.4 23.5 %collective-permute-start.5 = (f32[15,96,128]{2,1,0:T(8,128)S(1)}, f32[15,96,128]{2,1,0:T(8,128)S(1)}, u32[]{:S(2)}, u32[]{:S(2)}) collective-permute-start(f32[15,96,128]{2,1,0:T(8,128)S(1)} %get-tuple-element.33), channel_id=1, source_target_pairs={{0,8},{8,16},{16,24},{1,9},{9,17},{17,25},{2,10},{10,18},{18,26},{... | collective-permute-start | bytes 2211848 | tf_op jit(solution)/shard_map/ppermute | solution.py:484
  44.9 21.3 %collective-permute-start.6 = (f32[15,96,128]{2,1,0:T(8,128)S(1)}, f32[15,96,128]{2,1,0:T(8,128)S(1)}, u32[]{:S(2)}, u32[]{:S(2)}) collective-permute-start(f32[15,96,128]{2,1,0:T(8,128)S(1)} %get-tuple-element.34), channel_id=1, source_target_pairs={{8,0},{16,8},{24,16},{9,1},{17,9},{25,17},{10,2},{18,10},{26,18},{... | collective-permute-start | bytes 2211848 | tf_op jit(solution)/shard_map/ppermute | solution.py:484
  47.3 33.8 %collective-permute-start.7 = (f32[15,56,128]{2,1,0:T(8,128)S(1)}, f32[15,56,128]{2,1,0:T(8,128)S(1)}, u32[]{:S(2)}, u32[]{:S(2)}) collective-permute-start(f32[15,56,128]{2,1,0:T(8,128)S(1)} %get-tuple-element.35), channel_id=1, source_target_pairs={{0,8},{8,16},{16,24},{1,9},{9,17},{17,25},{2,10},{10,18},{18,26},{... | collective-permute-start | bytes 1290248 | tf_op jit(solution)/shard_map/ppermute | solution.py:484
  50.7 30.4 %collective-permute-start.8 = (f32[15,56,128]{2,1,0:T(8,128)S(1)}, f32[15,56,128]{2,1,0:T(8,128)S(1)}, u32[]{:S(2)}, u32[]{:S(2)}) collective-permute-start(f32[15,56,128]{2,1,0:T(8,128)S(1)} %get-tuple-element.36), channel_id=1, source_target_pairs={{8,0},{16,8},{24,16},{9,1},{17,9},{25,17},{10,2},{18,10},{26,18},{... | collective-permute-start | bytes 1290248 | tf_op jit(solution)/shard_map/ppermute | solution.py:484
  54.7 4.4 %copy-start.1 = (bf16[2,256,256]{2,1,0:T(8,128)(2,1)S(1)}, bf16[2,256,256]{2,1,0:T(8,128)(2,1)}, u32[]{:S(2)}) copy-start(bf16[2,256,256]{2,1,0:T(8,128)(2,1)} %copy-done) | copy-start | bytes 786436
  54.7 4.4 %copy-start.3 = (bf16[2,256,256]{2,1,0:T(8,128)(2,1)S(1)}, bf16[2,256,256]{2,1,0:T(8,128)(2,1)}, u32[]{:S(2)}) copy-start(bf16[2,256,256]{2,1,0:T(8,128)(2,1)} %copy-done.2) | copy-start | bytes 786436
  54.7 4.4 %copy-start.5 = (bf16[2,256,256]{2,1,0:T(8,128)(2,1)S(1)}, bf16[2,256,256]{2,1,0:T(8,128)(2,1)}, u32[]{:S(2)}) copy-start(bf16[2,256,256]{2,1,0:T(8,128)(2,1)} %copy-done.4) | copy-start | bytes 786436
  75.2 26.8 %collective-permute-start.10 = (f32[15,80,128]{2,1,0:T(8,128)S(1)}, f32[15,80,128]{2,1,0:T(8,128)S(1)}, u32[]{:S(2)}, u32[]{:S(2)}) collective-permute-start(f32[15,80,128]{2,1,0:T(8,128)S(1)} %get-tuple-element.44), channel_id=1, source_target_pairs={{8,0},{16,8},{24,16},{9,1},{17,9},{25,17},{10,2},{18,10},{26,18},{... | collective-permute-start | bytes 1843208 | tf_op jit(solution)/shard_map/ppermute | solution.py:484
  77.6 24.4 %collective-permute-start.9 = (f32[15,80,128]{2,1,0:T(8,128)S(1)}, f32[15,80,128]{2,1,0:T(8,128)S(1)}, u32[]{:S(2)}, u32[]{:S(2)}) collective-permute-start(f32[15,80,128]{2,1,0:T(8,128)S(1)} %get-tuple-element.43), channel_id=1, source_target_pairs={{0,8},{8,16},{16,24},{1,9},{9,17},{17,25},{2,10},{10,18},{18,26},{... | collective-permute-start | bytes 1843208 | tf_op jit(solution)/shard_map/ppermute | solution.py:484
  81.1 14.1 %copy-start.7 = (bf16[2,256,256]{2,1,0:T(8,128)(2,1)S(1)}, bf16[2,256,256]{2,1,0:T(8,128)(2,1)}, u32[]{:S(2)}) copy-start(bf16[2,256,256]{2,1,0:T(8,128)(2,1)} %copy-done.6) | copy-start | bytes 786436
  81.1 14.1 %copy-start.9 = (bf16[2,256,256]{2,1,0:T(8,128)(2,1)S(1)}, bf16[2,256,256]{2,1,0:T(8,128)(2,1)}, u32[]{:S(2)}) copy-start(bf16[2,256,256]{2,1,0:T(8,128)(2,1)} %copy-done.8) | copy-start | bytes 786436
  89.2 21.4 %collective-permute-start.11 = (f32[15,64,128]{2,1,0:T(8,128)S(1)}, f32[15,64,128]{2,1,0:T(8,128)S(1)}, u32[]{:S(2)}, u32[]{:S(2)}) collective-permute-start(f32[15,64,128]{2,1,0:T(8,128)S(1)} %get-tuple-element.48), channel_id=1, source_target_pairs={{0,8},{8,16},{16,24},{1,9},{9,17},{17,25},{2,10},{10,18},{18,26},{... | collective-permute-start | bytes 1474568 | tf_op jit(solution)/shard_map/ppermute | solution.py:484
  92.7 17.9 %collective-permute-start.12 = (f32[15,64,128]{2,1,0:T(8,128)S(1)}, f32[15,64,128]{2,1,0:T(8,128)S(1)}, u32[]{:S(2)}, u32[]{:S(2)}) collective-permute-start(f32[15,64,128]{2,1,0:T(8,128)S(1)} %get-tuple-element.49), channel_id=1, source_target_pairs={{8,0},{16,8},{24,16},{9,1},{17,9},{25,17},{10,2},{18,10},{26,18},{... | collective-permute-start | bytes 1474568 | tf_op jit(solution)/shard_map/ppermute | solution.py:484
  (4 other events, 2.9 us)

commit v4 on v3

--- a/solution.py
+++ b/solution.py
@@ -17,10 +17,12 @@
     return -(-value // unit) * unit
 
 
-def line(axis):
-    count = lax.axis_size(axis)
-    up = [(i, i + 1) for i in range(count - 1)]
-    return up, [(j, i) for i, j in up]
+def swaps(count):
+    return [[(i, i + 1) for i in range(first, count - 1, 2)] for first in (0, 1)]
+
+
+def both_ways(pairs):
+    return pairs + [(j, i) for i, j in pairs]
 
 
 def lane_is_low():
@@ -35,6 +37,16 @@
     if p >= half:
         value = pltpu.roll(value, LANES // 2, 1)
     return jnp.where(lane_is_low(), value, 0.0)
+
+
+def pack_both(src, pays, odd, packed, hx, blocks, src_block):
+    high = src.shape[1] - hx
+    pack_rows(src, pays[0], packed, hx, jnp.where(odd == 1, 0, high), blocks, src_block, 0)
+    pack_rows(src, pays[1], packed, hx, jnp.where(odd == 1, high, 0), blocks, src_block, 0)
+
+
+def by_side(odd, first, second):
+    return jnp.where(odd == 1, first, second), jnp.where(odd == 1, second, first)
 
 
 def pack_rows(src, pay, packed, hx, x0, blocks, src_block, pay_block):
@@ -169,36 +181,54 @@
     correct(mid_ref, ty_ref, (fh_ref, fl_ref, bh_ref, bl_ref), plan["shifted"], count // 2, rows, data_of, spread_ref)
 
 
-def norm_kernel(w_ref, tx_ref, ty_ref, out_ref, mid_ref):
+def norm_kernel(plan, place_ref, bands_ref, _, tx_ref, ty_ref, w_ref, out_ref, mid_ref):
+    cx, cy, hy, stacks_x, stacks_y = plan
     tiles, count = tx_ref.shape[:2]
     reach = (count - 1) // 2
     width = out_ref.shape[1]
+    full = w_ref.shape[1]
+    sx, sy = place_ref[0], place_ref[1]
+    row = lax.broadcasted_iota(jnp.int32, (full, LANES), 0)
+    for x in range(cx + 2 * reach):
+        a = (x - reach) // cx
+        px = (x - reach) % cx
+        gx = sx + a
+        value = jnp.zeros((full, LANES), jnp.float32)
+        for b, first in ((-1, 0), (0, hy), (1, hy + cy)):
+            gy = sy + b
+            inside = (gx >= 0) & (gx < stacks_x) & (gy >= 0) & (gy < stacks_y)
+            spot = 2 * (jnp.clip(gx, 0, stacks_x - 1) * stacks_y + jnp.clip(gy, 0, stacks_y - 1))
+            along = jnp.where(inside, jnp.where(px < bands_ref[spot], 0.5, 1.0), 0.0)
+            across = jnp.where(row - hy - b * cy < bands_ref[spot + 1], 0.5, 1.0)
+            value = jnp.where(row >= first, across * along, value)
+        w_ref[x] = value
+
+    def rows_in(t, j):
+        rows = pl.ds(pl.multiple_of(8 * j, 8), 8)
+        return [[w_ref[x, rows, :] for x in range(width + count - 1)]]
+
+    def rows_out(t, j, n, values):
+        rows = pl.ds(pl.multiple_of(8 * j, 8), 8)
+        for x, value in enumerate(values):
+            mid_ref[t, x, rows, :] = value
+
+    x_loop(tx_ref, True, 0, full // 8, rows_in, rows_out)
     for t in range(tiles):
-        k = [tx_ref[t, count - 1 - a] for a in range(count)]
-
-        def step(j, carry, k=k):
-            rows = pl.ds(pl.multiple_of(8 * j, 8), 8)
-            v = [w_ref[x, rows, :] for x in range(width + count - 1)]
-            for x, acc in enumerate(conv_rows(k, v, width)):
-                mid_ref[0, x, rows, :] = acc
-            return carry
-
-        lax.fori_loop(0, mid_ref.shape[2] // 8, step, 0)
         ky = [ty_ref[t, count - 1 - b] for b in range(count)]
 
         def ystep(x, carry, ky=ky, t=t):
             for j in range(out_ref.shape[2] // 8):
                 at = 8 * j + reach
-                acc = ky[0] * mid_ref[0, x, at : at + 8, :]
+                acc = ky[0] * mid_ref[t, x, at : at + 8, :]
                 for b in range(1, count):
-                    acc = acc + ky[b] * mid_ref[0, x, at + b : at + b + 8, :]
+                    acc = acc + ky[b] * mid_ref[t, x, at + b : at + b + 8, :]
                 out_ref[t, x, 8 * j : 8 * j + 8, :] = 1.0 / jnp.maximum(acc, TINY)
             return carry
 
         lax.fori_loop(0, width, ystep, 0)
 
 
-def band_kernel(lane0, psf_ref, fh_ref, fl_ref, bh_ref, bl_ref, sh_ref, sl_ref):
+def band_kernel(lane0, psf_ref, _, fh_ref, fl_ref, bh_ref, bl_ref, sh_ref, sl_ref):
     windows, size = fh_ref.shape[:2]
     taps = psf_ref.shape[0]
     total = psf_ref[0]
@@ -238,49 +268,83 @@
             sl_ref[w, r : r + step, :] = (part - hi.astype(jnp.float32)).astype(jnp.bfloat16)
 
 
-def edges_kernel(hy, after, vol_ref, low_ref, high_ref, *diags):
+def turned(shift, main, halo):
+    if halo is None:
+        return main
+    lane = lax.broadcasted_iota(jnp.int32, main[0].shape, 1)
+    moved = [pltpu.roll(m, shift, 1) for m in main]
+    out = [jnp.where(lane < shift, halo, moved[0])]
+    out += [jnp.where(lane < shift, moved[t - 1], moved[t]) for t in range(1, len(main))]
+    tail = jnp.where(lane < shift, moved[-1], jnp.where(lane < 2 * shift, halo, 0.0))
+    return out + [tail]
+
+
+def edges_kernel(hy, shift, place_ref, vol_ref, *refs):
     tiles, cx, cy = vol_ref.shape[:3]
+    odd = place_ref[1] % 2
+    direct = len(refs) > 2
+    if direct:
+        zones_ref, first_ref, second_ref, first_z, second_z, depth_ref = refs
+        lane = lax.broadcasted_iota(jnp.int32, (cy, LANES), 1)
+        half = cx // 2
+
+        def outmost(x):
+            return pltpu.roll(jnp.where(lane < LANES // 2, vol_ref[0, x], vol_ref[tiles - 1, x]), shift, 1)
+
+        for x in range(half):
+            other = pltpu.roll(outmost(x + half), LANES // 2, 1)
+            depth_ref[cy * x : cy * x + cy, :] = jnp.where(lane < LANES // 2, outmost(x), other)
+        depth_ref[cy * half :, :] = zones_ref[...]
+    else:
+        first_ref, second_ref = refs
+    lane = lax.broadcasted_iota(jnp.int32, (hy, LANES), 1)
     for x in range(cx):
         to = slice(hy * x, hy * x + hy)
-        for ref, rows, diag in ((low_ref, slice(cy - hy, cy), 0), (high_ref, slice(0, hy), 1)):
-            for t in range(tiles):
-                ref[t, to, :] = vol_ref[t, x, rows, :]
-            if diags:
-                lane = lax.broadcasted_iota(jnp.int32, (hy, LANES), 1)
-                diags[diag][to, :] = jnp.where(lane < after, vol_ref[tiles - 1, x, rows, :], vol_ref[0, x, rows, :])
-
-
-def assemble_kernel(packed, hx, cut, after, refs_in, *refs):
-    vol_ref, low_ref, high_ref = refs[:3]
-    halo_ref, low_z, high_z = refs[3:6] if refs_in == 6 else (None,) * 3
+        both = []
+        for t in range(tiles):
+            low, high = vol_ref[t, x, 0:hy, :], vol_ref[t, x, cy - hy : cy, :]
+            both.append((jnp.where(odd == 1, low, high), jnp.where(odd == 1, high, low)))
+            first_ref[t, to, :], second_ref[t, to, :] = both[-1]
+        if direct:
+            for n, ref in enumerate((first_z, second_z)):
+                ref[to, :] = pltpu.roll(jnp.where(lane < LANES // 2, both[0][n], both[-1][n]), shift, 1)
+
+
+def assemble_kernel(packed, hx, cut, shift, refs_in, place_ref, *refs):
+    vol_ref, first_ref, second_ref = refs[:3]
+    depth_ref, first_z, second_z = refs[3:6] if refs_in == 6 else (None,) * 3
     ext_ref, *pays = refs[refs_in:]
-    tiles, cx, cy = vol_ref.shape[:3]
-    hy = low_ref.shape[1] // cx
+    main, cx, cy = vol_ref.shape[:3]
+    hy = first_ref.shape[1] // cx
     end = cy + 2 * hy
-
-    def merge(t, value, halo, rows):
-        if halo is None or 0 < t < tiles - 1:
-            return value
-        lane = lax.broadcasted_iota(jnp.int32, value.shape, 1)
-        use = lane < after if t == 0 else (lane >= after) & (lane < 2 * after)
-        return jnp.where(use, halo[rows], value)
-
-    for t in range(tiles):
-        for x in range(cx):
-            edge = slice(hy * x, hy * x + hy)
-            ext_ref[t, x, 0:hy, :] = merge(t, low_ref[t, edge, :], low_z, edge)
-            ext_ref[t, x, hy : hy + cy, :] = merge(t, vol_ref[t, x], halo_ref, x)
-            ext_ref[t, x, hy + cy : end, :] = merge(t, high_ref[t, edge, :], high_z, edge)
+    odd = place_ref[1] % 2
+    half = cx // 2
+
+    for x in range(cx):
+        edge = slice(hy * x, hy * x + hy)
+        low, high = zip(*[by_side(odd, first_ref[t, edge, :], second_ref[t, edge, :]) for t in range(main)])
+        low_z = high_z = halo = None
+        if depth_ref is not None:
+            low_z, high_z = by_side(odd, first_z[edge, :], second_z[edge, :])
+            halo = depth_ref[cy * (x % half) : cy * (x % half) + cy, :]
+            halo = pltpu.roll(halo, LANES // 2, 1) if x >= half else halo
+        low = turned(shift, low, low_z)
+        mids = turned(shift, [vol_ref[t, x] for t in range(main)], halo)
+        high = turned(shift, high, high_z)
+        for t in range(ext_ref.shape[0]):
+            ext_ref[t, x, 0:hy, :] = low[t]
+            ext_ref[t, x, hy : hy + cy, :] = mids[t]
+            ext_ref[t, x, hy + cy : end, :] = high[t]
             ext_ref[t, x, end:, :] = jnp.zeros((ext_ref.shape[2] - end, LANES), jnp.float32)
-    for n, (pay_up, pay_down) in enumerate((pays[:2], pays[2:])):
-        first, last = (0, cut) if n == 0 else (cut, end)
-        blocks = -(-(last - first) // 8)
-        pack_rows(ext_ref, pay_up, packed, hx, cx - hx, blocks, first // 8, 0)
-        pack_rows(ext_ref, pay_down, packed, hx, 0, blocks, first // 8, 0)
-
-
-def outer_kernel(plan, *refs):
+    odd_x = place_ref[0] % 2
+    for n in range(2):
+        start, stop = (0, cut) if n == 0 else (cut, end)
+        pack_both(ext_ref, pays[2 * n : 2 * n + 2], odd_x, packed, hx, -(-(stop - start) // 8), start // 8)
+
+
+def outer_kernel(plan, place_ref, *refs):
     refs = list(refs)
+    odd = place_ref[0] % 2
     take = refs.pop
     est_ref = take(0)
     halos = [(take(0), take(0), first, last) for first, last in plan["halos"]]
@@ -309,11 +373,14 @@
         def rows_in(t, j, lo_ref=lo_ref, hi_ref=hi_ref, first=first):
             here = pl.ds(pl.multiple_of(8 * j, 8), 8)
             there = pl.ds(pl.multiple_of(8 * j - first, 8), 8)
-            one = [halo_row(lo_ref, tiles, packed, hx, t, p, there) for p in range(hx)]
-            one += [est_ref[t, x, here, :] for x in range(hx)]
-            two = [est_ref[t, x, here, :] for x in range(cx - hx, cx)]
-            two += [halo_row(hi_ref, tiles, packed, hx, t, p, there) for p in range(hx)]
-            return [one, two]
+            lows, highs = [], []
+            for p in range(hx):
+                came = [halo_row(ref, tiles, packed, hx, t, p, there) for ref in (lo_ref, hi_ref)]
+                low_row, high_row = by_side(odd, *came)
+                lows.append(low_row)
+                highs.append(high_row)
+            one = lows + [est_ref[t, x, here, :] for x in range(hx)]
+            return [one, [est_ref[t, x, here, :] for x in range(cx - hx, cx)] + highs]
 
         def keep(t, j, pair):
             here = pl.ds(pl.multiple_of(8 * j, 8), 8)
@@ -392,8 +459,7 @@
 
             lax.fori_loop(0, cx, copy, 0)
     if pays:
-        pack_rows(out_ref, pays[0], packed, hx, cx - hx, blocks, base // 8, 0)
-        pack_rows(out_ref, pays[1], packed, hx, 0, blocks, base // 8, 0)
+        pack_both(out_ref, pays, odd, packed, hx, blocks, base // 8)
 
 
 def body(observed, zone_of_slice, lateral_x, lateral_y, depth_psf, stitch_width):
@@ -409,32 +475,65 @@
     f32 = jnp.float32
 
     zones = zone_of_slice.astype(f32)
-
-    def with_zones(part, ids):
-        flat = jnp.pad(ids, (0, cx * cy - ids.shape[0]))
-        return jnp.concatenate([part, flat.reshape(1, cx, cy)], axis=0)
-
-    if slabs == 2:
-        both = jnp.concatenate([observed[nz - hz :], observed[:hz]], axis=0)
-        got = lax.ppermute(with_zones(both, jnp.concatenate([zones[nz - hz :], zones[:hz]])), "gz", [(0, 1), (1, 0)])
-        before, after = got[:hz], got[hz : 2 * hz]
-        got_ids = got[2 * hz].reshape(-1)
-        ids_before, ids_after = got_ids[:hz], got_ids[hz : 2 * hz]
+    pad = tiles * LANES - nz - 2 * hz
+    direct = slabs == 2 and nz % LANES == 0 and 4 * hz == LANES and cx % 2 == 0
+    sx, sy = lax.axis_index("sx"), lax.axis_index("sy")
+    place = jnp.stack([sx, sy]).astype(jnp.int32)
+
+    def shape(*dims):
+        return jax.ShapeDtypeStruct(dims, f32)
+
+    def call(kernel, out_shape, args, scratch, name, limit, flops, scalars=0, unread=()):
+        moved = sum(a.size * 4 for a in args) + sum(o.size * 4 for o in out_shape)
+        spaces = [pltpu.SMEM] * scalars + [pltpu.VMEM] * (len(args) - scalars)
+        spaces = [pl.ANY if n in unread else space for n, space in enumerate(spaces)]
+        return pl.pallas_call(
+            kernel,
+            out_shape=out_shape,
+            in_specs=[pl.BlockSpec(memory_space=space) for space in spaces],
+            out_specs=[VMEM] * len(out_shape),
+            scratch_shapes=[pltpu.VMEM(dims, f32) for dims in scratch],
+            compiler_params=pltpu.CompilerParams(vmem_limit_bytes=limit << 20),
+            cost_estimate=pl.CostEstimate(flops=flops, bytes_accessed=moved, transcendentals=0),
+            name=name,
+        )(*args)
+
+    rounds_y = swaps(lax.axis_size("sy"))
+    if direct:
+        volume = observed.reshape(-1, LANES, cx, cy).transpose(0, 2, 3, 1)
+        zone_rows = jnp.pad(zones.reshape(-1, LANES), ((0, 8 - nz // LANES), (0, 0)))
+        edge, edge_z = shape(volume.shape[0], cx * hy, LANES), shape(cx * hy, LANES)
+        first, second, first_z, second_z, borders = call(
+            functools.partial(edges_kernel, hy, hz), [edge, edge, edge_z, edge_z, shape(cx // 2 * cy + 8, LANES)],
+            (place, volume, zone_rows), [], "edges", 8, 1, scalars=1,
+        )
+        borders = lax.ppermute(borders, "gz", [(0, 1), (1, 0)])
+        parts = [volume, lax.ppermute(first, "sy", both_ways(rounds_y[0])), lax.ppermute(second, "sy", both_ways(rounds_y[1]))]
+        parts.append(borders)
+        for value, pairs in ((first_z, rounds_y[0]), (second_z, rounds_y[1])):
+            cross = [(2 * i + g, 2 * j + 1 - g) for i, j in pairs for g in range(2)]
+            parts.append(lax.ppermute(value, ("sy", "gz"), both_ways(cross)))
+        got_ids = borders[cx // 2 * cy :].reshape(-1)[:nz]
+        ids_before, ids_after = got_ids[nz - hz :], got_ids[:hz]
     else:
-        up = [(i, (i + 1) % slabs) for i in range(slabs)]
-        first = lax.ppermute(with_zones(observed[nz - hz :], zones[nz - hz :]), "gz", up)
-        second = lax.ppermute(with_zones(observed[:hz], zones[:hz]), "gz", [(j, i) for i, j in up])
+
+        def with_zones(part, ids):
+            flat = jnp.pad(ids, (0, cx * cy - ids.shape[0]))
+            return jnp.concatenate([part, flat.reshape(1, cx, cy)], axis=0)
+
+        ring = [(i, (i + 1) % slabs) for i in range(slabs)]
+        first = lax.ppermute(with_zones(observed[nz - hz :], zones[nz - hz :]), "gz", ring)
+        second = lax.ppermute(with_zones(observed[:hz], zones[:hz]), "gz", [(j, i) for i, j in ring])
         before, after = first[:hz], second[:hz]
         ids_before, ids_after = first[hz].reshape(-1)[:hz], second[hz].reshape(-1)[:hz]
-    pad = tiles * LANES - nz - 2 * hz
+        volume = jnp.concatenate([before, observed, after, jnp.zeros((pad, cx, cy), f32)], axis=0)
+        volume = volume.reshape(tiles, LANES, cx, cy).transpose(0, 2, 3, 1)
+        edge = shape(tiles, cx * hy, LANES)
+        first, second = call(
+            functools.partial(edges_kernel, hy, hz), [edge, edge], (place, volume), [], "edges", 8, 1, scalars=1
+        )
+        parts = [volume, lax.ppermute(first, "sy", both_ways(rounds_y[0])), lax.ppermute(second, "sy", both_ways(rounds_y[1]))]
     ids = jnp.concatenate([ids_before, zones, ids_after, jnp.full((pad,), -1.0, f32)])
-    direct = slabs == 2 and nz % LANES == 0 and 2 * hz <= LANES
-    if direct:
-        volume = jnp.pad(observed, ((hz, hz + pad), (0, 0), (0, 0)))
-        halo = jnp.pad(got[: 2 * hz], ((0, LANES - 2 * hz), (0, 0), (0, 0))).transpose(1, 2, 0)
-    else:
-        volume = jnp.concatenate([before, observed, after, jnp.zeros((pad, cx, cy), f32)], axis=0)
-    volume = volume.reshape(tiles, LANES, cx, cy).transpose(0, 2, 3, 1)
 
     def lanes_of(kernels, names):
         match = (names[None, :] == jnp.arange(lateral_x.shape[0], dtype=f32)[:, None]).astype(f32)
@@ -446,24 +545,6 @@
     own = ceil_to(nz, LANES) // LANES
     own_ids = jnp.concatenate([zones, jnp.full((own * LANES - nz,), -1.0, f32)])
     tx_own, ty_own = lanes_of(lateral_x, own_ids), lanes_of(lateral_y, own_ids)
-
-    sx, sy = lax.axis_index("sx"), lax.axis_index("sy")
-    stacks_x, stacks_y = stitch_width.shape[:2]
-    full = ceil_to(cy + 2 * hy + reach, 8)
-    gx = sx * cx - reach + jnp.arange(cx + 2 * reach)
-    gy = sy * cy - hy + jnp.arange(full)
-    near = lax.dynamic_slice(jnp.pad(stitch_width, ((1, 1), (1, 1), (0, 0))), (sx, sy, jnp.int32(0)), (3, 3, 2))
-    of_x = gx // cx - sx + 1
-    of_y = gy // cy - sy + 1
-    bands = jnp.zeros((2, gx.shape[0], full), jnp.int32)
-    for a in range(3):
-        for b in range(3):
-            hit = (of_x[:, None] == a) & (of_y[None, :] == b)
-            bands = jnp.where(hit[None], near[a, b][:, None, None], bands)
-    inside = ((gx >= 0) & (gx < stacks_x * cx))[:, None] & ((gy >= 0) & (gy < stacks_y * cy))[None, :]
-    weight = jnp.where((gx % cx)[:, None] < bands[0], 0.5, 1.0) * jnp.where((gy % cy)[None, :] < bands[1], 0.5, 1.0)
-    weight = jnp.where(inside, weight, 0.0).astype(f32)
-    weight = jnp.broadcast_to(weight[:, :, None], (cx + 2 * reach, full, LANES))
 
     wide = cx + 2 * reach
     packed = nz + 2 * hz - (tiles - 1) * LANES <= LANES // 2
@@ -472,29 +553,22 @@
     mid1 = ceil_to(end1 // 2, 8) + 8
     mid2 = mid1 - ceil_to(4 * reach, 8)
     cut = ceil_to(mid1 + 4 * reach, 8)
-    up, down = line("sx")
-
-    def shape(*dims):
-        return jax.ShapeDtypeStruct(dims, f32)
+    rounds_x = [both_ways(pairs) for pairs in swaps(lax.axis_size("sx"))]
+    full = ceil_to(cy + 2 * hy + reach, 8)
 
     def pay_shapes(rows):
         return [shape(planes, ceil_to(rows, 8), LANES)] * 2
 
     def swap(pays):
-        return lax.ppermute(pays[0], "sx", up), lax.ppermute(pays[1], "sx", down)
-
-    def call(kernel, out_shape, args, scratch, name, limit, flops, specs=VMEM):
-        moved = sum(a.size * 4 for a in args) + sum(o.size * 4 for o in out_shape)
-        return pl.pallas_call(
-            kernel,
-            out_shape=out_shape,
-            in_specs=[specs] * len(args),
-            out_specs=[VMEM] * len(out_shape),
-            scratch_shapes=[pltpu.VMEM(dims, f32) for dims in scratch],
-            compiler_params=pltpu.CompilerParams(vmem_limit_bytes=limit << 20),
-            cost_estimate=pl.CostEstimate(flops=flops, bytes_accessed=moved, transcendentals=0),
-            name=name,
-        )(*args)
+        return lax.ppermute(pays[0], "sx", rounds_x[0]), lax.ppermute(pays[1], "sx", rounds_x[1])
+
+    ext, *pays = call(
+        functools.partial(assemble_kernel, packed, hx, cut, hz, len(parts)),
+        [shape(tiles, cx, full, LANES)] + pay_shapes(cut) + pay_shapes(end0 - cut),
+        (place, *parts), [], "assemble", 8, 1, scalars=1,
+    )
+    halo_a = swap(pays[:2])
+    halo_b = swap(pays[2:])
 
     wins = windows_of(tiles)
     size = wins[0][1] * LANES
@@ -502,32 +576,13 @@
         functools.partial(band_kernel, hz),
         [jax.ShapeDtypeStruct((len(wins), size, size), jnp.bfloat16)] * 4
         + [jax.ShapeDtypeStruct((len(wins), size, own * LANES), jnp.bfloat16)] * 2,
-        (depth_psf,), [], "band", 8, 1,
-        specs=pl.BlockSpec(memory_space=pltpu.SMEM),
+        (depth_psf, pays[-1]), [], "band", 8, 1, scalars=1, unread=(1,),
     )
-
-    stacks = lax.axis_size("sy")
-    edge = shape(tiles, cx * hy, LANES)
-    diag = [shape(cx * hy, LANES)] * 2 if direct else []
-    low, high, *corner = call(functools.partial(edges_kernel, hy, hz), [edge, edge] + diag, (volume,), [], "edges", 8, 1)
-    yup, ydown = line("sy")
-    parts = [volume, lax.ppermute(low, "sy", yup), lax.ppermute(high, "sy", ydown)]
-    if direct:
-        cross = [(2 * i + g, 2 * i + 2 + (1 - g)) for i in range(stacks - 1) for g in range(2)]
-        parts.append(halo)
-        parts.append(lax.ppermute(corner[0], ("sy", "gz"), cross))
-        parts.append(lax.ppermute(corner[1], ("sy", "gz"), [(j, i) for i, j in cross]))
-
-    ext, *pays = call(
-        functools.partial(assemble_kernel, packed, hx, cut, hz, len(parts)),
-        [shape(tiles, cx, full, LANES)] + pay_shapes(cut) + pay_shapes(end0 - cut),
-        tuple(parts), [], "assemble", 8, 1,
-    )
-    halo_a = swap(pays[:2])
-    halo_b = swap(pays[2:])
-    (inv,) = call(
-        norm_kernel, [shape(tiles, cx, ceil_to(end1, 8), LANES)], (weight, tx, ty),
-        [(1, cx, full, LANES)], "norm", 8, 1,
+    stacks_x, stacks_y = stitch_width.shape[:2]
+    weight, inv = call(
+        functools.partial(norm_kernel, (cx, cy, hy, stacks_x, stacks_y)),
+        [shape(wide, full, LANES), shape(tiles, cx, ceil_to(end1, 8), LANES)],
+        (place, stitch_width.reshape(-1), pays[-1], tx, ty), [(tiles, cx, full, LANES)], "norm", 10, 1, scalars=2, unread=(2,),
     )
     shift = 2 * reach
 
@@ -544,14 +599,14 @@
     def outer(name, est, halos, extra, inner_part, last, plan, outs):
         rows = ceil_to(plan["high"] - plan["low"] + 2 * reach, 8)
         back, lateral = ((sh, sl), (tx_own, ty_own)) if last else ((bh, bl), (tx, ty))
-        args = (est,) + tuple(h for _, pair in halos for h in pair) + extra
+        args = (place, est) + tuple(h for _, pair in halos for h in pair) + extra
         args += (inner_part, inv, tx, ty) + lateral + (fh, fl) + back
         plan = dict(
             plan, hx=hx, packed=packed, halos=[rng for rng, _ in halos], make_data=not last, pay=not last,
             shifted=last, data_off=shift if last else 0, lane0=hz if last else 0,
         )
         scratch = [(tiles, cx, rows + 16, LANES), (own if last else tiles, 2 * hx, rows, LANES)]
-        return call(functools.partial(outer_kernel, plan), outs, args, scratch, name, 16, 1)
+        return call(functools.partial(outer_kernel, plan), outs, args, scratch, name, 16, 1, scalars=1)
 
     data_at = mid2 + 8
     spread1 = inner("inner_1", ext, 0, False, end1 + shift, end0, (bh, bl))

time: 122 us -> 109 us (0.89)
  waiting for transfers between devices: 1.28 us -> 20 us
  starting transfers between devices: 37 us -> 21.3 us
  local copies, waits for them, and re-layouts: 18.4 us -> 4.46 us
  other arithmetic: 6.3 us -> 0.55 us
  Pallas kernels: 57.9 us -> 61.7 us
    ppermute x13, waiting for transfers between devices: 1.28 us -> 20 us  [the longest x2 8.77 us: body(): parts.append(lax.ppermute(value, ('sy', 'gz'), both_ways(cross)))]
    ppermute x13, starting transfers between devices: 37 us -> 21.3 us  [the longest x4 11.7 us: swap(): lax.ppermute(pays[1], 'sx', rounds_x[1])]
    unnamed x33 -> x13, local copies, waits for them, and re-layouts: 6.17 us -> 0.3 us
    pallas_call x10, Pallas kernels: 57.9 us -> 61.7 us  [call(): pl.pallas_call(kernel, out_shape=out_shape, in_specs=[pl.BlockSpec(memory...]
    slice x5 -> x2, local copies, waits for them, and re-layouts: 3.43 us -> 0.08 us  [the longest x1 0.07 us: body(): ids_before, ids_after = (got_ids[nz - hz:], got_ids[:hz])]
    pad x1, local copies, waits for them, and re-layouts: 1.83 us -> 0.01 us  [body(): jnp.pad(zones.reshape(-1, LANES), ((0, 8 - nz // LANES), (0, 0)))]
    select_n x4 -> x0, other arithmetic: 1.46 us -> none  [the longest x1 0.75 us: body(): weight = jnp.where(inside, weight, 0.0).astype(f32)]
    and x3 -> x0, other arithmetic: 1.41 us -> none  [the longest x1 0.79 us: body(): hit = (of_x[:, None] == a) & (of_y[None, :] == b)]
  transfers between devices with their start and end apart: 13 -> 13, of which waited for: 1 -> 3; matrix products, arithmetic and copies ran while one was open for 13% -> 1% of each run, Pallas kernels for 37% -> 43%
where the time goes in v4:
time: 109 us; the launch traced here: 108 us
  Pallas kernels  61.7 us (57%)
  starting transfers between devices  21.3 us (20%)
  waiting for transfers between devices  20 us (18%)
  local copies, waits for them, and re-layouts  4.46 us (4%)
    pallas_call x10, Pallas kernels, call(): pl.pallas_call(kernel, out_shape=out_shape, in_specs=[pl.BlockSpec(memory...  61.7 us
    ppermute x4, starting transfers between devices, swap(): lax.ppermute(pays[1], 'sx', rounds_x[1])  11.7 us
    ppermute x2, waiting for transfers between devices, body(): parts.append(lax.ppermute(value, ('sy', 'gz'), both_ways(cross)))  8.77 us
    ppermute x4, waiting for transfers between devices, swap(): lax.ppermute(pays[0], 'sx', rounds_x[0])  5.66 us
    ppermute x4, waiting for transfers between devices, swap(): lax.ppermute(pays[1], 'sx', rounds_x[1])  5.52 us
    ppermute x2, starting transfers between devices, body(): parts.append(lax.ppermute(value, ('sy', 'gz'), both_ways(cross)))  3.02 us
    ppermute x4, starting transfers between devices, swap(): lax.ppermute(pays[0], 'sx', rounds_x[0])  2.57 us
    ppermute x1, starting transfers between devices, body(): lax.ppermute(second, 'sy', both_ways(rounds_y[1]))  2.54 us
  transfers between devices with their start and end apart: 13, of which 3 were waited for; matrix products, arithmetic and copies ran while one was open for 1% of the time, Pallas kernels for 43%

profile of v4, /device:TPU:10, one launch (start us, length us, event | category | flops | bytes accessed | tf_op | source)
XLA Modules:
  0.0 108.3 jit_solution(15898162137338459003)
XLA Ops:
  0.0 2.0 %copy.22 = f32[2,128,16,128]{1,3,2,0:T(8,128)S(1)} copy(f32[2,128,16,128]{3,2,1,0:T(8,128)} %bitcast.33) | data formatting | bytes 4194304 | tf_op jit(solution)/shard_map/reshape | solution.py:503
  2.1 2.2 %edges.1 = (f32[2,192,128]{2,1,0:T(8,128)}, f32[2,192,128]{2,1,0:T(8,128)S(1)}, f32[192,128]{1,0:T(8,128)}, f32[192,128]{1,0:T(8,128)S(1)}, f32[1032,128]{1,0:T(8,128)}) custom-call(s32[2]{0:T(128)S(1)} %pad_add_fusion.place_ref, f32[2,16,128,128]{3,2,1,0:T(8,128)S(1)} %bitcast.31, f32[8,128]{1,0:T(8,128)S(1)} %pad.4.refs_0_), custom_call_target="tpu_custom_call" | custom-call | flops 1 | bytes 3219464 | tf_op jit(solution)/shard_map/edges/pallas_call | solution.py:490
  4.4 1.5 %collective-permute-start.2 = (f32[1032,128]{1,0:T(8,128)}, f32[1032,128]{1,0:T(8,128)S(1)}, u32[]{:S(2)}, u32[]{:S(2)}) collective-permute-start(f32[1032,128]{1,0:T(8,128)} %get-tuple-element.33), channel_id=1, source_target_pairs={{0,1},{1,0},{2,3},{3,2},{4,5},{5,4},{6,7},{7,6},{8,9},{9,8},{10,11... | collective-permute-start | bytes 1585160 | tf_op jit(solution)/shard_map/ppermute | solution.py:510
  5.9 2.5 %collective-permute-start.1 = (f32[2,192,128]{2,1,0:T(8,128)S(1)}, f32[2,192,128]{2,1,0:T(8,128)S(1)}, u32[]{:S(2)}, u32[]{:S(2)}) collective-permute-start(f32[2,192,128]{2,1,0:T(8,128)S(1)} %get-tuple-element.32), channel_id=1, source_target_pairs={{2,4},{4,2},{3,5},{5,3},{10,12},{12,10},{11,13},{13,11},{18,20},{2... | collective-permute-start | bytes 589832 | tf_op jit(solution)/shard_map/ppermute | solution.py:511
  8.5 3.0 %collective-permute-start.4 = (f32[192,128]{1,0:T(8,128)S(1)}, f32[192,128]{1,0:T(8,128)S(1)}, u32[]{:S(2)}, u32[]{:S(2)}) collective-permute-start(f32[192,128]{1,0:T(8,128)S(1)} %get-tuple-element.35), channel_id=1, source_target_pairs={{2,5},{3,4},{5,2},{4,3},{10,13},{11,12},{13,10},{12,11},{18,21},{1... | collective-permute-start | bytes 294920 | tf_op jit(solution)/shard_map/ppermute | solution.py:515
  11.9 8.8 %collective-permute-done.3.refs_4_ = f32[192,128]{1,0:T(8,128)S(1)} collective-permute-done((f32[192,128]{1,0:T(8,128)}, f32[192,128]{1,0:T(8,128)S(1)}, u32[]{:S(2)}, u32[]{:S(2)}) %collective-permute-start.3) | collective-permute-done | bytes 98336 | tf_op jit(solution)/shard_map/ppermute | solution.py:515
  20.7 4.1 %assemble.1 = (f32[3,16,160,128]{3,2,1,0:T(8,128)S(1)}, f32[15,96,128]{2,1,0:T(8,128)S(1)}, f32[15,96,128]{2,1,0:T(8,128)S(1)}, f32[15,56,128]{2,1,0:T(8,128)S(1)}, f32[15,56,128]{2,1,0:T(8,128)S(1)}) custom-call(s32[2]{0:T(128)S(1)} %pad_add_fusion.place_ref, f32[2,16,128,128]{3,2,1,0:T(8,128)S(1)} %bitcast.32, ...), custom_call_target="tpu_custom_call" | custom-call | flops 1 | bytes 9482248 | tf_op jit(solution)/shard_map/assemble/pallas_call | solution.py:490
  24.8 3.5 %collective-permute-start.8 = (f32[15,56,128]{2,1,0:T(8,128)S(1)}, f32[15,56,128]{2,1,0:T(8,128)S(1)}, u32[]{:S(2)}, u32[]{:S(2)}) collective-permute-start(f32[15,56,128]{2,1,0:T(8,128)S(1)} %get-tuple-element.40._), channel_id=1, source_target_pairs={{8,16},{16,8},{9,17},{17,9},{10,18},{18,10},{11,19},{19,11},{12,20... | collective-permute-start | bytes 1290248 | tf_op jit(solution)/shard_map/ppermute | solution.py:563
  28.3 1.7 %band.1 = (bf16[2,256,256]{2,1,0:T(8,128)(2,1)S(1)}, bf16[2,256,256]{2,1,0:T(8,128)(2,1)S(1)}, bf16[2,256,256]{2,1,0:T(8,128)(2,1)S(1)}, bf16[2,256,256]{2,1,0:T...) custom-call(f32[17]{0:T(128)S(1)} %copy-done, f32[15,56,128]{2,1,0:T(8,128)S(1)} %get-tuple-element.40._), custom_call_target="tpu_custom_call" | custom-call | flops 1 | bytes 3575876 | tf_op jit(solution)/shard_map/band/pallas_call | solution.py:490
  30.1 2.4 %collective-permute-start.6 = (f32[15,96,128]{2,1,0:T(8,128)S(1)}, f32[15,96,128]{2,1,0:T(8,128)S(1)}, u32[]{:S(2)}, u32[]{:S(2)}) collective-permute-start(f32[15,96,128]{2,1,0:T(8,128)S(1)} %get-tuple-element.38), channel_id=1, source_target_pairs={{8,16},{16,8},{9,17},{17,9},{10,18},{18,10},{11,19},{19,11},{12,20... | collective-permute-start | bytes 2211848 | tf_op jit(solution)/shard_map/ppermute | solution.py:563
  32.5 0.4 collective-permute-start.7
  33.2 4.9 %norm.1 = (f32[22,160,128]{2,1,0:T(8,128)S(1)}, f32[3,16,144,128]{3,2,1,0:T(8,128)S(1)}) custom-call(s32[2]{0:T(128)S(1)} %pad_add_fusion.place_ref, s32[32]{0:T(128)S(1)} %reshape.66.bands_ref, f32[15,56,128]{2,1,0:T(8,128)S(1)} %get-tuple-element.40._, f32[3,7,8,128]{3,2,1,0:T(8,128)S(1)} %broadcast_in_dim.20.tx_ref.refs_6_.refs_8_.refs_9_.refs_11_, ...), custom_call_target="tpu_custom_call" | custom-call | flops 1 | bytes 5943432 | tf_op jit(solution)/shard_map/norm/pallas_call | solution.py:490
  38.1 5.7 %inner_1.1.refs_4_.refs_7_ = f32[3,10,152,128]{3,2,1,0:T(8,128)S(1)} custom-call(f32[3,16,160,128]{3,2,1,0:T(8,128)S(1)} %get-tuple-element.36.est_ref.obs_ref.refs_0_, f32[3,16,160,128]{3,2,1,0:T(8,128)S(1)} %get-tuple-element.36.est_ref.obs_ref.refs_0_, f32[22,160,128]{2,1,0:T(8,128)S(1)} %get-tuple-element.41.w_ref.refs_3_.refs_5_, ...), custom_call_target="tpu_custom_call" | custom-call | flops 1 | bytes 14270464 | tf_op jit(solution)/shard_map/inner_1/pallas_call | solution.py:490
  43.8 5.6 %collective-permute-done.5.refs_1_ = f32[15,96,128]{2,1,0:T(8,128)S(1)} collective-permute-done((f32[15,96,128]{2,1,0:T(8,128)S(1)}, f32[15,96,128]{2,1,0:T(8,128)S(1)}, u32[]{:S(2)}, u32[]{:S(2)}) %collective-permute-start.5) | collective-permute-done | bytes 737312 | tf_op jit(solution)/shard_map/ppermute | solution.py:563
  49.5 5.5 %collective-permute-done.6.refs_2_ = f32[15,96,128]{2,1,0:T(8,128)S(1)} collective-permute-done((f32[15,96,128]{2,1,0:T(8,128)S(1)}, f32[15,96,128]{2,1,0:T(8,128)S(1)}, u32[]{:S(2)}, u32[]{:S(2)}) %collective-permute-start.6) | collective-permute-done | bytes 737312 | tf_op jit(solution)/shard_map/ppermute | solution.py:563
  55.0 9.6 %outer_1a.1 = (f32[3,16,80,128]{3,2,1,0:T(8,128)S(1)}, f32[3,12,96,128]{3,2,1,0:T(8,128)S(1)}, f32[15,80,128]{2,1,0:T(8,128)S(1)}, f32[15,80,128]{2,1,0:T(8,128)S(1)}) custom-call(s32[2]{0:T(128)S(1)} %pad_add_fusion.place_ref, f32[3,16,160,128]{3,2,1,0:T(8,128)S(1)} %get-tuple-element.36.est_ref.obs_ref.refs_0_, ...), custom_call_target="tpu_custom_call" | custom-call | flops 1 | bytes 20488200 | tf_op jit(solution)/shard_map/outer_1a/pallas_call | solution.py:490
  64.6 3.5 %collective-permute-start.10 = (f32[15,80,128]{2,1,0:T(8,128)S(1)}, f32[15,80,128]{2,1,0:T(8,128)S(1)}, u32[]{:S(2)}, u32[]{:S(2)}) collective-permute-start(f32[15,80,128]{2,1,0:T(8,128)S(1)} %get-tuple-element.50), channel_id=1, source_target_pairs={{8,16},{16,8},{9,17},{17,9},{10,18},{18,10},{11,19},{19,11},{12,20... | collective-permute-start | bytes 1843208 | tf_op jit(solution)/shard_map/ppermute | solution.py:563
  68.1 8.5 %outer_1b.1 = (f32[3,16,144,128]{3,2,1,0:T(8,128)S(1)}, f32[3,12,88,128]{3,2,1,0:T(8,128)S(1)}, f32[15,64,128]{2,1,0:T(8,128)S(1)}, f32[15,64,128]{2,1,0:T(8,128)S(1)}) custom-call(s32[2]{0:T(128)S(1)} %pad_add_fusion.place_ref, f32[3,16,160,128]{3,2,1,0:T(8,128)S(1)} %get-tuple-element.36.est_ref.obs_ref.refs_0_, ...), custom_call_target="tpu_custom_call" | custom-call | flops 1 | bytes 24494088 | tf_op jit(solution)/shard_map/outer_1b/pallas_call | solution.py:490
  76.7 2.0 %collective-permute-start.11 = (f32[15,64,128]{2,1,0:T(8,128)S(1)}, f32[15,64,128]{2,1,0:T(8,128)S(1)}, u32[]{:S(2)}, u32[]{:S(2)}) collective-permute-start(f32[15,64,128]{2,1,0:T(8,128)S(1)} %get-tuple-element.54), channel_id=1, source_target_pairs={{0,8},{16,24},{8,0},{24,16},{1,9},{17,25},{9,1},{25,17},{2,10},{18... | collective-permute-start | bytes 1474568 | tf_op jit(solution)/shard_map/ppermute | solution.py:563
  78.7 2.4 %collective-permute-start.12 = (f32[15,64,128]{2,1,0:T(8,128)S(1)}, f32[15,64,128]{2,1,0:T(8,128)S(1)}, u32[]{:S(2)}, u32[]{:S(2)}) collective-permute-start(f32[15,64,128]{2,1,0:T(8,128)S(1)} %get-tuple-element.55), channel_id=1, source_target_pairs={{8,16},{16,8},{9,17},{17,9},{10,18},{18,10},{11,19},{19,11},{12,20... | collective-permute-start | bytes 1474568 | tf_op jit(solution)/shard_map/ppermute | solution.py:563
  81.2 6.8 %inner_2.1.refs_4_.refs_6_ = f32[2,10,136,128]{3,2,1,0:T(8,128)S(1)} custom-call(f32[3,16,144,128]{3,2,1,0:T(8,128)S(1)} %get-tuple-element.48.est_ref.refs_0_, f32[3,16,160,128]{3,2,1,0:T(8,128)S(1)} %get-tuple-element.36.est_ref.obs_ref.refs_0_, f32[22,160,128]{2,1,0:T(8,128)S(1)} %get-tuple-element.41.w_ref.refs_3_.refs_5_, ...), custom_call_target="tpu_custom_call" | custom-call | flops 1 | bytes 12935168 | tf_op jit(solution)/shard_map/inner_2/pallas_call | solution.py:490
  88.0 9.0 %outer_2a.1 = f32[2,16,64,128]{3,2,1,0:T(8,128)S(1)} custom-call(s32[2]{0:T(128)S(1)} %pad_add_fusion.place_ref, f32[3,16,144,128]{3,2,1,0:T(8,128)S(1)} %get-tuple-element.48.est_ref.refs_0_, f32[15,80,128]{2,1,0:T(8,128)S(1)} %collective-permute-done.9.refs_1_, f32[15,80,128]{2,1,0:T(8,128)S(1)} %collective-permute-done.10.refs_2_, ...), custom_call_target="tpu_custom_call" | custom-call | flops 1 | bytes 14901256 | tf_op jit(solution)/shard_map/outer_2a/pallas_call | solution.py:490
  97.1 9.1 %outer_2b.1 = f32[2,16,64,128]{3,2,1,0:T(8,128)S(1)} custom-call(s32[2]{0:T(128)S(1)} %pad_add_fusion.place_ref, f32[3,16,144,128]{3,2,1,0:T(8,128)S(1)} %get-tuple-element.48.est_ref.refs_0_, f32[15,80,128]{2,1,0:T(8,128)S(1)} %collective-permute-done.9.refs_1_, f32[15,80,128]{2,1,0:T(8,128)S(1)} %collective-permute-done.10.refs_2_, ...), custom_call_target="tpu_custom_call" | custom-call | flops 1 | bytes 15736840 | tf_op jit(solution)/shard_map/outer_2b/pallas_call | solution.py:490
  106.3 2.0 %copy.30 = f32[2,128,16,128]{3,2,1,0:T(8,128)} copy(f32[2,128,16,128]{1,3,2,0:T(8,128)S(1)} %maximum_bitcast_fusion) | data formatting | bytes 4194304 | tf_op jit(solution)/shard_map/transpose | solution.py:635
  (44 shorter events, 1.3 us)
Async XLA Ops:
  0.0 2.0 %copy-start.4 = (s32[256]{0:T(256)S(1)}, s32[256]{0:T(256)}, u32[]{:S(2)}) copy-start(s32[256]{0:T(256)} %param.7) | copy-start | bytes 3076
  2.0 9.5 %copy-start.2 = (f32[8,7]{1,0:T(8,128)S(1)}, f32[8,7]{1,0:T(8,128)}, u32[]{:S(2)}) copy-start(f32[8,7]{1,0:T(8,128)} %param.8) | copy-start | bytes 676
  2.0 9.6 %copy-start.3 = (f32[8,7]{1,0:T(8,128)S(1)}, f32[8,7]{1,0:T(8,128)}, u32[]{:S(2)}) copy-start(f32[8,7]{1,0:T(8,128)} %param.9) | copy-start | bytes 676
  2.0 9.6 %copy-start.1 = (s32[4,4,2]{1,2,0:T(2,128)S(1)}, s32[4,4,2]{1,2,0:T(2,128)}, u32[]{:S(2)}) copy-start(s32[4,4,2]{1,2,0:T(2,128)} %param.11) | copy-start | bytes 388
  4.4 23.9 %copy-start = (f32[17]{0:T(128)S(1)}, f32[17]{0:T(128)}, u32[]{:S(2)}) copy-start(f32[17]{0:T(128)} %psf_ref.1) | copy-start | bytes 208
  4.4 16.3 %collective-permute-start.2 = (f32[1032,128]{1,0:T(8,128)}, f32[1032,128]{1,0:T(8,128)S(1)}, u32[]{:S(2)}, u32[]{:S(2)}) collective-permute-start(f32[1032,128]{1,0:T(8,128)} %get-tuple-element.33), channel_id=1, source_target_pairs={{0,1},{1,0},{2,3},{3,2},{4,5},{5,4},{6,7},{7,6},{8,9},{9,8},{10,11... | collective-permute-start | bytes 1585160 | tf_op jit(solution)/shard_map/ppermute | solution.py:510
  5.9 14.8 %collective-permute-start = (f32[2,192,128]{2,1,0:T(8,128)}, f32[2,192,128]{2,1,0:T(8,128)S(1)}, u32[]{:S(2)}, u32[]{:S(2)}) collective-permute-start(f32[2,192,128]{2,1,0:T(8,128)} %get-tuple-element.31), channel_id=1, source_target_pairs={{0,2},{4,6},{2,0},{6,4},{1,3},{5,7},{3,1},{7,5},{8,10},{12,14},{10... | collective-permute-start | bytes 589832 | tf_op jit(solution)/shard_map/ppermute | solution.py:511
  5.9 14.8 %collective-permute-start.1 = (f32[2,192,128]{2,1,0:T(8,128)S(1)}, f32[2,192,128]{2,1,0:T(8,128)S(1)}, u32[]{:S(2)}, u32[]{:S(2)}) collective-permute-start(f32[2,192,128]{2,1,0:T(8,128)S(1)} %get-tuple-element.32), channel_id=1, source_target_pairs={{2,4},{4,2},{3,5},{5,3},{10,12},{12,10},{11,13},{13,11},{18,20},{2... | collective-permute-start | bytes 589832 | tf_op jit(solution)/shard_map/ppermute | solution.py:511
  8.5 12.2 %collective-permute-start.3 = (f32[192,128]{1,0:T(8,128)}, f32[192,128]{1,0:T(8,128)S(1)}, u32[]{:S(2)}, u32[]{:S(2)}) collective-permute-start(f32[192,128]{1,0:T(8,128)} %get-tuple-element.34), channel_id=1, source_target_pairs={{0,3},{1,2},{4,7},{5,6},{3,0},{2,1},{7,4},{6,5},{8,11},{9,10},{12,... | collective-permute-start | bytes 294920 | tf_op jit(solution)/shard_map/ppermute | solution.py:515
  8.5 12.1 %collective-permute-start.4 = (f32[192,128]{1,0:T(8,128)S(1)}, f32[192,128]{1,0:T(8,128)S(1)}, u32[]{:S(2)}, u32[]{:S(2)}) collective-permute-start(f32[192,128]{1,0:T(8,128)S(1)} %get-tuple-element.35), channel_id=1, source_target_pairs={{2,5},{3,4},{5,2},{4,3},{10,13},{11,12},{13,10},{12,11},{18,21},{1... | collective-permute-start | bytes 294920 | tf_op jit(solution)/shard_map/ppermute | solution.py:515
  24.8 43.3 %collective-permute-start.8 = (f32[15,56,128]{2,1,0:T(8,128)S(1)}, f32[15,56,128]{2,1,0:T(8,128)S(1)}, u32[]{:S(2)}, u32[]{:S(2)}) collective-permute-start(f32[15,56,128]{2,1,0:T(8,128)S(1)} %get-tuple-element.40._), channel_id=1, source_target_pairs={{8,16},{16,8},{9,17},{17,9},{10,18},{18,10},{11,19},{19,11},{12,20... | collective-permute-start | bytes 1290248 | tf_op jit(solution)/shard_map/ppermute | solution.py:563
  30.1 19.4 %collective-permute-start.5 = (f32[15,96,128]{2,1,0:T(8,128)S(1)}, f32[15,96,128]{2,1,0:T(8,128)S(1)}, u32[]{:S(2)}, u32[]{:S(2)}) collective-permute-start(f32[15,96,128]{2,1,0:T(8,128)S(1)} %get-tuple-element.37), channel_id=1, source_target_pairs={{0,8},{16,24},{8,0},{24,16},{1,9},{17,25},{9,1},{25,17},{2,10},{18... | collective-permute-start | bytes 2211848 | tf_op jit(solution)/shard_map/ppermute | solution.py:563
  30.1 24.9 %collective-permute-start.6 = (f32[15,96,128]{2,1,0:T(8,128)S(1)}, f32[15,96,128]{2,1,0:T(8,128)S(1)}, u32[]{:S(2)}, u32[]{:S(2)}) collective-permute-start(f32[15,96,128]{2,1,0:T(8,128)S(1)} %get-tuple-element.38), channel_id=1, source_target_pairs={{8,16},{16,8},{9,17},{17,9},{10,18},{18,10},{11,19},{19,11},{12,20... | collective-permute-start | bytes 2211848 | tf_op jit(solution)/shard_map/ppermute | solution.py:563
  32.5 35.6 %collective-permute-start.7 = (f32[15,56,128]{2,1,0:T(8,128)S(1)}, f32[15,56,128]{2,1,0:T(8,128)S(1)}, u32[]{:S(2)}, u32[]{:S(2)}) collective-permute-start(f32[15,56,128]{2,1,0:T(8,128)S(1)} %get-tuple-element.39), channel_id=1, source_target_pairs={{0,8},{16,24},{8,0},{24,16},{1,9},{17,25},{9,1},{25,17},{2,10},{18... | collective-permute-start | bytes 1290248 | tf_op jit(solution)/shard_map/ppermute | solution.py:563
  64.6 23.4 %collective-permute-start.10 = (f32[15,80,128]{2,1,0:T(8,128)S(1)}, f32[15,80,128]{2,1,0:T(8,128)S(1)}, u32[]{:S(2)}, u32[]{:S(2)}) collective-permute-start(f32[15,80,128]{2,1,0:T(8,128)S(1)} %get-tuple-element.50), channel_id=1, source_target_pairs={{8,16},{16,8},{9,17},{17,9},{10,18},{18,10},{11,19},{19,11},{12,20... | collective-permute-start | bytes 1843208 | tf_op jit(solution)/shard_map/ppermute | solution.py:563
  68.0 19.9 %collective-permute-start.9 = (f32[15,80,128]{2,1,0:T(8,128)S(1)}, f32[15,80,128]{2,1,0:T(8,128)S(1)}, u32[]{:S(2)}, u32[]{:S(2)}) collective-permute-start(f32[15,80,128]{2,1,0:T(8,128)S(1)} %get-tuple-element.49), channel_id=1, source_target_pairs={{0,8},{16,24},{8,0},{24,16},{1,9},{17,25},{9,1},{25,17},{2,10},{18... | collective-permute-start | bytes 1843208 | tf_op jit(solution)/shard_map/ppermute | solution.py:563
  76.7 20.4 %collective-permute-start.11 = (f32[15,64,128]{2,1,0:T(8,128)S(1)}, f32[15,64,128]{2,1,0:T(8,128)S(1)}, u32[]{:S(2)}, u32[]{:S(2)}) collective-permute-start(f32[15,64,128]{2,1,0:T(8,128)S(1)} %get-tuple-element.54), channel_id=1, source_target_pairs={{0,8},{16,24},{8,0},{24,16},{1,9},{17,25},{9,1},{25,17},{2,10},{18... | collective-permute-start | bytes 1474568 | tf_op jit(solution)/shard_map/ppermute | solution.py:563
  78.7 18.4 %collective-permute-start.12 = (f32[15,64,128]{2,1,0:T(8,128)S(1)}, f32[15,64,128]{2,1,0:T(8,128)S(1)}, u32[]{:S(2)}, u32[]{:S(2)}) collective-permute-start(f32[15,64,128]{2,1,0:T(8,128)S(1)} %get-tuple-element.55), channel_id=1, source_target_pairs={{8,16},{16,8},{9,17},{17,9},{10,18},{18,10},{11,19},{19,11},{12,20... | collective-permute-start | bytes 1474568 | tf_op jit(solution)/shard_map/ppermute | solution.py:563

commit v5 on v4

--- a/solution.py
+++ b/solution.py
@@ -6,6 +6,7 @@
 from jax.experimental import pallas as pl
 from jax.experimental.pallas import tpu as pltpu
 from jax.sharding import PartitionSpec as P
+
 
 ITERS = 2
 LANES = 128
@@ -129,11 +130,11 @@
         lax.fori_loop(first, last, step, 0)
 
 
-def y_pair(mid_ref, taps, t, i, blocks):
+def y_group(mid_ref, taps, t, first, group, blocks):
     count = taps.shape[1]
     k = [taps[t, b] for b in range(count)]
     out = []
-    for x in (2 * i, 2 * i + 1):
+    for x in [first + n for n in range(group)]:
         for j in range(blocks):
             acc = k[0] * mid_ref[t, x, 8 * j : 8 * j + 8, :]
             for b in range(1, count):
@@ -142,22 +143,25 @@
     return jnp.concatenate(out, axis=0)
 
 
-def correct(mid_ref, ty_ref, mats, shifted, pairs, rows, data_of, spread_ref, at=lambda i: 2 * i):
+def correct(mid_ref, ty_ref, mats, shifted, group, count, rows, data_of, spread_ref):
     fh_ref, fl_ref, bh_ref, bl_ref = mats
     tiles = mid_ref.shape[0]
+    group = next(n for n in range(group, 0, -1) if count % n == 0 and n * rows % 16 == 0)
 
     def depth(i, carry):
-        blurred = depth_rows([y_pair(mid_ref, ty_ref, t, i, rows // 8) for t in range(tiles)], fh_ref, fl_ref)
-        ratio = [data_of(t, i) / jnp.maximum(blurred[t], TINY) for t in range(tiles)]
+        first = group * i
+        blurred = [y_group(mid_ref, ty_ref, t, first, group, rows // 8) for t in range(tiles)]
+        blurred = depth_rows(blurred, fh_ref, fl_ref)
+        ratio = [data_of(t, first, group) / jnp.maximum(blurred[t], TINY) for t in range(tiles)]
         for t, value in enumerate(depth_rows(ratio, bh_ref, bl_ref, shifted)):
-            spread_ref[t, pl.ds(2 * i, 2), 0:rows, :] = value.reshape(2, rows, LANES)
+            spread_ref[t, pl.ds(first, group), 0:rows, :] = value.reshape(group, rows, LANES)
         return carry
 
-    lax.fori_loop(0, pairs, depth, 0)
+    lax.fori_loop(0, count // group, depth, 0)
 
 
 def inner_kernel(plan, est_ref, obs_ref, w_ref, tx_ref, ty_ref, fh_ref, fl_ref, bh_ref, bl_ref, spread_ref, mid_ref):
-    tiles, cx = est_ref.shape[:2]
+    _, cx = est_ref.shape[:2]
     reach = (tx_ref.shape[1] - 1) // 2
     rows = spread_ref.shape[2]
     first = plan["data_off"] + reach
@@ -174,11 +178,12 @@
 
     x_loop(tx_ref, False, 0, -(-plan["need"] // 8), rows_in, rows_out)
 
-    def data_of(t, i):
-        seen = obs_ref[t, pl.ds(2 * i + reach, 2), first : first + rows, :]
-        return (seen * w_ref[pl.ds(2 * i + 2 * reach, 2), first : first + rows, :]).reshape(2 * rows, LANES)
-
-    correct(mid_ref, ty_ref, (fh_ref, fl_ref, bh_ref, bl_ref), plan["shifted"], count // 2, rows, data_of, spread_ref)
+    def data_of(t, x, group):
+        seen = obs_ref[t, pl.ds(x + reach, group), first : first + rows, :]
+        return (seen * w_ref[pl.ds(x + 2 * reach, group), first : first + rows, :]).reshape(group * rows, LANES)
+
+    mats = (fh_ref, fl_ref, bh_ref, bl_ref)
+    correct(mid_ref, ty_ref, mats, plan["shifted"], 2, count, rows, data_of, spread_ref)
 
 
 def norm_kernel(plan, place_ref, bands_ref, _, tx_ref, ty_ref, w_ref, out_ref, mid_ref):
@@ -412,10 +417,10 @@
 
     spot0 = low + off + reach - data_base
 
-    def data_of(t, i):
-        return data_ref[t, pl.ds(2 * i, 2), spot0 : spot0 + rows, :].reshape(2 * rows, LANES)
-
-    correct(mid_ref, ty_ref, mats, plan["shifted"], hx, rows, data_of, edge_ref)
+    def data_of(t, x, group):
+        return data_ref[t, pl.ds(x, group), spot0 : spot0 + rows, :].reshape(group * rows, LANES)
+
+    correct(mid_ref, ty_ref, mats, plan["shifted"], 6, 2 * hx, rows, data_of, edge_ref)
 
     blocks = -(-(high - low) // 8)
 
@@ -483,7 +488,7 @@
     def shape(*dims):
         return jax.ShapeDtypeStruct(dims, f32)
 
-    def call(kernel, out_shape, args, scratch, name, limit, flops, scalars=0, unread=()):
+    def call(kernel, out_shape, args, scratch, limit, flops, scalars=0, unread=()):
         moved = sum(a.size * 4 for a in args) + sum(o.size * 4 for o in out_shape)
         spaces = [pltpu.SMEM] * scalars + [pltpu.VMEM] * (len(args) - scalars)
         spaces = [pl.ANY if n in unread else space for n, space in enumerate(spaces)]
@@ -495,7 +500,6 @@
             scratch_shapes=[pltpu.VMEM(dims, f32) for dims in scratch],
             compiler_params=pltpu.CompilerParams(vmem_limit_bytes=limit << 20),
             cost_estimate=pl.CostEstimate(flops=flops, bytes_accessed=moved, transcendentals=0),
-            name=name,
         )(*args)
 
     rounds_y = swaps(lax.axis_size("sy"))
@@ -505,7 +509,7 @@
         edge, edge_z = shape(volume.shape[0], cx * hy, LANES), shape(cx * hy, LANES)
         first, second, first_z, second_z, borders = call(
             functools.partial(edges_kernel, hy, hz), [edge, edge, edge_z, edge_z, shape(cx // 2 * cy + 8, LANES)],
-            (place, volume, zone_rows), [], "edges", 8, 1, scalars=1,
+            (place, volume, zone_rows), [], 8, 1, scalars=1,
         )
         borders = lax.ppermute(borders, "gz", [(0, 1), (1, 0)])
         parts = [volume, lax.ppermute(first, "sy", both_ways(rounds_y[0])), lax.ppermute(second, "sy", both_ways(rounds_y[1]))]
@@ -530,7 +534,7 @@
         volume = volume.reshape(tiles, LANES, cx, cy).transpose(0, 2, 3, 1)
         edge = shape(tiles, cx * hy, LANES)
         first, second = call(
-            functools.partial(edges_kernel, hy, hz), [edge, edge], (place, volume), [], "edges", 8, 1, scalars=1
+            functools.partial(edges_kernel, hy, hz), [edge, edge], (place, volume), [], 8, 1, scalars=1
         )
         parts = [volume, lax.ppermute(first, "sy", both_ways(rounds_y[0])), lax.ppermute(second, "sy", both_ways(rounds_y[1]))]
     ids = jnp.concatenate([ids_before, zones, ids_after, jnp.full((pad,), -1.0, f32)])
@@ -560,12 +564,15 @@
         return [shape(planes, ceil_to(rows, 8), LANES)] * 2
 
     def swap(pays):
-        return lax.ppermute(pays[0], "sx", rounds_x[0]), lax.ppermute(pays[1], "sx", rounds_x[1])
+        got = []
+        for n in range(2):
+            got.append(lax.ppermute(pays[n], "sx", rounds_x[n]))
+        return got
 
     ext, *pays = call(
         functools.partial(assemble_kernel, packed, hx, cut, hz, len(parts)),
         [shape(tiles, cx, full, LANES)] + pay_shapes(cut) + pay_shapes(end0 - cut),
-        (place, *parts), [], "assemble", 8, 1, scalars=1,
+        (place, *parts), [], 8, 1, scalars=1,
     )
     halo_a = swap(pays[:2])
     halo_b = swap(pays[2:])
@@ -576,27 +583,27 @@
         functools.partial(band_kernel, hz),
         [jax.ShapeDtypeStruct((len(wins), size, size), jnp.bfloat16)] * 4
         + [jax.ShapeDtypeStruct((len(wins), size, own * LANES), jnp.bfloat16)] * 2,
-        (depth_psf, pays[-1]), [], "band", 8, 1, scalars=1, unread=(1,),
+        (depth_psf, pays[-1]), [], 8, 1, scalars=1, unread=(1,),
     )
     stacks_x, stacks_y = stitch_width.shape[:2]
     weight, inv = call(
         functools.partial(norm_kernel, (cx, cy, hy, stacks_x, stacks_y)),
         [shape(wide, full, LANES), shape(tiles, cx, ceil_to(end1, 8), LANES)],
-        (place, stitch_width.reshape(-1), pays[-1], tx, ty), [(tiles, cx, full, LANES)], "norm", 10, 1, scalars=2, unread=(2,),
+        (place, stitch_width.reshape(-1), pays[-1], tx, ty), [(tiles, cx, full, LANES)], 10, 1, scalars=2, unread=(2,),
     )
     shift = 2 * reach
 
-    def inner(name, est, data_off, shifted, rows, need, back):
+    def inner(est, data_off, shifted, rows, need, back):
         plan = dict(data_off=data_off, shifted=shifted, need=need)
         args = (est, ext, weight, tx, ty, fh, fl) + back
         rows = ceil_to(rows, 8)
         return call(
             functools.partial(inner_kernel, plan),
             [shape(own if shifted else tiles, cx - shift, rows, LANES)], args,
-            [(tiles, cx - shift, rows + 16, LANES)], name, 24, 1,
+            [(tiles, cx - shift, rows + 16, LANES)], 24, 1,
         )[0]
 
-    def outer(name, est, halos, extra, inner_part, last, plan, outs):
+    def outer(est, halos, extra, inner_part, last, plan, outs):
         rows = ceil_to(plan["high"] - plan["low"] + 2 * reach, 8)
         back, lateral = ((sh, sl), (tx_own, ty_own)) if last else ((bh, bl), (tx, ty))
         args = (place, est) + tuple(h for _, pair in halos for h in pair) + extra
@@ -606,29 +613,29 @@
             shifted=last, data_off=shift if last else 0, lane0=hz if last else 0,
         )
         scratch = [(tiles, cx, rows + 16, LANES), (own if last else tiles, 2 * hx, rows, LANES)]
-        return call(functools.partial(outer_kernel, plan), outs, args, scratch, name, 16, 1, scalars=1)
+        return call(functools.partial(outer_kernel, plan), outs, args, scratch, 16, 1, scalars=1)
 
     data_at = mid2 + 8
-    spread1 = inner("inner_1", ext, 0, False, end1 + shift, end0, (bh, bl))
+    spread1 = inner(ext, 0, False, end1 + shift, end0, (bh, bl))
     est_a, data_a, *pays = outer(
-        "outer_1a", ext, [((0, cut), halo_a)], (weight,), spread1, False,
+        ext, [((0, cut), halo_a)], (weight,), spread1, False,
         dict(low=0, high=mid1, data_base=0, prior=False),
         [shape(tiles, cx, mid1, LANES), shape(tiles, 2 * hx, cut, LANES)] + pay_shapes(mid1),
     )
     halo_c = swap(pays)
     est, data_b, *pays = outer(
-        "outer_1b", ext, [((0, cut), halo_a), ((cut, end0), halo_b)], (weight, est_a), spread1, False,
+        ext, [((0, cut), halo_a), ((cut, end0), halo_b)], (weight, est_a), spread1, False,
         dict(low=mid1, high=end1, data_base=data_at, prior=True),
         [shape(tiles, cx, ceil_to(end1, 8), LANES), shape(tiles, 2 * hx, full - data_at, LANES)] + pay_shapes(end1 - mid1),
     )
     halo_d = swap(pays)
-    spread2 = inner("inner_2", est, shift, True, end2 + shift, end1, (sh, sl))
+    spread2 = inner(est, shift, True, end2 + shift, end1, (sh, sl))
     (out_a,) = outer(
-        "outer_2a", est, [((0, mid1), halo_c)], (data_a,), spread2, True,
+        est, [((0, mid1), halo_c)], (data_a,), spread2, True,
         dict(low=0, high=mid2, data_base=0, prior=False), [shape(own, cx, mid2, LANES)],
     )
     (out_b,) = outer(
-        "outer_2b", est, [((0, mid1), halo_c), ((mid1, end1), halo_d)], (data_b,), spread2, True,
+        est, [((0, mid1), halo_c), ((mid1, end1), halo_d)], (data_b,), spread2, True,
         dict(low=mid2, high=end2, data_base=data_at, prior=False), [shape(own, cx, end2 - mid2, LANES)],
     )
     estimate = jnp.concatenate([out_a, out_b], axis=2)

time: 109 us -> 104 us (0.954)
  Pallas kernels: 61.7 us -> 56.8 us
    pallas_call x10, Pallas kernels: 61.7 us -> 56.8 us  [call(): pl.pallas_call(kernel, out_shape=out_shape, in_specs=[pl.BlockSpec(memory...]
  transfers between devices with their start and end apart: 13 -> 13, of which waited for: 3 -> 3; matrix products, arithmetic and copies ran while one was open for 1% -> 1% of each run, Pallas kernels for 43% -> 41%
where the time goes in v5:
time: 104 us
  Pallas kernels  56.8 us (55%)
  starting transfers between devices  21.5 us (21%)
  waiting for transfers between devices  20 us (19%)
  local copies, waits for them, and re-layouts  4.46 us (4%)
    pallas_call x10, Pallas kernels, call(): pl.pallas_call(kernel, out_shape=out_shape, in_specs=[pl.BlockSpec(memory...  56.8 us
    ppermute x8, starting transfers between devices, swap(): got.append(lax.ppermute(pays[n], 'sx', rounds_x[n]))  14.4 us
    ppermute x8, waiting for transfers between devices, swap(): got.append(lax.ppermute(pays[n], 'sx', rounds_x[n]))  11.2 us
    ppermute x2, waiting for transfers between devices, body(): parts.append(lax.ppermute(value, ('sy', 'gz'), both_ways(cross)))  8.77 us
    ppermute x2, starting transfers between devices, body(): parts.append(lax.ppermute(value, ('sy', 'gz'), both_ways(cross)))  3.02 us
    ppermute x1, starting transfers between devices, body(): lax.ppermute(second, 'sy', both_ways(rounds_y[1]))  2.54 us
  transfers between devices with their start and end apart: 13, of which 3 were waited for; matrix products, arithmetic and copies ran while one was open for 1% of the time, Pallas kernels for 41%

profile of v5, /device:TPU:10, one launch (start us, length us, event | category | flops | bytes accessed | tf_op | source)
XLA Modules:
  0.0 103.6 jit_solution(17952556122521412191)
XLA Ops:
  0.0 2.0 %copy.22 = f32[2,128,16,128]{1,3,2,0:T(8,128)S(1)} copy(f32[2,128,16,128]{3,2,1,0:T(8,128)} %bitcast.33) | data formatting | bytes 4194304 | tf_op jit(solution)/shard_map/reshape | solution.py:507
  2.1 2.2 %shard_map.64 = (f32[2,192,128]{2,1,0:T(8,128)}, f32[2,192,128]{2,1,0:T(8,128)S(1)}, f32[192,128]{1,0:T(8,128)}, f32[192,128]{1,0:T(8,128)S(1)}, f32[1032,128]{1,0:T(8,128)}) custom-call(s32[2]{0:T(128)S(1)} %pad_add_fusion.place_ref, f32[2,16,128,128]{3,2,1,0:T(8,128)S(1)} %bitcast.31, f32[8,128]{1,0:T(8,128)S(1)} %pad.4.refs_0_), custom_call_target="tpu_custom_call" | custom-call | flops 1 | bytes 3219464 | tf_op jit(solution)/shard_map/pallas_call | solution.py:495
  4.4 1.5 %collective-permute-start.2 = (f32[1032,128]{1,0:T(8,128)}, f32[1032,128]{1,0:T(8,128)S(1)}, u32[]{:S(2)}, u32[]{:S(2)}) collective-permute-start(f32[1032,128]{1,0:T(8,128)} %get-tuple-element.33), channel_id=1, source_target_pairs={{0,1},{1,0},{2,3},{3,2},{4,5},{5,4},{6,7},{7,6},{8,9},{9,8},{10,11... | collective-permute-start | bytes 1585160 | tf_op jit(solution)/shard_map/ppermute | solution.py:514
  5.9 2.5 %collective-permute-start.1 = (f32[2,192,128]{2,1,0:T(8,128)S(1)}, f32[2,192,128]{2,1,0:T(8,128)S(1)}, u32[]{:S(2)}, u32[]{:S(2)}) collective-permute-start(f32[2,192,128]{2,1,0:T(8,128)S(1)} %get-tuple-element.32), channel_id=1, source_target_pairs={{2,4},{4,2},{3,5},{5,3},{10,12},{12,10},{11,13},{13,11},{18,20},{2... | collective-permute-start | bytes 589832 | tf_op jit(solution)/shard_map/ppermute | solution.py:515
  8.5 3.0 %collective-permute-start.4 = (f32[192,128]{1,0:T(8,128)S(1)}, f32[192,128]{1,0:T(8,128)S(1)}, u32[]{:S(2)}, u32[]{:S(2)}) collective-permute-start(f32[192,128]{1,0:T(8,128)S(1)} %get-tuple-element.35), channel_id=1, source_target_pairs={{2,5},{3,4},{5,2},{4,3},{10,13},{11,12},{13,10},{12,11},{18,21},{1... | collective-permute-start | bytes 294920 | tf_op jit(solution)/shard_map/ppermute | solution.py:519
  11.9 8.8 %collective-permute-done.3.refs_4_ = f32[192,128]{1,0:T(8,128)S(1)} collective-permute-done((f32[192,128]{1,0:T(8,128)}, f32[192,128]{1,0:T(8,128)S(1)}, u32[]{:S(2)}, u32[]{:S(2)}) %collective-permute-start.3) | collective-permute-done | bytes 98336 | tf_op jit(solution)/shard_map/ppermute | solution.py:519
  20.7 4.1 %shard_map.65 = (f32[3,16,160,128]{3,2,1,0:T(8,128)S(1)}, f32[15,96,128]{2,1,0:T(8,128)S(1)}, f32[15,96,128]{2,1,0:T(8,128)S(1)}, f32[15,56,128]{2,1,0:T(8,128)S(1)}, f32[15,56,128]{2,1,0:T(8,128)S(1)}) custom-call(s32[2]{0:T(128)S(1)} %pad_add_fusion.place_ref, f32[2,16,128,128]{3,2,1,0:T(8,128)S(1)} %bitcast.32, ...), custom_call_target="tpu_custom_call" | custom-call | flops 1 | bytes 9482248 | tf_op jit(solution)/shard_map/pallas_call | solution.py:495
  24.8 3.5 %collective-permute-start.8 = (f32[15,56,128]{2,1,0:T(8,128)S(1)}, f32[15,56,128]{2,1,0:T(8,128)S(1)}, u32[]{:S(2)}, u32[]{:S(2)}) collective-permute-start(f32[15,56,128]{2,1,0:T(8,128)S(1)} %get-tuple-element.40._), channel_id=1, source_target_pairs={{8,16},{16,8},{9,17},{17,9},{10,18},{18,10},{11,19},{19,11},{12,20... | collective-permute-start | bytes 1290248 | tf_op jit(solution)/shard_map/ppermute | solution.py:569
  28.3 1.7 %shard_map.67 = (bf16[2,256,256]{2,1,0:T(8,128)(2,1)S(1)}, bf16[2,256,256]{2,1,0:T(8,128)(2,1)S(1)}, bf16[2,256,256]{2,1,0:T(8,128)(2,1)S(1)}, bf16[2,256,256]{2...) custom-call(f32[17]{0:T(128)S(1)} %copy-done, ...), custom_call_target="tpu_custom_call" | custom-call | flops 1 | bytes 3575876 | tf_op jit(solution)/shard_map/pallas_call | solution.py:495
  30.1 2.4 %collective-permute-start.6 = (f32[15,96,128]{2,1,0:T(8,128)S(1)}, f32[15,96,128]{2,1,0:T(8,128)S(1)}, u32[]{:S(2)}, u32[]{:S(2)}) collective-permute-start(f32[15,96,128]{2,1,0:T(8,128)S(1)} %get-tuple-element.38), channel_id=1, source_target_pairs={{8,16},{16,8},{9,17},{17,9},{10,18},{18,10},{11,19},{19,11},{12,20... | collective-permute-start | bytes 2211848 | tf_op jit(solution)/shard_map/ppermute | solution.py:569
  32.5 0.4 collective-permute-start.7
  33.2 4.9 %shard_map.66 = (f32[22,160,128]{2,1,0:T(8,128)S(1)}, f32[3,16,144,128]{3,2,1,0:T(8,128)S(1)}) custom-call(s32[2]{0:T(128)S(1)} %pad_add_fusion.place_ref, s32[32]{0:T(128)S(1)} %reshape.66.bands_ref, f32[15,56,128]{2,1,0:T(8,128)S(1)} %get-tuple-element.40._, f32[3,7,8,128]{3,2,1,0:T(8,128)S(1)} %broadcast_in_dim.20.tx_ref.refs_6_.refs_8_.refs_9_.refs_11_, ...), custom_call_target="tpu_custom_call" | custom-call | flops 1 | bytes 5943432 | tf_op jit(solution)/shard_map/pallas_call | solution.py:495
  38.1 5.7 %shard_map.68.refs_4_.refs_7_ = f32[3,10,152,128]{3,2,1,0:T(8,128)S(1)} custom-call(f32[3,16,160,128]{3,2,1,0:T(8,128)S(1)} %get-tuple-element.36.est_ref.obs_ref.refs_0_, f32[3,16,160,128]{3,2,1,0:T(8,128)S(1)} %get-tuple-element.36.est_ref.obs_ref.refs_0_, f32[22,160,128]{2,1,0:T(8,128)S(1)} %get-tuple-element.41.w_ref.refs_3_.refs_5_, ...), custom_call_target="tpu_custom_call" | custom-call | flops 1 | bytes 14270464 | tf_op jit(solution)/shard_map/pallas_call | solution.py:495
  43.8 5.7 %collective-permute-done.5.refs_1_ = f32[15,96,128]{2,1,0:T(8,128)S(1)} collective-permute-done((f32[15,96,128]{2,1,0:T(8,128)S(1)}, f32[15,96,128]{2,1,0:T(8,128)S(1)}, u32[]{:S(2)}, u32[]{:S(2)}) %collective-permute-start.5) | collective-permute-done | bytes 737312 | tf_op jit(solution)/shard_map/ppermute | solution.py:569
  49.5 5.5 %collective-permute-done.6.refs_2_ = f32[15,96,128]{2,1,0:T(8,128)S(1)} collective-permute-done((f32[15,96,128]{2,1,0:T(8,128)S(1)}, f32[15,96,128]{2,1,0:T(8,128)S(1)}, u32[]{:S(2)}, u32[]{:S(2)}) %collective-permute-start.6) | collective-permute-done | bytes 737312 | tf_op jit(solution)/shard_map/ppermute | solution.py:569
  55.0 8.2 %shard_map.69 = (f32[3,16,80,128]{3,2,1,0:T(8,128)S(1)}, f32[3,12,96,128]{3,2,1,0:T(8,128)S(1)}, f32[15,80,128]{2,1,0:T(8,128)S(1)}, f32[15,80,128]{2,1,0:T(8,128)S(1)}) custom-call(s32[2]{0:T(128)S(1)} %pad_add_fusion.place_ref, f32[3,16,160,128]{3,2,1,0:T(8,128)S(1)} %get-tuple-element.36.est_ref.obs_ref.refs_0_, ...), custom_call_target="tpu_custom_call" | custom-call | flops 1 | bytes 20488200 | tf_op jit(solution)/shard_map/pallas_call | solution.py:495
  63.2 3.5 %collective-permute-start.10 = (f32[15,80,128]{2,1,0:T(8,128)S(1)}, f32[15,80,128]{2,1,0:T(8,128)S(1)}, u32[]{:S(2)}, u32[]{:S(2)}) collective-permute-start(f32[15,80,128]{2,1,0:T(8,128)S(1)} %get-tuple-element.50), channel_id=1, source_target_pairs={{8,16},{16,8},{9,17},{17,9},{10,18},{18,10},{11,19},{19,11},{12,20... | collective-permute-start | bytes 1843208 | tf_op jit(solution)/shard_map/ppermute | solution.py:569
  66.8 7.2 %shard_map.70 = (f32[3,16,144,128]{3,2,1,0:T(8,128)S(1)}, f32[3,12,88,128]{3,2,1,0:T(8,128)S(1)}, f32[15,64,128]{2,1,0:T(8,128)S(1)}, f32[15,64,128]{2,1,0:T(8,128)S(1)}) custom-call(s32[2]{0:T(128)S(1)} %pad_add_fusion.place_ref, f32[3,16,160,128]{3,2,1,0:T(8,128)S(1)} %get-tuple-element.36.est_ref.obs_ref.refs_0_, ...), custom_call_target="tpu_custom_call" | custom-call | flops 1 | bytes 24494088 | tf_op jit(solution)/shard_map/pallas_call | solution.py:495
  74.0 2.0 %collective-permute-start.11 = (f32[15,64,128]{2,1,0:T(8,128)S(1)}, f32[15,64,128]{2,1,0:T(8,128)S(1)}, u32[]{:S(2)}, u32[]{:S(2)}) collective-permute-start(f32[15,64,128]{2,1,0:T(8,128)S(1)} %get-tuple-element.54), channel_id=1, source_target_pairs={{0,8},{16,24},{8,0},{24,16},{1,9},{17,25},{9,1},{25,17},{2,10},{18... | collective-permute-start | bytes 1474568 | tf_op jit(solution)/shard_map/ppermute | solution.py:569
  76.0 2.5 %collective-permute-start.12 = (f32[15,64,128]{2,1,0:T(8,128)S(1)}, f32[15,64,128]{2,1,0:T(8,128)S(1)}, u32[]{:S(2)}, u32[]{:S(2)}) collective-permute-start(f32[15,64,128]{2,1,0:T(8,128)S(1)} %get-tuple-element.55), channel_id=1, source_target_pairs={{8,16},{16,8},{9,17},{17,9},{10,18},{18,10},{11,19},{19,11},{12,20... | collective-permute-start | bytes 1474568 | tf_op jit(solution)/shard_map/ppermute | solution.py:569
  78.6 6.8 %shard_map.71.refs_4_.refs_6_ = f32[2,10,136,128]{3,2,1,0:T(8,128)S(1)} custom-call(f32[3,16,144,128]{3,2,1,0:T(8,128)S(1)} %get-tuple-element.48.est_ref.refs_0_, f32[3,16,160,128]{3,2,1,0:T(8,128)S(1)} %get-tuple-element.36.est_ref.obs_ref.refs_0_, f32[22,160,128]{2,1,0:T(8,128)S(1)} %get-tuple-element.41.w_ref.refs_3_.refs_5_, ...), custom_call_target="tpu_custom_call" | custom-call | flops 1 | bytes 12935168 | tf_op jit(solution)/shard_map/pallas_call | solution.py:495
  85.5 7.9 %shard_map.72 = f32[2,16,64,128]{3,2,1,0:T(8,128)S(1)} custom-call(s32[2]{0:T(128)S(1)} %pad_add_fusion.place_ref, f32[3,16,144,128]{3,2,1,0:T(8,128)S(1)} %get-tuple-element.48.est_ref.refs_0_, f32[15,80,128]{2,1,0:T(8,128)S(1)} %collective-permute-done.9.refs_1_, f32[15,80,128]{2,1,0:T(8,128)S(1)} %collective-permute-done.10.refs_2_, ...), custom_call_target="tpu_custom_call" | custom-call | flops 1 | bytes 14901256 | tf_op jit(solution)/shard_map/pallas_call | solution.py:495
  93.4 8.0 %shard_map.73 = f32[2,16,64,128]{3,2,1,0:T(8,128)S(1)} custom-call(s32[2]{0:T(128)S(1)} %pad_add_fusion.place_ref, f32[3,16,144,128]{3,2,1,0:T(8,128)S(1)} %get-tuple-element.48.est_ref.refs_0_, f32[15,80,128]{2,1,0:T(8,128)S(1)} %collective-permute-done.9.refs_1_, f32[15,80,128]{2,1,0:T(8,128)S(1)} %collective-permute-done.10.refs_2_, ...), custom_call_target="tpu_custom_call" | custom-call | flops 1 | bytes 15736840 | tf_op jit(solution)/shard_map/pallas_call | solution.py:495
  101.6 2.0 %copy.30 = f32[2,128,16,128]{3,2,1,0:T(8,128)} copy(f32[2,128,16,128]{1,3,2,0:T(8,128)S(1)} %maximum_bitcast_fusion) | data formatting | bytes 4194304 | tf_op jit(solution)/shard_map/transpose | solution.py:642
  (44 shorter events, 1.3 us)
Async XLA Ops:
  0.0 2.0 %copy-start.4 = (s32[256]{0:T(256)S(1)}, s32[256]{0:T(256)}, u32[]{:S(2)}) copy-start(s32[256]{0:T(256)} %param.7) | copy-start | bytes 3076
  2.0 9.5 %copy-start.2 = (f32[8,7]{1,0:T(8,128)S(1)}, f32[8,7]{1,0:T(8,128)}, u32[]{:S(2)}) copy-start(f32[8,7]{1,0:T(8,128)} %param.8) | copy-start | bytes 676
  2.0 9.6 %copy-start.3 = (f32[8,7]{1,0:T(8,128)S(1)}, f32[8,7]{1,0:T(8,128)}, u32[]{:S(2)}) copy-start(f32[8,7]{1,0:T(8,128)} %param.9) | copy-start | bytes 676
  2.0 9.6 %copy-start.1 = (s32[4,4,2]{1,2,0:T(2,128)S(1)}, s32[4,4,2]{1,2,0:T(2,128)}, u32[]{:S(2)}) copy-start(s32[4,4,2]{1,2,0:T(2,128)} %param.11) | copy-start | bytes 388
  4.4 23.9 %copy-start = (f32[17]{0:T(128)S(1)}, f32[17]{0:T(128)}, u32[]{:S(2)}) copy-start(f32[17]{0:T(128)} %psf_ref.1) | copy-start | bytes 208
  4.4 16.3 %collective-permute-start.2 = (f32[1032,128]{1,0:T(8,128)}, f32[1032,128]{1,0:T(8,128)S(1)}, u32[]{:S(2)}, u32[]{:S(2)}) collective-permute-start(f32[1032,128]{1,0:T(8,128)} %get-tuple-element.33), channel_id=1, source_target_pairs={{0,1},{1,0},{2,3},{3,2},{4,5},{5,4},{6,7},{7,6},{8,9},{9,8},{10,11... | collective-permute-start | bytes 1585160 | tf_op jit(solution)/shard_map/ppermute | solution.py:514
  5.9 14.8 %collective-permute-start = (f32[2,192,128]{2,1,0:T(8,128)}, f32[2,192,128]{2,1,0:T(8,128)S(1)}, u32[]{:S(2)}, u32[]{:S(2)}) collective-permute-start(f32[2,192,128]{2,1,0:T(8,128)} %get-tuple-element.31), channel_id=1, source_target_pairs={{0,2},{4,6},{2,0},{6,4},{1,3},{5,7},{3,1},{7,5},{8,10},{12,14},{10... | collective-permute-start | bytes 589832 | tf_op jit(solution)/shard_map/ppermute | solution.py:515
  5.9 14.8 %collective-permute-start.1 = (f32[2,192,128]{2,1,0:T(8,128)S(1)}, f32[2,192,128]{2,1,0:T(8,128)S(1)}, u32[]{:S(2)}, u32[]{:S(2)}) collective-permute-start(f32[2,192,128]{2,1,0:T(8,128)S(1)} %get-tuple-element.32), channel_id=1, source_target_pairs={{2,4},{4,2},{3,5},{5,3},{10,12},{12,10},{11,13},{13,11},{18,20},{2... | collective-permute-start | bytes 589832 | tf_op jit(solution)/shard_map/ppermute | solution.py:515
  8.5 12.2 %collective-permute-start.3 = (f32[192,128]{1,0:T(8,128)}, f32[192,128]{1,0:T(8,128)S(1)}, u32[]{:S(2)}, u32[]{:S(2)}) collective-permute-start(f32[192,128]{1,0:T(8,128)} %get-tuple-element.34), channel_id=1, source_target_pairs={{0,3},{1,2},{4,7},{5,6},{3,0},{2,1},{7,4},{6,5},{8,11},{9,10},{12,... | collective-permute-start | bytes 294920 | tf_op jit(solution)/shard_map/ppermute | solution.py:519
  8.5 12.1 %collective-permute-start.4 = (f32[192,128]{1,0:T(8,128)S(1)}, f32[192,128]{1,0:T(8,128)S(1)}, u32[]{:S(2)}, u32[]{:S(2)}) collective-permute-start(f32[192,128]{1,0:T(8,128)S(1)} %get-tuple-element.35), channel_id=1, source_target_pairs={{2,5},{3,4},{5,2},{4,3},{10,13},{11,12},{13,10},{12,11},{18,21},{1... | collective-permute-start | bytes 294920 | tf_op jit(solution)/shard_map/ppermute | solution.py:519
  24.8 42.0 %collective-permute-start.8 = (f32[15,56,128]{2,1,0:T(8,128)S(1)}, f32[15,56,128]{2,1,0:T(8,128)S(1)}, u32[]{:S(2)}, u32[]{:S(2)}) collective-permute-start(f32[15,56,128]{2,1,0:T(8,128)S(1)} %get-tuple-element.40._), channel_id=1, source_target_pairs={{8,16},{16,8},{9,17},{17,9},{10,18},{18,10},{11,19},{19,11},{12,20... | collective-permute-start | bytes 1290248 | tf_op jit(solution)/shard_map/ppermute | solution.py:569
  30.1 19.4 %collective-permute-start.5 = (f32[15,96,128]{2,1,0:T(8,128)S(1)}, f32[15,96,128]{2,1,0:T(8,128)S(1)}, u32[]{:S(2)}, u32[]{:S(2)}) collective-permute-start(f32[15,96,128]{2,1,0:T(8,128)S(1)} %get-tuple-element.37), channel_id=1, source_target_pairs={{0,8},{16,24},{8,0},{24,16},{1,9},{17,25},{9,1},{25,17},{2,10},{18... | collective-permute-start | bytes 2211848 | tf_op jit(solution)/shard_map/ppermute | solution.py:569
  30.1 24.9 %collective-permute-start.6 = (f32[15,96,128]{2,1,0:T(8,128)S(1)}, f32[15,96,128]{2,1,0:T(8,128)S(1)}, u32[]{:S(2)}, u32[]{:S(2)}) collective-permute-start(f32[15,96,128]{2,1,0:T(8,128)S(1)} %get-tuple-element.38), channel_id=1, source_target_pairs={{8,16},{16,8},{9,17},{17,9},{10,18},{18,10},{11,19},{19,11},{12,20... | collective-permute-start | bytes 2211848 | tf_op jit(solution)/shard_map/ppermute | solution.py:569
  32.5 34.3 %collective-permute-start.7 = (f32[15,56,128]{2,1,0:T(8,128)S(1)}, f32[15,56,128]{2,1,0:T(8,128)S(1)}, u32[]{:S(2)}, u32[]{:S(2)}) collective-permute-start(f32[15,56,128]{2,1,0:T(8,128)S(1)} %get-tuple-element.39), channel_id=1, source_target_pairs={{0,8},{16,24},{8,0},{24,16},{1,9},{17,25},{9,1},{25,17},{2,10},{18... | collective-permute-start | bytes 1290248 | tf_op jit(solution)/shard_map/ppermute | solution.py:569
  63.2 22.2 %collective-permute-start.10 = (f32[15,80,128]{2,1,0:T(8,128)S(1)}, f32[15,80,128]{2,1,0:T(8,128)S(1)}, u32[]{:S(2)}, u32[]{:S(2)}) collective-permute-start(f32[15,80,128]{2,1,0:T(8,128)S(1)} %get-tuple-element.50), channel_id=1, source_target_pairs={{8,16},{16,8},{9,17},{17,9},{10,18},{18,10},{11,19},{19,11},{12,20... | collective-permute-start | bytes 1843208 | tf_op jit(solution)/shard_map/ppermute | solution.py:569
  66.7 18.7 %collective-permute-start.9 = (f32[15,80,128]{2,1,0:T(8,128)S(1)}, f32[15,80,128]{2,1,0:T(8,128)S(1)}, u32[]{:S(2)}, u32[]{:S(2)}) collective-permute-start(f32[15,80,128]{2,1,0:T(8,128)S(1)} %get-tuple-element.49), channel_id=1, source_target_pairs={{0,8},{16,24},{8,0},{24,16},{1,9},{17,25},{9,1},{25,17},{2,10},{18... | collective-permute-start | bytes 1843208 | tf_op jit(solution)/shard_map/ppermute | solution.py:569
  74.0 19.4 %collective-permute-start.11 = (f32[15,64,128]{2,1,0:T(8,128)S(1)}, f32[15,64,128]{2,1,0:T(8,128)S(1)}, u32[]{:S(2)}, u32[]{:S(2)}) collective-permute-start(f32[15,64,128]{2,1,0:T(8,128)S(1)} %get-tuple-element.54), channel_id=1, source_target_pairs={{0,8},{16,24},{8,0},{24,16},{1,9},{17,25},{9,1},{25,17},{2,10},{18... | collective-permute-start | bytes 1474568 | tf_op jit(solution)/shard_map/ppermute | solution.py:569
  76.0 17.4 %collective-permute-start.12 = (f32[15,64,128]{2,1,0:T(8,128)S(1)}, f32[15,64,128]{2,1,0:T(8,128)S(1)}, u32[]{:S(2)}, u32[]{:S(2)}) collective-permute-start(f32[15,64,128]{2,1,0:T(8,128)S(1)} %get-tuple-element.55), channel_id=1, source_target_pairs={{8,16},{16,8},{9,17},{17,9},{10,18},{18,10},{11,19},{19,11},{12,20... | collective-permute-start | bytes 1474568 | tf_op jit(solution)/shard_map/ppermute | solution.py:569

commit v6 on v5

--- a/solution.py
+++ b/solution.py
@@ -11,6 +11,8 @@
 ITERS = 2
 LANES = 128
 TINY = 1e-30
+EDGE = 16
+STEP = LANES - 2 * EDGE
 VMEM = pl.BlockSpec(memory_space=pltpu.VMEM)
 
 
@@ -30,14 +32,57 @@
     return lax.broadcasted_iota(jnp.int32, (8, LANES), 1) < LANES // 2
 
 
-def halo_row(ref, tiles, packed, hx, t, p, rows):
-    if not packed or t < tiles - 1:
-        return ref[hx * t + p, rows, :]
-    half = hx // 2
-    value = ref[hx * t + p % half, rows, :]
-    if p >= half:
-        value = pltpu.roll(value, LANES // 2, 1)
-    return jnp.where(lane_is_low(), value, 0.0)
+def spin(value, shift):
+    return pltpu.roll(value, shift % LANES, 1) if shift % LANES else value
+
+
+def regroup(tiles, start):
+    lane = lax.broadcasted_iota(jnp.int32, tiles[0].shape, 1)
+    out = None
+    for t, tile in enumerate(tiles):
+        first = 0 if t == 0 else STEP * t + EDGE - start
+        stop = LANES if t == len(tiles) - 1 else STEP * (t + 1) + EDGE - start
+        if max(first, 0) < min(stop, LANES):
+            value = spin(tile, STEP * t - start)
+            out = value if out is None else jnp.where(lane >= first, value, out)
+    return out
+
+
+def window(roll_of, start, shape):
+    first, off = divmod(start, LANES)
+    if off == 0:
+        return roll_of(first, 0)
+    lane = lax.broadcasted_iota(jnp.int32, shape, 1)
+    return jnp.where(lane < LANES - off, roll_of(first, LANES - off), roll_of(first + 1, LANES - off))
+
+
+def halo_tiles(refs, odd, tiles, packed, hx, rows):
+    planes, half = {}, hx // 2
+
+    def plane(index):
+        if index not in planes:
+            planes[index] = by_side(odd, refs[0][index, rows, :], refs[1][index, rows, :])
+        return planes[index]
+
+    spans = contiguous(tiles)
+    sides = []
+    for side in range(2):
+        out = [[] for _ in range(tiles)]
+        for p in range(hx):
+
+            def roll_of(k, shift, p=p):
+                if packed and k == spans - 1:
+                    return spin(plane(hx * k + p % half)[side], shift + (LANES // 2 if p >= half else 0))
+                return spin(plane(hx * k + p)[side], shift)
+
+            for t in range(tiles):
+                out[t].append(window(roll_of, STEP * t, (8, LANES)))
+        sides.append(out)
+    return sides
+
+
+def contiguous(tiles):
+    return -(-(LANES + STEP * (tiles - 1)) // LANES)
 
 
 def pack_both(src, pays, odd, packed, hx, blocks, src_block):
@@ -52,18 +97,21 @@
 
 def pack_rows(src, pay, packed, hx, x0, blocks, src_block, pay_block):
     tiles = src.shape[0]
+    spans = contiguous(tiles)
+    half = hx // 2
 
     def step(j, carry):
         here = pl.ds(pl.multiple_of(8 * (j + src_block), 8), 8)
         there = pl.ds(pl.multiple_of(8 * (j + pay_block), 8), 8)
-        for t in range(tiles - 1 if packed else tiles):
+        rows = [[src[t, x0 + p, here, :] for t in range(tiles)] for p in range(hx)]
+        for k in range(spans - 1 if packed else spans):
             for p in range(hx):
-                pay[hx * t + p, there, :] = src[t, x0 + p, here, :]
+                pay[hx * k + p, there, :] = regroup(rows[p], LANES * k)
         if packed:
-            half = hx // 2
+            last = LANES * (spans - 1)
             for p in range(half):
-                other = pltpu.roll(src[tiles - 1, x0 + p + half, here, :], LANES // 2, 1)
-                pay[hx * (tiles - 1) + p, there, :] = jnp.where(lane_is_low(), src[tiles - 1, x0 + p, here, :], other)
+                other = spin(regroup(rows[p + half], last), LANES // 2)
+                pay[hx * (spans - 1) + p, there, :] = jnp.where(lane_is_low(), regroup(rows[p], last), other)
         return carry
 
     lax.fori_loop(0, blocks, step, 0)
@@ -94,35 +142,24 @@
     lax.fori_loop(0, width, step, 0)
 
 
-def windows_of(tiles):
-    return [(0, tiles)] if tiles <= 2 else [(w, 2) for w in range(tiles - 1)]
-
-
-def depth_rows(parts, hi_ref, lo_ref, shifted=False):
-    split = []
-    for part in parts:
-        hi = part.astype(jnp.bfloat16)
-        split.append((hi, (part - hi.astype(jnp.float32)).astype(jnp.bfloat16)))
-    dot = functools.partial(jnp.dot, preferred_element_type=jnp.float32)
-    out = {}
-    for index, (first, span) in enumerate(windows_of(len(parts))):
-        his = jnp.concatenate([split[first + s][0] for s in range(span)], axis=1)
-        los = jnp.concatenate([split[first + s][1] for s in range(span)], axis=1)
-        res = dot(his, hi_ref[index]) + (dot(los, hi_ref[index]) + dot(his, lo_ref[index]))
-        for s in range(res.shape[1] // LANES):
-            to = s if shifted else first + s
-            piece = res[:, s * LANES : (s + 1) * LANES]
-            out[to] = out[to] + piece if to in out else piece
-    return [out[t] for t in range(len(out))]
+def depth_rows(parts, both_ref):
+    rows = parts[0].shape[0]
+    whole = jnp.concatenate(parts, axis=0)
+    hi = whole.astype(jnp.bfloat16)
+    lo = (whole - hi.astype(jnp.float32)).astype(jnp.bfloat16)
+    res = jnp.dot(jnp.concatenate([hi, lo], axis=1), both_ref[...], preferred_element_type=jnp.float32)
+    res = res[:, :LANES] + res[:, LANES:]
+    return [res[rows * t : rows * (t + 1)] for t in range(len(parts))]
 
 
 def x_loop(taps, reverse, first, last, rows_in, rows_out):
     tiles, count = taps.shape[:2]
 
     def step(j, carry):
+        rows = rows_in(j)
         for t in range(tiles):
             k = [taps[t, count - 1 - a if reverse else a] for a in range(count)]
-            for n, v in enumerate(rows_in(t, j)):
+            for n, v in enumerate(rows[t]):
                 rows_out(t, j, n, conv_rows(k, v, len(v) - count + 1))
         return carry
 
@@ -143,33 +180,34 @@
     return jnp.concatenate(out, axis=0)
 
 
-def correct(mid_ref, ty_ref, mats, shifted, group, count, rows, data_of, spread_ref):
-    fh_ref, fl_ref, bh_ref, bl_ref = mats
+def correct(mid_ref, ty_ref, mats, starts, group, count, rows, data_of, spread_ref):
+    forward_ref, back_ref = mats
     tiles = mid_ref.shape[0]
     group = next(n for n in range(group, 0, -1) if count % n == 0 and n * rows % 16 == 0)
 
     def depth(i, carry):
         first = group * i
         blurred = [y_group(mid_ref, ty_ref, t, first, group, rows // 8) for t in range(tiles)]
-        blurred = depth_rows(blurred, fh_ref, fl_ref)
+        blurred = depth_rows(blurred, forward_ref)
         ratio = [data_of(t, first, group) / jnp.maximum(blurred[t], TINY) for t in range(tiles)]
-        for t, value in enumerate(depth_rows(ratio, bh_ref, bl_ref, shifted)):
-            spread_ref[t, pl.ds(first, group), 0:rows, :] = value.reshape(group, rows, LANES)
+        spread = depth_rows(ratio, back_ref)
+        for t, start in enumerate(starts):
+            spread_ref[t, pl.ds(first, group), 0:rows, :] = regroup(spread, start).reshape(group, rows, LANES)
         return carry
 
     lax.fori_loop(0, count // group, depth, 0)
 
 
-def inner_kernel(plan, est_ref, obs_ref, w_ref, tx_ref, ty_ref, fh_ref, fl_ref, bh_ref, bl_ref, spread_ref, mid_ref):
-    _, cx = est_ref.shape[:2]
+def inner_kernel(plan, est_ref, obs_ref, w_ref, tx_ref, ty_ref, forward_ref, back_ref, spread_ref, mid_ref):
+    tiles, cx = est_ref.shape[:2]
     reach = (tx_ref.shape[1] - 1) // 2
     rows = spread_ref.shape[2]
     first = plan["data_off"] + reach
     count = cx - 2 * reach
 
-    def rows_in(t, j):
+    def rows_in(j):
         here = pl.ds(pl.multiple_of(8 * j, 8), 8)
-        return [[est_ref[t, x, here, :] for x in range(cx)]]
+        return [[[est_ref[t, x, here, :] for x in range(cx)]] for t in range(tiles)]
 
     def rows_out(t, j, n, values):
         here = pl.ds(pl.multiple_of(8 * j, 8), 8)
@@ -182,8 +220,7 @@
         seen = obs_ref[t, pl.ds(x + reach, group), first : first + rows, :]
         return (seen * w_ref[pl.ds(x + 2 * reach, group), first : first + rows, :]).reshape(group * rows, LANES)
 
-    mats = (fh_ref, fl_ref, bh_ref, bl_ref)
-    correct(mid_ref, ty_ref, mats, plan["shifted"], 2, count, rows, data_of, spread_ref)
+    correct(mid_ref, ty_ref, (forward_ref, back_ref), plan["starts"], 2, count, rows, data_of, spread_ref)
 
 
 def norm_kernel(plan, place_ref, bands_ref, _, tx_ref, ty_ref, w_ref, out_ref, mid_ref):
@@ -208,9 +245,9 @@
             value = jnp.where(row >= first, across * along, value)
         w_ref[x] = value
 
-    def rows_in(t, j):
+    def rows_in(j):
         rows = pl.ds(pl.multiple_of(8 * j, 8), 8)
-        return [[w_ref[x, rows, :] for x in range(width + count - 1)]]
+        return [[[w_ref[x, rows, :] for x in range(width + count - 1)]]] * tiles
 
     def rows_out(t, j, n, values):
         rows = pl.ds(pl.multiple_of(8 * j, 8), 8)
@@ -233,55 +270,30 @@
         lax.fori_loop(0, width, ystep, 0)
 
 
-def band_kernel(lane0, psf_ref, _, fh_ref, fl_ref, bh_ref, bl_ref, sh_ref, sl_ref):
-    windows, size = fh_ref.shape[:2]
+def band_kernel(psf_ref, _, forward_ref, back_ref):
     taps = psf_ref.shape[0]
     total = psf_ref[0]
     for j in range(1, taps):
         total = total + psf_ref[j]
-    step = LANES // 2
-    for r in range(0, size, step):
-        shape = (step, size)
-        cols = lax.broadcasted_iota(jnp.int32, shape, 1)
-        off = cols - lax.broadcasted_iota(jnp.int32, shape, 0) - r + (taps - 1) // 2
-        band, flip = jnp.zeros(shape, jnp.float32), jnp.zeros(shape, jnp.float32)
-        for j in range(taps):
-            band = jnp.where(off == j, psf_ref[j], band)
-            flip = jnp.where(off == taps - 1 - j, psf_ref[j], flip)
-        for matrix, hi_ref, lo_ref in ((band, fh_ref, fl_ref), (flip, bh_ref, bl_ref)):
-            matrix = matrix / jnp.full(shape, total, jnp.float32)
-            for w in range(windows):
-                first = 0 if w == 0 else LANES // 2
-                last = size if w == windows - 1 else LANES + LANES // 2
-                part = jnp.where((cols >= first) & (cols < last), matrix, 0.0)
-                hi = part.astype(jnp.bfloat16)
-                hi_ref[w, r : r + step, :] = hi
-                lo_ref[w, r : r + step, :] = (part - hi.astype(jnp.float32)).astype(jnp.bfloat16)
-        shape = (step, sh_ref.shape[2])
-        for w in range(windows):
-            ext = lax.broadcasted_iota(jnp.int32, shape, 0) + r + w * LANES
-            off = ext - lax.broadcasted_iota(jnp.int32, shape, 1) - lane0 + (taps - 1) // 2
-            part = jnp.zeros(shape, jnp.float32)
-            first = 0 if w == 0 else LANES // 2
-            last = size if w == windows - 1 else LANES + LANES // 2
-            if first <= r < last:
-                for j in range(taps):
-                    part = jnp.where(off == j, psf_ref[j], part)
-                part = part / jnp.full(shape, total, jnp.float32)
-            hi = part.astype(jnp.bfloat16)
-            sh_ref[w, r : r + step, :] = hi
-            sl_ref[w, r : r + step, :] = (part - hi.astype(jnp.float32)).astype(jnp.bfloat16)
-
-
-def turned(shift, main, halo):
-    if halo is None:
-        return main
-    lane = lax.broadcasted_iota(jnp.int32, main[0].shape, 1)
-    moved = [pltpu.roll(m, shift, 1) for m in main]
-    out = [jnp.where(lane < shift, halo, moved[0])]
-    out += [jnp.where(lane < shift, moved[t - 1], moved[t]) for t in range(1, len(main))]
-    tail = jnp.where(lane < shift, moved[-1], jnp.where(lane < 2 * shift, halo, 0.0))
-    return out + [tail]
+    shape = (LANES, LANES)
+    off = lax.broadcasted_iota(jnp.int32, shape, 1) - lax.broadcasted_iota(jnp.int32, shape, 0) + (taps - 1) // 2
+    band, flip = jnp.zeros(shape, jnp.float32), jnp.zeros(shape, jnp.float32)
+    for j in range(taps):
+        band = jnp.where(off == j, psf_ref[j], band)
+        flip = jnp.where(off == taps - 1 - j, psf_ref[j], flip)
+    for matrix, ref in ((band, forward_ref), (flip, back_ref)):
+        matrix = matrix / jnp.full(shape, total, jnp.float32)
+        hi = matrix.astype(jnp.bfloat16)
+        ref[:LANES, :LANES] = hi
+        ref[LANES:, :LANES] = hi
+        ref[:LANES, LANES:] = (matrix - hi.astype(jnp.float32)).astype(jnp.bfloat16)
+        ref[LANES:, LANES:] = jnp.zeros(shape, jnp.bfloat16)
+
+
+def overlapping(tiles, shift, main, halo):
+    series = main if halo is None else [halo, *main, halo]
+    start = 0 if halo is None else LANES - shift
+    return [window(lambda k, turn: spin(series[k], turn), start + STEP * t, main[0].shape) for t in range(tiles)]
 
 
 def edges_kernel(hy, shift, place_ref, vol_ref, *refs):
@@ -312,7 +324,7 @@
             first_ref[t, to, :], second_ref[t, to, :] = both[-1]
         if direct:
             for n, ref in enumerate((first_z, second_z)):
-                ref[to, :] = pltpu.roll(jnp.where(lane < LANES // 2, both[0][n], both[-1][n]), shift, 1)
+                ref[to, :] = jnp.where(lane < LANES // 2, both[0][n], both[-1][n])
 
 
 def assemble_kernel(packed, hx, cut, shift, refs_in, place_ref, *refs):
@@ -332,10 +344,11 @@
         if depth_ref is not None:
             low_z, high_z = by_side(odd, first_z[edge, :], second_z[edge, :])
             halo = depth_ref[cy * (x % half) : cy * (x % half) + cy, :]
-            halo = pltpu.roll(halo, LANES // 2, 1) if x >= half else halo
-        low = turned(shift, low, low_z)
-        mids = turned(shift, [vol_ref[t, x] for t in range(main)], halo)
-        high = turned(shift, high, high_z)
+            halo = spin(halo, (LANES // 2 if x >= half else 0) - shift)
+        tiles = ext_ref.shape[0]
+        low = overlapping(tiles, shift, list(low), low_z)
+        mids = overlapping(tiles, shift, [vol_ref[t, x] for t in range(main)], halo)
+        high = overlapping(tiles, shift, list(high), high_z)
         for t in range(ext_ref.shape[0]):
             ext_ref[t, x, 0:hy, :] = low[t]
             ext_ref[t, x, hy : hy + cy, :] = mids[t]
@@ -358,13 +371,13 @@
     data_in = None if make else take(0)
     prior_ref = take(0) if plan["prior"] else None
     inner_ref, inv_ref, tx_ref, ty_ref, bx_ref, by_ref = [take(0) for _ in range(6)]
-    mats = [take(0) for _ in range(4)]
+    mats = [take(0) for _ in range(2)]
     out_ref = take(0)
     data_ref = take(0) if make else data_in
     pays = [take(0), take(0)] if plan["pay"] else None
     mid_ref, edge_ref = refs
     packed, hx, low, high = plan["packed"], plan["hx"], plan["low"], plan["high"]
-    data_base, off, lane0 = plan["data_base"], plan["data_off"], plan["lane0"]
+    data_base, off, starts = plan["data_base"], plan["data_off"], plan["starts"]
     tiles, cx = est_ref.shape[:2]
     outs = out_ref.shape[0]
     count = tx_ref.shape[1]
@@ -375,17 +388,17 @@
 
     for lo_ref, hi_ref, first, last in halos:
 
-        def rows_in(t, j, lo_ref=lo_ref, hi_ref=hi_ref, first=first):
+        def rows_in(j, lo_ref=lo_ref, hi_ref=hi_ref, first=first):
             here = pl.ds(pl.multiple_of(8 * j, 8), 8)
             there = pl.ds(pl.multiple_of(8 * j - first, 8), 8)
-            lows, highs = [], []
-            for p in range(hx):
-                came = [halo_row(ref, tiles, packed, hx, t, p, there) for ref in (lo_ref, hi_ref)]
-                low_row, high_row = by_side(odd, *came)
-                lows.append(low_row)
-                highs.append(high_row)
-            one = lows + [est_ref[t, x, here, :] for x in range(hx)]
-            return [one, [est_ref[t, x, here, :] for x in range(cx - hx, cx)] + highs]
+            lows, highs = halo_tiles((lo_ref, hi_ref), odd, tiles, packed, hx, there)
+            return [
+                [
+                    lows[t] + [est_ref[t, x, here, :] for x in range(hx)],
+                    [est_ref[t, x, here, :] for x in range(cx - hx, cx)] + highs[t],
+                ]
+                for t in range(tiles)
+            ]
 
         def keep(t, j, pair):
             here = pl.ds(pl.multiple_of(8 * j, 8), 8)
@@ -394,11 +407,12 @@
                 for x in range(hx):
                     data_ref[t, hx * n + x, there, :] = w_ref[x + cx * n, here, :] * v[x + reach]
 
-        def rows_in_keep(t, j, rows_in=rows_in, keep=keep):
-            pair = rows_in(t, j)
+        def rows_in_keep(j, rows_in=rows_in, keep=keep):
+            rows = rows_in(j)
             if make:
-                keep(t, j, pair)
-            return pair
+                for t in range(tiles):
+                    keep(t, j, rows[t])
+            return rows
 
         def rows_out(t, j, n, values):
             mid = pl.ds(pl.multiple_of(8 * j - low, 8), 8)
@@ -406,8 +420,8 @@
                 mid_ref[t, hx * n + x, mid, :] = value
 
         def only_data(j, carry, rows_in=rows_in, keep=keep):
-            for t in range(tiles):
-                keep(t, j, rows_in(t, j))
+            for t, pair in enumerate(rows_in(j)):
+                keep(t, j, pair)
             return carry
 
         a, b = max(first // 8, data_first), min(last // 8, low // 8)
@@ -420,16 +434,19 @@
     def data_of(t, x, group):
         return data_ref[t, pl.ds(x, group), spot0 : spot0 + rows, :].reshape(group * rows, LANES)
 
-    correct(mid_ref, ty_ref, mats, plan["shifted"], 6, 2 * hx, rows, data_of, edge_ref)
+    correct(mid_ref, ty_ref, mats, starts, 6, 2 * hx, rows, data_of, edge_ref)
 
     blocks = -(-(high - low) // 8)
 
-    def back_in(t, j):
+    def back_in(j):
         here = pl.ds(pl.multiple_of(8 * j, 8), 8)
         there = pl.ds(pl.multiple_of(8 * j + low, 8), 8)
-        v = [edge_ref[t, x, here, :] for x in range(hx)]
-        v += [inner_ref[t, x, there, :] for x in range(cx - 2 * reach)]
-        return [v + [edge_ref[t, x, here, :] for x in range(hx, 2 * hx)]]
+        rows = []
+        for t in range(outs):
+            v = [edge_ref[t, x, here, :] for x in range(hx)]
+            v += [inner_ref[t, x, there, :] for x in range(cx - 2 * reach)]
+            rows.append([v + [edge_ref[t, x, here, :] for x in range(hx, 2 * hx)]])
+        return rows
 
     def back_out(t, j, n, values):
         here = pl.ds(pl.multiple_of(8 * j, 8), 8)
@@ -442,13 +459,11 @@
     def finish(t, x, j, acc):
         at = 8 * j + low + 2 * reach
         scale = 8 * j + low + off
-        old = est_ref[t, x, at : at + 8, :] * inv_ref[t, x, scale : scale + 8, :]
-        if lane0:
-            if t + 1 < tiles:
-                more = est_ref[t + 1, x, at : at + 8, :] * inv_ref[t + 1, x, scale : scale + 8, :]
-                lane = lax.broadcasted_iota(jnp.int32, (8, LANES), 1)
-                old = jnp.where(lane >= lane0, old, more)
-            old = pltpu.roll(old, LANES - lane0, 1)
+        if starts[t] == STEP * t:
+            old = est_ref[t, x, at : at + 8, :] * inv_ref[t, x, scale : scale + 8, :]
+        else:
+            old = [est_ref[n, x, at : at + 8, :] * inv_ref[n, x, scale : scale + 8, :] for n in range(tiles)]
+            old = regroup(old, starts[t])
         to = 8 * j + base
         out_ref[t, x, to : to + 8, :] = old * acc
 
@@ -476,11 +491,12 @@
     hy = 2 * reach * ITERS
     hx = 2 * reach
     slabs = lax.axis_size("gz")
-    tiles = ceil_to(nz + 2 * hz, LANES) // LANES
+    tiles = 1 + max(0, -(-(nz + 2 * hz - LANES) // STEP))
+    spans = contiguous(tiles)
     f32 = jnp.float32
 
     zones = zone_of_slice.astype(f32)
-    pad = tiles * LANES - nz - 2 * hz
+    pad = spans * LANES - nz - 2 * hz
     direct = slabs == 2 and nz % LANES == 0 and 4 * hz == LANES and cx % 2 == 0
     sx, sy = lax.axis_index("sx"), lax.axis_index("sy")
     place = jnp.stack([sx, sy]).astype(jnp.int32)
@@ -531,13 +547,14 @@
         before, after = first[:hz], second[:hz]
         ids_before, ids_after = first[hz].reshape(-1)[:hz], second[hz].reshape(-1)[:hz]
         volume = jnp.concatenate([before, observed, after, jnp.zeros((pad, cx, cy), f32)], axis=0)
-        volume = volume.reshape(tiles, LANES, cx, cy).transpose(0, 2, 3, 1)
-        edge = shape(tiles, cx * hy, LANES)
+        volume = volume.reshape(spans, LANES, cx, cy).transpose(0, 2, 3, 1)
+        edge = shape(spans, cx * hy, LANES)
         first, second = call(
             functools.partial(edges_kernel, hy, hz), [edge, edge], (place, volume), [], 8, 1, scalars=1
         )
         parts = [volume, lax.ppermute(first, "sy", both_ways(rounds_y[0])), lax.ppermute(second, "sy", both_ways(rounds_y[1]))]
     ids = jnp.concatenate([ids_before, zones, ids_after, jnp.full((pad,), -1.0, f32)])
+    ids = jnp.concatenate([ids[STEP * t : STEP * t + LANES] for t in range(tiles)])
 
     def lanes_of(kernels, names):
         match = (names[None, :] == jnp.arange(lateral_x.shape[0], dtype=f32)[:, None]).astype(f32)
@@ -551,8 +568,8 @@
     tx_own, ty_own = lanes_of(lateral_x, own_ids), lanes_of(lateral_y, own_ids)
 
     wide = cx + 2 * reach
-    packed = nz + 2 * hz - (tiles - 1) * LANES <= LANES // 2
-    planes = hx * (tiles - 1) + hx // 2 if packed else hx * tiles
+    packed = LANES + STEP * (tiles - 1) - (spans - 1) * LANES <= LANES // 2
+    planes = hx * (spans - 1) + hx // 2 if packed else hx * spans
     end0, end1, end2 = cy + 2 * hy, cy + 2 * hy - 4 * reach, cy
     mid1 = ceil_to(end1 // 2, 8) + 8
     mid2 = mid1 - ceil_to(4 * reach, 8)
@@ -577,12 +594,8 @@
     halo_a = swap(pays[:2])
     halo_b = swap(pays[2:])
 
-    wins = windows_of(tiles)
-    size = wins[0][1] * LANES
-    fh, fl, bh, bl, sh, sl = call(
-        functools.partial(band_kernel, hz),
-        [jax.ShapeDtypeStruct((len(wins), size, size), jnp.bfloat16)] * 4
-        + [jax.ShapeDtypeStruct((len(wins), size, own * LANES), jnp.bfloat16)] * 2,
+    forward, back = call(
+        band_kernel, [jax.ShapeDtypeStruct((2 * LANES, 2 * LANES), jnp.bfloat16)] * 2,
         (depth_psf, pays[-1]), [], 8, 1, scalars=1, unread=(1,),
     )
     stacks_x, stacks_y = stitch_width.shape[:2]
@@ -593,30 +606,32 @@
     )
     shift = 2 * reach
 
-    def inner(est, data_off, shifted, rows, need, back):
-        plan = dict(data_off=data_off, shifted=shifted, need=need)
-        args = (est, ext, weight, tx, ty, fh, fl) + back
+    overlap = tuple(STEP * t for t in range(tiles))
+    alone = tuple(hz + LANES * t for t in range(own))
+
+    def inner(est, data_off, starts, rows, need):
+        plan = dict(data_off=data_off, starts=starts, need=need)
         rows = ceil_to(rows, 8)
         return call(
-            functools.partial(inner_kernel, plan),
-            [shape(own if shifted else tiles, cx - shift, rows, LANES)], args,
-            [(tiles, cx - shift, rows + 16, LANES)], 24, 1,
+            functools.partial(inner_kernel, plan), [shape(len(starts), cx - shift, rows, LANES)],
+            (est, ext, weight, tx, ty, forward, back), [(tiles, cx - shift, rows + 16, LANES)], 24, 1,
         )[0]
 
     def outer(est, halos, extra, inner_part, last, plan, outs):
         rows = ceil_to(plan["high"] - plan["low"] + 2 * reach, 8)
-        back, lateral = ((sh, sl), (tx_own, ty_own)) if last else ((bh, bl), (tx, ty))
+        lateral = (tx_own, ty_own) if last else (tx, ty)
+        starts = alone if last else overlap
         args = (place, est) + tuple(h for _, pair in halos for h in pair) + extra
-        args += (inner_part, inv, tx, ty) + lateral + (fh, fl) + back
+        args += (inner_part, inv, tx, ty) + lateral + (forward, back)
         plan = dict(
             plan, hx=hx, packed=packed, halos=[rng for rng, _ in halos], make_data=not last, pay=not last,
-            shifted=last, data_off=shift if last else 0, lane0=hz if last else 0,
+            starts=starts, data_off=shift if last else 0,
         )
-        scratch = [(tiles, cx, rows + 16, LANES), (own if last else tiles, 2 * hx, rows, LANES)]
+        scratch = [(tiles, cx, rows + 16, LANES), (len(starts), 2 * hx, rows, LANES)]
         return call(functools.partial(outer_kernel, plan), outs, args, scratch, 16, 1, scalars=1)
 
     data_at = mid2 + 8
-    spread1 = inner(ext, 0, False, end1 + shift, end0, (bh, bl))
+    spread1 = inner(ext, 0, overlap, end1 + shift, end0)
     est_a, data_a, *pays = outer(
         ext, [((0, cut), halo_a)], (weight,), spread1, False,
         dict(low=0, high=mid1, data_base=0, prior=False),
@@ -629,7 +644,7 @@
         [shape(tiles, cx, ceil_to(end1, 8), LANES), shape(tiles, 2 * hx, full - data_at, LANES)] + pay_shapes(end1 - mid1),
     )
     halo_d = swap(pays)
-    spread2 = inner(est, shift, True, end2 + shift, end1, (sh, sl))
+    spread2 = inner(est, shift, alone, end2 + shift, end1)
     (out_a,) = outer(
         est, [((0, mid1), halo_c)], (data_a,), spread2, True,
         dict(low=0, high=mid2, data_base=0, prior=False), [shape(own, cx, mid2, LANES)],

time: 104 us -> 109 us (1.048); the launches traced: 104 us -> 107 us
  waiting for transfers between devices: 20 us -> 24 us
    ppermute x8, waiting for transfers between devices: 11.2 us -> 15.3 us  [swap(): got.append(lax.ppermute(pays[n], 'sx', rounds_x[n]))]
  transfers between devices with their start and end apart: 13 -> 13, of which waited for: 3 -> 4; matrix products, arithmetic and copies ran while one was open for 1% -> 1% of each run, Pallas kernels for 41% -> 36%
where the time goes in v6:
time: 109 us; the launch traced here: 107 us
  Pallas kernels  56.7 us (52%)
  waiting for transfers between devices  24 us (22%)
  starting transfers between devices  21.2 us (19%)
  local copies, waits for them, and re-layouts  4.61 us (4%)
    pallas_call x10, Pallas kernels, call(): pl.pallas_call(kernel, out_shape=out_shape, in_specs=[pl.BlockSpec(memory...  56.7 us
    ppermute x8, waiting for transfers between devices, swap(): got.append(lax.ppermute(pays[n], 'sx', rounds_x[n]))  15.3 us
    ppermute x8, starting transfers between devices, swap(): got.append(lax.ppermute(pays[n], 'sx', rounds_x[n]))  14.2 us
    ppermute x2, waiting for transfers between devices, body(): parts.append(lax.ppermute(value, ('sy', 'gz'), both_ways(cross)))  8.71 us
    ppermute x2, starting transfers between devices, body(): parts.append(lax.ppermute(value, ('sy', 'gz'), both_ways(cross)))  3.02 us
    ppermute x1, starting transfers between devices, body(): lax.ppermute(second, 'sy', both_ways(rounds_y[1]))  2.54 us
  transfers between devices with their start and end apart: 13, of which 4 were waited for; matrix products, arithmetic and copies ran while one was open for 1% of the time, Pallas kernels for 36%

profile of v6, /device:TPU:10, one launch (start us, length us, event | category | flops | bytes accessed | tf_op | source)
XLA Modules:
  0.0 107.5 jit_solution(17320341541587058364)
XLA Ops:
  0.0 2.0 %copy.22 = f32[2,128,16,128]{1,3,2,0:T(8,128)S(1)} copy(f32[2,128,16,128]{3,2,1,0:T(8,128)} %bitcast.33) | data formatting | bytes 4194304 | tf_op jit(solution)/shard_map/reshape | solution.py:523
  2.1 2.2 %shard_map.64 = (f32[2,192,128]{2,1,0:T(8,128)}, f32[2,192,128]{2,1,0:T(8,128)S(1)}, f32[192,128]{1,0:T(8,128)}, f32[192,128]{1,0:T(8,128)S(1)}, f32[1032,128]{1,0:T(8,128)}) custom-call(s32[2]{0:T(128)S(1)} %pad_add_fusion.place_ref, f32[2,16,128,128]{3,2,1,0:T(8,128)S(1)} %bitcast.31, f32[8,128]{1,0:T(8,128)S(1)} %pad.4.refs_0_), custom_call_target="tpu_custom_call" | custom-call | flops 1 | bytes 3219464 | tf_op jit(solution)/shard_map/pallas_call | solution.py:511
  4.4 1.5 %collective-permute-start.2 = (f32[1032,128]{1,0:T(8,128)}, f32[1032,128]{1,0:T(8,128)S(1)}, u32[]{:S(2)}, u32[]{:S(2)}) collective-permute-start(f32[1032,128]{1,0:T(8,128)} %get-tuple-element.29), channel_id=1, source_target_pairs={{0,1},{1,0},{2,3},{3,2},{4,5},{5,4},{6,7},{7,6},{8,9},{9,8},{10,11... | collective-permute-start | bytes 1585160 | tf_op jit(solution)/shard_map/ppermute | solution.py:530
  5.9 2.5 %collective-permute-start.1 = (f32[2,192,128]{2,1,0:T(8,128)S(1)}, f32[2,192,128]{2,1,0:T(8,128)S(1)}, u32[]{:S(2)}, u32[]{:S(2)}) collective-permute-start(f32[2,192,128]{2,1,0:T(8,128)S(1)} %get-tuple-element.28), channel_id=1, source_target_pairs={{2,4},{4,2},{3,5},{5,3},{10,12},{12,10},{11,13},{13,11},{18,20},{2... | collective-permute-start | bytes 589832 | tf_op jit(solution)/shard_map/ppermute | solution.py:531
  8.5 3.0 %collective-permute-start.4 = (f32[192,128]{1,0:T(8,128)S(1)}, f32[192,128]{1,0:T(8,128)S(1)}, u32[]{:S(2)}, u32[]{:S(2)}) collective-permute-start(f32[192,128]{1,0:T(8,128)S(1)} %get-tuple-element.31), channel_id=1, source_target_pairs={{2,5},{3,4},{5,2},{4,3},{10,13},{11,12},{13,10},{12,11},{18,21},{1... | collective-permute-start | bytes 294920 | tf_op jit(solution)/shard_map/ppermute | solution.py:535
  11.9 8.7 %collective-permute-done.3.refs_4_ = f32[192,128]{1,0:T(8,128)S(1)} collective-permute-done((f32[192,128]{1,0:T(8,128)}, f32[192,128]{1,0:T(8,128)S(1)}, u32[]{:S(2)}, u32[]{:S(2)}) %collective-permute-start.3) | collective-permute-done | bytes 98336 | tf_op jit(solution)/shard_map/ppermute | solution.py:535
  20.6 8.8 %shard_map.65 = (f32[3,16,160,128]{3,2,1,0:T(8,128)S(1)}, f32[15,96,128]{2,1,0:T(8,128)S(1)}, f32[15,96,128]{2,1,0:T(8,128)S(1)}, f32[15,56,128]{2,1,0:T(8,128)S(1)}, f32[15,56,128]{2,1,0:T(8,128)S(1)}) custom-call(s32[2]{0:T(128)S(1)} %pad_add_fusion.place_ref, f32[2,16,128,128]{3,2,1,0:T(8,128)S(1)} %bitcast.32, ...), custom_call_target="tpu_custom_call" | custom-call | flops 1 | bytes 9482248 | tf_op jit(solution)/shard_map/pallas_call | solution.py:511
  29.4 3.5 %collective-permute-start.8 = (f32[15,56,128]{2,1,0:T(8,128)S(1)}, f32[15,56,128]{2,1,0:T(8,128)S(1)}, u32[]{:S(2)}, u32[]{:S(2)}) collective-permute-start(f32[15,56,128]{2,1,0:T(8,128)S(1)} %get-tuple-element.36._), channel_id=1, source_target_pairs={{8,16},{16,8},{9,17},{17,9},{10,18},{18,10},{11,19},{19,11},{12,20... | collective-permute-start | bytes 1290248 | tf_op jit(solution)/shard_map/ppermute | solution.py:586
  32.9 0.7 shard_map.67
  33.8 2.4 %collective-permute-start.6 = (f32[15,96,128]{2,1,0:T(8,128)S(1)}, f32[15,96,128]{2,1,0:T(8,128)S(1)}, u32[]{:S(2)}, u32[]{:S(2)}) collective-permute-start(f32[15,96,128]{2,1,0:T(8,128)S(1)} %get-tuple-element.34), channel_id=1, source_target_pairs={{8,16},{16,8},{9,17},{17,9},{10,18},{18,10},{11,19},{19,11},{12,20... | collective-permute-start | bytes 2211848 | tf_op jit(solution)/shard_map/ppermute | solution.py:586
  36.9 4.9 %shard_map.66 = (f32[22,160,128]{2,1,0:T(8,128)S(1)}, f32[3,16,144,128]{3,2,1,0:T(8,128)S(1)}) custom-call(s32[2]{0:T(128)S(1)} %pad_add_fusion.place_ref, s32[32]{0:T(128)S(1)} %reshape.66.bands_ref, f32[15,56,128]{2,1,0:T(8,128)S(1)} %get-tuple-element.36._, f32[3,7,8,128]{3,2,1,0:T(8,128)S(1)} %broadcast_in_dim.17.tx_ref.refs_6_.refs_8_.refs_9_.refs_11_, ...), custom_call_target="tpu_custom_call" | custom-call | flops 1 | bytes 5943432 | tf_op jit(solution)/shard_map/pallas_call | solution.py:511
  41.8 4.5 %shard_map.68.refs_4_.refs_7_ = f32[3,10,152,128]{3,2,1,0:T(8,128)S(1)} custom-call(f32[3,16,160,128]{3,2,1,0:T(8,128)S(1)} %get-tuple-element.32.est_ref.obs_ref.refs_0_, f32[3,16,160,128]{3,2,1,0:T(8,128)S(1)} %get-tuple-element.32.est_ref.obs_ref.refs_0_, f32[22,160,128]{2,1,0:T(8,128)S(1)} %get-tuple-element.37.w_ref.refs_3_.refs_5_, ...), custom_call_target="tpu_custom_call" | custom-call | flops 1 | bytes 12697600 | tf_op jit(solution)/shard_map/pallas_call | solution.py:511
  46.3 6.8 %collective-permute-done.5.refs_1_ = f32[15,96,128]{2,1,0:T(8,128)S(1)} collective-permute-done((f32[15,96,128]{2,1,0:T(8,128)S(1)}, f32[15,96,128]{2,1,0:T(8,128)S(1)}, u32[]{:S(2)}, u32[]{:S(2)}) %collective-permute-start.5) | collective-permute-done | bytes 737312 | tf_op jit(solution)/shard_map/ppermute | solution.py:586
  53.1 6.5 %collective-permute-done.6.refs_2_ = f32[15,96,128]{2,1,0:T(8,128)S(1)} collective-permute-done((f32[15,96,128]{2,1,0:T(8,128)S(1)}, f32[15,96,128]{2,1,0:T(8,128)S(1)}, u32[]{:S(2)}, u32[]{:S(2)}) %collective-permute-start.6) | collective-permute-done | bytes 737312 | tf_op jit(solution)/shard_map/ppermute | solution.py:586
  59.6 9.4 %shard_map.69 = (f32[3,16,80,128]{3,2,1,0:T(8,128)S(1)}, f32[3,12,96,128]{3,2,1,0:T(8,128)S(1)}, f32[15,80,128]{2,1,0:T(8,128)S(1)}, f32[15,80,128]{2,1,0:T(8,128)S(1)}) custom-call(s32[2]{0:T(128)S(1)} %pad_add_fusion.place_ref, f32[3,16,160,128]{3,2,1,0:T(8,128)S(1)} %get-tuple-element.32.est_ref.obs_ref.refs_0_, ...), custom_call_target="tpu_custom_call" | custom-call | flops 1 | bytes 18915336 | tf_op jit(solution)/shard_map/pallas_call | solution.py:511
  69.0 3.5 %collective-permute-start.10 = (f32[15,80,128]{2,1,0:T(8,128)S(1)}, f32[15,80,128]{2,1,0:T(8,128)S(1)}, u32[]{:S(2)}, u32[]{:S(2)}) collective-permute-start(f32[15,80,128]{2,1,0:T(8,128)S(1)} %get-tuple-element.44), channel_id=1, source_target_pairs={{8,16},{16,8},{9,17},{17,9},{10,18},{18,10},{11,19},{19,11},{12,20... | collective-permute-start | bytes 1843208 | tf_op jit(solution)/shard_map/ppermute | solution.py:586
  72.6 8.1 %shard_map.70 = (f32[3,16,144,128]{3,2,1,0:T(8,128)S(1)}, f32[3,12,88,128]{3,2,1,0:T(8,128)S(1)}, f32[15,64,128]{2,1,0:T(8,128)S(1)}, f32[15,64,128]{2,1,0:T(8,128)S(1)}) custom-call(s32[2]{0:T(128)S(1)} %pad_add_fusion.place_ref, f32[3,16,160,128]{3,2,1,0:T(8,128)S(1)} %get-tuple-element.32.est_ref.obs_ref.refs_0_, ...), custom_call_target="tpu_custom_call" | custom-call | flops 1 | bytes 22921224 | tf_op jit(solution)/shard_map/pallas_call | solution.py:511
  80.8 2.0 %collective-permute-start.11 = (f32[15,64,128]{2,1,0:T(8,128)S(1)}, f32[15,64,128]{2,1,0:T(8,128)S(1)}, u32[]{:S(2)}, u32[]{:S(2)}) collective-permute-start(f32[15,64,128]{2,1,0:T(8,128)S(1)} %get-tuple-element.46), channel_id=1, source_target_pairs={{0,8},{16,24},{8,0},{24,16},{1,9},{17,25},{9,1},{25,17},{2,10},{18... | collective-permute-start | bytes 1474568 | tf_op jit(solution)/shard_map/ppermute | solution.py:586
  82.8 2.3 %collective-permute-start.12 = (f32[15,64,128]{2,1,0:T(8,128)S(1)}, f32[15,64,128]{2,1,0:T(8,128)S(1)}, u32[]{:S(2)}, u32[]{:S(2)}) collective-permute-start(f32[15,64,128]{2,1,0:T(8,128)S(1)} %get-tuple-element.47), channel_id=1, source_target_pairs={{8,16},{16,8},{9,17},{17,9},{10,18},{18,10},{11,19},{19,11},{12,20... | collective-permute-start | bytes 1474568 | tf_op jit(solution)/shard_map/ppermute | solution.py:586
  85.2 4.2 %shard_map.71.refs_4_.refs_6_ = f32[2,10,136,128]{3,2,1,0:T(8,128)S(1)} custom-call(f32[3,16,144,128]{3,2,1,0:T(8,128)S(1)} %get-tuple-element.42.est_ref.refs_0_, f32[3,16,160,128]{3,2,1,0:T(8,128)S(1)} %get-tuple-element.32.est_ref.obs_ref.refs_0_, f32[22,160,128]{2,1,0:T(8,128)S(1)} %get-tuple-element.37.w_ref.refs_3_.refs_5_, ...), custom_call_target="tpu_custom_call" | custom-call | flops 1 | bytes 11362304 | tf_op jit(solution)/shard_map/pallas_call | solution.py:511
  89.5 6.9 %shard_map.72 = f32[2,16,64,128]{3,2,1,0:T(8,128)S(1)} custom-call(s32[2]{0:T(128)S(1)} %pad_add_fusion.place_ref, f32[3,16,144,128]{3,2,1,0:T(8,128)S(1)} %get-tuple-element.42.est_ref.refs_0_, f32[15,80,128]{2,1,0:T(8,128)S(1)} %collective-permute-done.9.refs_1_, f32[15,80,128]{2,1,0:T(8,128)S(1)} %collective-permute-done.10.refs_2_, ...), custom_call_target="tpu_custom_call" | custom-call | flops 1 | bytes 13328392 | tf_op jit(solution)/shard_map/pallas_call | solution.py:511
  96.4 2.0 %collective-permute-done.11.refs_3_ = f32[15,64,128]{2,1,0:T(8,128)S(1)} collective-permute-done((f32[15,64,128]{2,1,0:T(8,128)S(1)}, f32[15,64,128]{2,1,0:T(8,128)S(1)}, u32[]{:S(2)}, u32[]{:S(2)}) %collective-permute-start.11) | collective-permute-done | bytes 491552 | tf_op jit(solution)/shard_map/ppermute | solution.py:586
  98.4 6.8 %shard_map.73 = f32[2,16,64,128]{3,2,1,0:T(8,128)S(1)} custom-call(s32[2]{0:T(128)S(1)} %pad_add_fusion.place_ref, f32[3,16,144,128]{3,2,1,0:T(8,128)S(1)} %get-tuple-element.42.est_ref.refs_0_, f32[15,80,128]{2,1,0:T(8,128)S(1)} %collective-permute-done.9.refs_1_, f32[15,80,128]{2,1,0:T(8,128)S(1)} %collective-permute-done.10.refs_2_, ...), custom_call_target="tpu_custom_call" | custom-call | flops 1 | bytes 14163976 | tf_op jit(solution)/shard_map/pallas_call | solution.py:511
  105.5 2.0 %copy.30 = f32[2,128,16,128]{3,2,1,0:T(8,128)} copy(f32[2,128,16,128]{1,3,2,0:T(8,128)S(1)} %maximum_bitcast_fusion) | data formatting | bytes 4194304 | tf_op jit(solution)/shard_map/transpose | solution.py:657
  (47 shorter events, 1.9 us)
Async XLA Ops:
  0.0 2.0 %copy-start.4 = (s32[256]{0:T(256)S(1)}, s32[256]{0:T(256)}, u32[]{:S(2)}) copy-start(s32[256]{0:T(256)} %param.7) | copy-start | bytes 3076
  2.0 9.5 %copy-start.2 = (f32[8,7]{1,0:T(8,128)S(1)}, f32[8,7]{1,0:T(8,128)}, u32[]{:S(2)}) copy-start(f32[8,7]{1,0:T(8,128)} %param.8) | copy-start | bytes 676
  2.0 9.6 %copy-start.3 = (f32[8,7]{1,0:T(8,128)S(1)}, f32[8,7]{1,0:T(8,128)}, u32[]{:S(2)}) copy-start(f32[8,7]{1,0:T(8,128)} %param.9) | copy-start | bytes 676
  2.0 9.7 %copy-start.1 = (s32[4,4,2]{1,2,0:T(2,128)S(1)}, s32[4,4,2]{1,2,0:T(2,128)}, u32[]{:S(2)}) copy-start(s32[4,4,2]{1,2,0:T(2,128)} %param.11) | copy-start | bytes 388
  4.4 28.6 %copy-start = (f32[17]{0:T(128)S(1)}, f32[17]{0:T(128)}, u32[]{:S(2)}) copy-start(f32[17]{0:T(128)} %psf_ref.1) | copy-start | bytes 208
  4.4 16.3 %collective-permute-start.2 = (f32[1032,128]{1,0:T(8,128)}, f32[1032,128]{1,0:T(8,128)S(1)}, u32[]{:S(2)}, u32[]{:S(2)}) collective-permute-start(f32[1032,128]{1,0:T(8,128)} %get-tuple-element.29), channel_id=1, source_target_pairs={{0,1},{1,0},{2,3},{3,2},{4,5},{5,4},{6,7},{7,6},{8,9},{9,8},{10,11... | collective-permute-start | bytes 1585160 | tf_op jit(solution)/shard_map/ppermute | solution.py:530
  5.9 14.8 %collective-permute-start = (f32[2,192,128]{2,1,0:T(8,128)}, f32[2,192,128]{2,1,0:T(8,128)S(1)}, u32[]{:S(2)}, u32[]{:S(2)}) collective-permute-start(f32[2,192,128]{2,1,0:T(8,128)} %get-tuple-element.27), channel_id=1, source_target_pairs={{0,2},{4,6},{2,0},{6,4},{1,3},{5,7},{3,1},{7,5},{8,10},{12,14},{10... | collective-permute-start | bytes 589832 | tf_op jit(solution)/shard_map/ppermute | solution.py:531
  5.9 14.8 %collective-permute-start.1 = (f32[2,192,128]{2,1,0:T(8,128)S(1)}, f32[2,192,128]{2,1,0:T(8,128)S(1)}, u32[]{:S(2)}, u32[]{:S(2)}) collective-permute-start(f32[2,192,128]{2,1,0:T(8,128)S(1)} %get-tuple-element.28), channel_id=1, source_target_pairs={{2,4},{4,2},{3,5},{5,3},{10,12},{12,10},{11,13},{13,11},{18,20},{2... | collective-permute-start | bytes 589832 | tf_op jit(solution)/shard_map/ppermute | solution.py:531
  8.4 12.2 %collective-permute-start.3 = (f32[192,128]{1,0:T(8,128)}, f32[192,128]{1,0:T(8,128)S(1)}, u32[]{:S(2)}, u32[]{:S(2)}) collective-permute-start(f32[192,128]{1,0:T(8,128)} %get-tuple-element.30), channel_id=1, source_target_pairs={{0,3},{1,2},{4,7},{5,6},{3,0},{2,1},{7,4},{6,5},{8,11},{9,10},{12,... | collective-permute-start | bytes 294920 | tf_op jit(solution)/shard_map/ppermute | solution.py:535
  8.5 12.1 %collective-permute-start.4 = (f32[192,128]{1,0:T(8,128)S(1)}, f32[192,128]{1,0:T(8,128)S(1)}, u32[]{:S(2)}, u32[]{:S(2)}) collective-permute-start(f32[192,128]{1,0:T(8,128)S(1)} %get-tuple-element.31), channel_id=1, source_target_pairs={{2,5},{3,4},{5,2},{4,3},{10,13},{11,12},{13,10},{12,11},{18,21},{1... | collective-permute-start | bytes 294920 | tf_op jit(solution)/shard_map/ppermute | solution.py:535
  29.4 43.2 %collective-permute-start.8 = (f32[15,56,128]{2,1,0:T(8,128)S(1)}, f32[15,56,128]{2,1,0:T(8,128)S(1)}, u32[]{:S(2)}, u32[]{:S(2)}) collective-permute-start(f32[15,56,128]{2,1,0:T(8,128)S(1)} %get-tuple-element.36._), channel_id=1, source_target_pairs={{8,16},{16,8},{9,17},{17,9},{10,18},{18,10},{11,19},{19,11},{12,20... | collective-permute-start | bytes 1290248 | tf_op jit(solution)/shard_map/ppermute | solution.py:586
  33.7 19.4 %collective-permute-start.5 = (f32[15,96,128]{2,1,0:T(8,128)S(1)}, f32[15,96,128]{2,1,0:T(8,128)S(1)}, u32[]{:S(2)}, u32[]{:S(2)}) collective-permute-start(f32[15,96,128]{2,1,0:T(8,128)S(1)} %get-tuple-element.33), channel_id=1, source_target_pairs={{0,8},{16,24},{8,0},{24,16},{1,9},{17,25},{9,1},{25,17},{2,10},{18... | collective-permute-start | bytes 2211848 | tf_op jit(solution)/shard_map/ppermute | solution.py:586
  33.8 25.8 %collective-permute-start.6 = (f32[15,96,128]{2,1,0:T(8,128)S(1)}, f32[15,96,128]{2,1,0:T(8,128)S(1)}, u32[]{:S(2)}, u32[]{:S(2)}) collective-permute-start(f32[15,96,128]{2,1,0:T(8,128)S(1)} %get-tuple-element.34), channel_id=1, source_target_pairs={{8,16},{16,8},{9,17},{17,9},{10,18},{18,10},{11,19},{19,11},{12,20... | collective-permute-start | bytes 2211848 | tf_op jit(solution)/shard_map/ppermute | solution.py:586
  36.4 36.3 %collective-permute-start.7 = (f32[15,56,128]{2,1,0:T(8,128)S(1)}, f32[15,56,128]{2,1,0:T(8,128)S(1)}, u32[]{:S(2)}, u32[]{:S(2)}) collective-permute-start(f32[15,56,128]{2,1,0:T(8,128)S(1)} %get-tuple-element.35), channel_id=1, source_target_pairs={{0,8},{16,24},{8,0},{24,16},{1,9},{17,25},{9,1},{25,17},{2,10},{18... | collective-permute-start | bytes 1290248 | tf_op jit(solution)/shard_map/ppermute | solution.py:586
  69.0 20.5 %collective-permute-start.10 = (f32[15,80,128]{2,1,0:T(8,128)S(1)}, f32[15,80,128]{2,1,0:T(8,128)S(1)}, u32[]{:S(2)}, u32[]{:S(2)}) collective-permute-start(f32[15,80,128]{2,1,0:T(8,128)S(1)} %get-tuple-element.44), channel_id=1, source_target_pairs={{8,16},{16,8},{9,17},{17,9},{10,18},{18,10},{11,19},{19,11},{12,20... | collective-permute-start | bytes 1843208 | tf_op jit(solution)/shard_map/ppermute | solution.py:586
  72.5 17.0 %collective-permute-start.9 = (f32[15,80,128]{2,1,0:T(8,128)S(1)}, f32[15,80,128]{2,1,0:T(8,128)S(1)}, u32[]{:S(2)}, u32[]{:S(2)}) collective-permute-start(f32[15,80,128]{2,1,0:T(8,128)S(1)} %get-tuple-element.43), channel_id=1, source_target_pairs={{0,8},{16,24},{8,0},{24,16},{1,9},{17,25},{9,1},{25,17},{2,10},{18... | collective-permute-start | bytes 1843208 | tf_op jit(solution)/shard_map/ppermute | solution.py:586
  80.8 17.7 %collective-permute-start.11 = (f32[15,64,128]{2,1,0:T(8,128)S(1)}, f32[15,64,128]{2,1,0:T(8,128)S(1)}, u32[]{:S(2)}, u32[]{:S(2)}) collective-permute-start(f32[15,64,128]{2,1,0:T(8,128)S(1)} %get-tuple-element.46), channel_id=1, source_target_pairs={{0,8},{16,24},{8,0},{24,16},{1,9},{17,25},{9,1},{25,17},{2,10},{18... | collective-permute-start | bytes 1474568 | tf_op jit(solution)/shard_map/ppermute | solution.py:586
  82.8 15.7 %collective-permute-start.12 = (f32[15,64,128]{2,1,0:T(8,128)S(1)}, f32[15,64,128]{2,1,0:T(8,128)S(1)}, u32[]{:S(2)}, u32[]{:S(2)}) collective-permute-start(f32[15,64,128]{2,1,0:T(8,128)S(1)} %get-tuple-element.47), channel_id=1, source_target_pairs={{8,16},{16,8},{9,17},{17,9},{10,18},{18,10},{11,19},{19,11},{12,20... | collective-permute-start | bytes 1474568 | tf_op jit(solution)/shard_map/ppermute | solution.py:586

commit v7 on v6

--- a/solution.py
+++ b/solution.py
@@ -13,6 +13,7 @@
 TINY = 1e-30
 EDGE = 16
 STEP = LANES - 2 * EDGE
+LAP = LANES - STEP
 VMEM = pl.BlockSpec(memory_space=pltpu.VMEM)
 
 
@@ -26,10 +27,6 @@
 
 def both_ways(pairs):
     return pairs + [(j, i) for i, j in pairs]
-
-
-def lane_is_low():
-    return lax.broadcasted_iota(jnp.int32, (8, LANES), 1) < LANES // 2
 
 
 def spin(value, shift):
@@ -48,41 +45,29 @@
     return out
 
 
-def window(roll_of, start, shape):
-    first, off = divmod(start, LANES)
-    if off == 0:
-        return roll_of(first, 0)
-    lane = lax.broadcasted_iota(jnp.int32, shape, 1)
-    return jnp.where(lane < LANES - off, roll_of(first, LANES - off), roll_of(first + 1, LANES - off))
-
-
 def halo_tiles(refs, odd, tiles, packed, hx, rows):
     planes, half = {}, hx // 2
 
-    def plane(index):
+    def plane(index, side):
         if index not in planes:
             planes[index] = by_side(odd, refs[0][index, rows, :], refs[1][index, rows, :])
-        return planes[index]
-
-    spans = contiguous(tiles)
+        return planes[index][side]
+
     sides = []
+    lane = lax.broadcasted_iota(jnp.int32, (8, LANES), 1)
     for side in range(2):
         out = [[] for _ in range(tiles)]
         for p in range(hx):
-
-            def roll_of(k, shift, p=p):
-                if packed and k == spans - 1:
-                    return spin(plane(hx * k + p % half)[side], shift + (LANES // 2 if p >= half else 0))
-                return spin(plane(hx * k + p)[side], shift)
-
-            for t in range(tiles):
-                out[t].append(window(roll_of, STEP * t, (8, LANES)))
+            if not packed:
+                for t in range(tiles):
+                    out[t].append(plane(hx * t + p, side))
+                continue
+            one, two, end = plane(p, side), plane(hx + p, side), plane(2 * hx + p % half, side)
+            out[0].append(one)
+            out[1].append(jnp.where(lane < LAP, spin(one, LAP), two))
+            out[2].append(jnp.where(lane < 2 * LAP, spin(two, LAP), spin(end, LANES // 2 if p >= half else 0)))
         sides.append(out)
     return sides
-
-
-def contiguous(tiles):
-    return -(-(LANES + STEP * (tiles - 1)) // LANES)
 
 
 def pack_both(src, pays, odd, packed, hx, blocks, src_block):
@@ -97,21 +82,21 @@
 
 def pack_rows(src, pay, packed, hx, x0, blocks, src_block, pay_block):
     tiles = src.shape[0]
-    spans = contiguous(tiles)
     half = hx // 2
 
     def step(j, carry):
         here = pl.ds(pl.multiple_of(8 * (j + src_block), 8), 8)
         there = pl.ds(pl.multiple_of(8 * (j + pay_block), 8), 8)
-        rows = [[src[t, x0 + p, here, :] for t in range(tiles)] for p in range(hx)]
-        for k in range(spans - 1 if packed else spans):
-            for p in range(hx):
-                pay[hx * k + p, there, :] = regroup(rows[p], LANES * k)
-        if packed:
-            last = LANES * (spans - 1)
-            for p in range(half):
-                other = spin(regroup(rows[p + half], last), LANES // 2)
-                pay[hx * (spans - 1) + p, there, :] = jnp.where(lane_is_low(), regroup(rows[p], last), other)
+        lane = lax.broadcasted_iota(jnp.int32, (8, LANES), 1)
+        for p in range(hx):
+            for t in range(1 if packed else tiles):
+                pay[hx * t + p, there, :] = src[t, x0 + p, here, :]
+            if packed:
+                last = src[2, x0 + p, here, :]
+                pay[hx + p, there, :] = jnp.where(lane < LAP, spin(last, -LAP), src[1, x0 + p, here, :])
+                if p < half:
+                    other = spin(src[2, x0 + p + half, here, :], LANES // 2)
+                    pay[2 * hx + p, there, :] = jnp.where(lane < LANES // 2, other, last)
         return carry
 
     lax.fori_loop(0, blocks, step, 0)
@@ -142,14 +127,26 @@
     lax.fori_loop(0, width, step, 0)
 
 
-def depth_rows(parts, both_ref):
-    rows = parts[0].shape[0]
+def halves(parts):
     whole = jnp.concatenate(parts, axis=0)
     hi = whole.astype(jnp.bfloat16)
-    lo = (whole - hi.astype(jnp.float32)).astype(jnp.bfloat16)
-    res = jnp.dot(jnp.concatenate([hi, lo], axis=1), both_ref[...], preferred_element_type=jnp.float32)
-    res = res[:, :LANES] + res[:, LANES:]
-    return [res[rows * t : rows * (t + 1)] for t in range(len(parts))]
+    return jnp.concatenate([hi, (whole - hi.astype(jnp.float32)).astype(jnp.bfloat16)], axis=1)
+
+
+def depth_sums(pair, matrix):
+    res = jnp.dot(pair, matrix, preferred_element_type=jnp.float32)
+    return res[:, :LANES] + res[:, LANES:]
+
+
+def own_pairs(tiles, starts):
+    pairs = []
+    for k, start in enumerate(starts):
+        for t in range(tiles):
+            first = max(0 if t == 0 else STEP * t + EDGE - start, 0)
+            stop = min(LANES if t == tiles - 1 else STEP * (t + 1) + EDGE - start, LANES)
+            if first < stop:
+                pairs.append((k, t, first, stop))
+    return pairs
 
 
 def x_loop(taps, reverse, first, last, rows_in, rows_out):
@@ -181,24 +178,45 @@
 
 
 def correct(mid_ref, ty_ref, mats, starts, group, count, rows, data_of, spread_ref):
-    forward_ref, back_ref = mats
+    forward_ref, back_ref, *more = mats
     tiles = mid_ref.shape[0]
     group = next(n for n in range(group, 0, -1) if count % n == 0 and n * rows % 16 == 0)
 
     def depth(i, carry):
         first = group * i
         blurred = [y_group(mid_ref, ty_ref, t, first, group, rows // 8) for t in range(tiles)]
-        blurred = depth_rows(blurred, forward_ref)
-        ratio = [data_of(t, first, group) / jnp.maximum(blurred[t], TINY) for t in range(tiles)]
-        spread = depth_rows(ratio, back_ref)
-        for t, start in enumerate(starts):
-            spread_ref[t, pl.ds(first, group), 0:rows, :] = regroup(spread, start).reshape(group, rows, LANES)
+        size = group * rows
+        blurred = depth_sums(halves(blurred), forward_ref[...])
+        ratio = []
+        for t in range(tiles):
+            ratio.append(data_of(t, first, group) / jnp.maximum(blurred[size * t : size * (t + 1)], TINY))
+        ratio = halves(ratio)
+        if starts[0] == 0:
+            spread = depth_sums(ratio, back_ref[...])
+            spread = [spread[size * t : size * (t + 1)] for t in range(tiles)]
+            if tiles > 1:
+                ends = depth_sums(ratio, more[0][...])
+                ends = [ends[size * t : size * (t + 1)] for t in range(tiles)]
+                lane = lax.broadcasted_iota(jnp.int32, (size, LANES), 1)
+                for t in range(tiles):
+                    if t > 0:
+                        spread[t] = jnp.where(lane < EDGE, ends[t - 1], spread[t])
+                    if t < tiles - 1:
+                        spread[t] = jnp.where(lane >= LANES - EDGE, ends[t + 1], spread[t])
+        else:
+            spread = [None] * len(starts)
+            for n, (k, t, _, _) in enumerate(own_pairs(tiles, starts)):
+                part = depth_sums(ratio[size * t : size * (t + 1)], back_ref[n])
+                spread[k] = part if spread[k] is None else spread[k] + part
+        for t, value in enumerate(spread):
+            spread_ref[t, pl.ds(first, group), 0:rows, :] = value.reshape(group, rows, LANES)
         return carry
 
     lax.fori_loop(0, count // group, depth, 0)
 
 
-def inner_kernel(plan, est_ref, obs_ref, w_ref, tx_ref, ty_ref, forward_ref, back_ref, spread_ref, mid_ref):
+def inner_kernel(plan, est_ref, obs_ref, w_ref, tx_ref, ty_ref, *refs):
+    *mats, spread_ref, mid_ref = refs
     tiles, cx = est_ref.shape[:2]
     reach = (tx_ref.shape[1] - 1) // 2
     rows = spread_ref.shape[2]
@@ -220,7 +238,7 @@
         seen = obs_ref[t, pl.ds(x + reach, group), first : first + rows, :]
         return (seen * w_ref[pl.ds(x + 2 * reach, group), first : first + rows, :]).reshape(group * rows, LANES)
 
-    correct(mid_ref, ty_ref, (forward_ref, back_ref), plan["starts"], 2, count, rows, data_of, spread_ref)
+    correct(mid_ref, ty_ref, mats, plan["starts"], 2, count, rows, data_of, spread_ref)
 
 
 def norm_kernel(plan, place_ref, bands_ref, _, tx_ref, ty_ref, w_ref, out_ref, mid_ref):
@@ -270,33 +288,47 @@
         lax.fori_loop(0, width, ystep, 0)
 
 
-def band_kernel(psf_ref, _, forward_ref, back_ref):
+def band_kernel(pairs, starts, psf_ref, _, forward_ref, back_ref, ends_ref, own_ref):
     taps = psf_ref.shape[0]
     total = psf_ref[0]
     for j in range(1, taps):
         total = total + psf_ref[j]
     shape = (LANES, LANES)
-    off = lax.broadcasted_iota(jnp.int32, shape, 1) - lax.broadcasted_iota(jnp.int32, shape, 0) + (taps - 1) // 2
-    band, flip = jnp.zeros(shape, jnp.float32), jnp.zeros(shape, jnp.float32)
-    for j in range(taps):
-        band = jnp.where(off == j, psf_ref[j], band)
-        flip = jnp.where(off == taps - 1 - j, psf_ref[j], flip)
-    for matrix, ref in ((band, forward_ref), (flip, back_ref)):
+    row = lax.broadcasted_iota(jnp.int32, shape, 0)
+    lane = lax.broadcasted_iota(jnp.int32, shape, 1)
+
+    def fill(ref, target, sign, keep):
+        off = sign * (target - row) + (taps - 1) // 2
+        matrix = jnp.zeros(shape, jnp.float32)
+        for j in range(taps):
+            matrix = jnp.where(off == j, psf_ref[j], matrix)
         matrix = matrix / jnp.full(shape, total, jnp.float32)
+        if keep is not None:
+            matrix = jnp.where(keep, matrix, 0.0)
         hi = matrix.astype(jnp.bfloat16)
         ref[:LANES, :LANES] = hi
         ref[LANES:, :LANES] = hi
         ref[:LANES, LANES:] = (matrix - hi.astype(jnp.float32)).astype(jnp.bfloat16)
         ref[LANES:, LANES:] = jnp.zeros(shape, jnp.bfloat16)
 
-
-def overlapping(tiles, shift, main, halo):
-    series = main if halo is None else [halo, *main, halo]
-    start = 0 if halo is None else LANES - shift
-    return [window(lambda k, turn: spin(series[k], turn), start + STEP * t, main[0].shape) for t in range(tiles)]
-
-
-def edges_kernel(hy, shift, place_ref, vol_ref, *refs):
+    fill(forward_ref, lane, 1, None)
+    fill(back_ref, lane, -1, None)
+    side = (lane < EDGE) | (lane >= LANES - EDGE)
+    fill(ends_ref, jnp.where(lane < EDGE, lane + STEP, lane - STEP), -1, side)
+    for n, (k, t, first, stop) in enumerate(pairs):
+        fill(own_ref.at[n], lane + starts[k] - STEP * t, -1, (lane >= first) & (lane < stop))
+
+
+def with_halo(parts, halo, turned, width):
+    if halo is None:
+        return parts
+    lane = lax.broadcasted_iota(jnp.int32, halo.shape, 1)
+    first = jnp.where(lane < width, halo, parts[0])
+    last = jnp.where(lane >= LANES - width, turned, parts[-1])
+    return [first, *parts[1:-1], last]
+
+
+def edges_kernel(hy, width, turn, place_ref, vol_ref, *refs):
     tiles, cx, cy = vol_ref.shape[:3]
     odd = place_ref[1] % 2
     direct = len(refs) > 2
@@ -305,12 +337,12 @@
         lane = lax.broadcasted_iota(jnp.int32, (cy, LANES), 1)
         half = cx // 2
 
-        def outmost(x):
-            return pltpu.roll(jnp.where(lane < LANES // 2, vol_ref[0, x], vol_ref[tiles - 1, x]), shift, 1)
+        def outmost(low, high, at):
+            return jnp.where(at < width, spin(high, -turn), low)
 
         for x in range(half):
-            other = pltpu.roll(outmost(x + half), LANES // 2, 1)
-            depth_ref[cy * x : cy * x + cy, :] = jnp.where(lane < LANES // 2, outmost(x), other)
+            one, two = [outmost(vol_ref[0, n], vol_ref[tiles - 1, n], lane) for n in (x, x + half)]
+            depth_ref[cy * x : cy * x + cy, :] = jnp.where(lane < LANES // 2, one, spin(two, LANES // 2))
         depth_ref[cy * half :, :] = zones_ref[...]
     else:
         first_ref, second_ref = refs
@@ -324,7 +356,7 @@
             first_ref[t, to, :], second_ref[t, to, :] = both[-1]
         if direct:
             for n, ref in enumerate((first_z, second_z)):
-                ref[to, :] = jnp.where(lane < LANES // 2, both[0][n], both[-1][n])
+                ref[to, :] = outmost(both[0][n], both[-1][n], lane)
 
 
 def assemble_kernel(packed, hx, cut, shift, refs_in, place_ref, *refs):
@@ -337,19 +369,19 @@
     odd = place_ref[1] % 2
     half = cx // 2
 
+    tiles = ext_ref.shape[0]
     for x in range(cx):
         edge = slice(hy * x, hy * x + hy)
         low, high = zip(*[by_side(odd, first_ref[t, edge, :], second_ref[t, edge, :]) for t in range(main)])
-        low_z = high_z = halo = None
+        mids = [vol_ref[t, x] for t in range(main)]
         if depth_ref is not None:
             low_z, high_z = by_side(odd, first_z[edge, :], second_z[edge, :])
+            low = with_halo(low, low_z, spin(low_z, LANES // 2), shift)
+            high = with_halo(high, high_z, spin(high_z, LANES // 2), shift)
             halo = depth_ref[cy * (x % half) : cy * (x % half) + cy, :]
-            halo = spin(halo, (LANES // 2 if x >= half else 0) - shift)
-        tiles = ext_ref.shape[0]
-        low = overlapping(tiles, shift, list(low), low_z)
-        mids = overlapping(tiles, shift, [vol_ref[t, x] for t in range(main)], halo)
-        high = overlapping(tiles, shift, list(high), high_z)
-        for t in range(ext_ref.shape[0]):
+            pair = (halo, spin(halo, LANES // 2))
+            mids = with_halo(mids, *(pair if x < half else pair[::-1]), shift)
+        for t in range(tiles):
             ext_ref[t, x, 0:hy, :] = low[t]
             ext_ref[t, x, hy : hy + cy, :] = mids[t]
             ext_ref[t, x, hy + cy : end, :] = high[t]
@@ -371,7 +403,7 @@
     data_in = None if make else take(0)
     prior_ref = take(0) if plan["prior"] else None
     inner_ref, inv_ref, tx_ref, ty_ref, bx_ref, by_ref = [take(0) for _ in range(6)]
-    mats = [take(0) for _ in range(2)]
+    mats = [take(0) for _ in range(plan["mats"])]
     out_ref = take(0)
     data_ref = take(0) if make else data_in
     pays = [take(0), take(0)] if plan["pay"] else None
@@ -492,12 +524,11 @@
     hx = 2 * reach
     slabs = lax.axis_size("gz")
     tiles = 1 + max(0, -(-(nz + 2 * hz - LANES) // STEP))
-    spans = contiguous(tiles)
     f32 = jnp.float32
 
     zones = zone_of_slice.astype(f32)
-    pad = spans * LANES - nz - 2 * hz
-    direct = slabs == 2 and nz % LANES == 0 and 4 * hz == LANES and cx % 2 == 0
+    pad = LANES + STEP * (tiles - 1) - nz - 2 * hz
+    direct = slabs == 2 and tiles > 1 and pad == 0 and nz % LANES == 0 and hz == LAP and cx % 2 == 0
     sx, sy = lax.axis_index("sx"), lax.axis_index("sy")
     place = jnp.stack([sx, sy]).astype(jnp.int32)
 
@@ -518,13 +549,17 @@
             cost_estimate=pl.CostEstimate(flops=flops, bytes_accessed=moved, transcendentals=0),
         )(*args)
 
+    def lanes_first(value):
+        parts = jnp.stack([value[STEP * t : STEP * t + LANES] for t in range(tiles)])
+        return parts.transpose(0, 2, 3, 1)
+
     rounds_y = swaps(lax.axis_size("sy"))
     if direct:
-        volume = observed.reshape(-1, LANES, cx, cy).transpose(0, 2, 3, 1)
+        volume = lanes_first(jnp.pad(observed, ((hz, hz), (0, 0), (0, 0))))
         zone_rows = jnp.pad(zones.reshape(-1, LANES), ((0, 8 - nz // LANES), (0, 0)))
         edge, edge_z = shape(volume.shape[0], cx * hy, LANES), shape(cx * hy, LANES)
         first, second, first_z, second_z, borders = call(
-            functools.partial(edges_kernel, hy, hz), [edge, edge, edge_z, edge_z, shape(cx // 2 * cy + 8, LANES)],
+            functools.partial(edges_kernel, hy, hz, nz - STEP * (tiles - 1)), [edge, edge, edge_z, edge_z, shape(cx // 2 * cy + 8, LANES)],
             (place, volume, zone_rows), [], 8, 1, scalars=1,
         )
         borders = lax.ppermute(borders, "gz", [(0, 1), (1, 0)])
@@ -546,11 +581,10 @@
         second = lax.ppermute(with_zones(observed[:hz], zones[:hz]), "gz", [(j, i) for i, j in ring])
         before, after = first[:hz], second[:hz]
         ids_before, ids_after = first[hz].reshape(-1)[:hz], second[hz].reshape(-1)[:hz]
-        volume = jnp.concatenate([before, observed, after, jnp.zeros((pad, cx, cy), f32)], axis=0)
-        volume = volume.reshape(spans, LANES, cx, cy).transpose(0, 2, 3, 1)
-        edge = shape(spans, cx * hy, LANES)
+        volume = lanes_first(jnp.concatenate([before, observed, after, jnp.zeros((pad, cx, cy), f32)], axis=0))
+        edge = shape(tiles, cx * hy, LANES)
         first, second = call(
-            functools.partial(edges_kernel, hy, hz), [edge, edge], (place, volume), [], 8, 1, scalars=1
+            functools.partial(edges_kernel, hy, hz, nz - STEP * (tiles - 1)), [edge, edge], (place, volume), [], 8, 1, scalars=1
         )
         parts = [volume, lax.ppermute(first, "sy", both_ways(rounds_y[0])), lax.ppermute(second, "sy", both_ways(rounds_y[1]))]
     ids = jnp.concatenate([ids_before, zones, ids_after, jnp.full((pad,), -1.0, f32)])
@@ -568,8 +602,8 @@
     tx_own, ty_own = lanes_of(lateral_x, own_ids), lanes_of(lateral_y, own_ids)
 
     wide = cx + 2 * reach
-    packed = LANES + STEP * (tiles - 1) - (spans - 1) * LANES <= LANES // 2
-    planes = hx * (spans - 1) + hx // 2 if packed else hx * spans
+    packed = tiles == 3
+    planes = 2 * hx + hx // 2 if packed else hx * tiles
     end0, end1, end2 = cy + 2 * hy, cy + 2 * hy - 4 * reach, cy
     mid1 = ceil_to(end1 // 2, 8) + 8
     mid2 = mid1 - ceil_to(4 * reach, 8)
@@ -594,8 +628,13 @@
     halo_a = swap(pays[:2])
     halo_b = swap(pays[2:])
 
-    forward, back = call(
-        band_kernel, [jax.ShapeDtypeStruct((2 * LANES, 2 * LANES), jnp.bfloat16)] * 2,
+    overlap = tuple(STEP * t for t in range(tiles))
+    alone = tuple(hz + LANES * t for t in range(own))
+    pairs = own_pairs(tiles, alone)
+    forward, back, ends, back_own = call(
+        functools.partial(band_kernel, pairs, alone),
+        [jax.ShapeDtypeStruct((2 * LANES, 2 * LANES), jnp.bfloat16)] * 3
+        + [jax.ShapeDtypeStruct((len(pairs), 2 * LANES, 2 * LANES), jnp.bfloat16)],
         (depth_psf, pays[-1]), [], 8, 1, scalars=1, unread=(1,),
     )
     stacks_x, stacks_y = stitch_width.shape[:2]
@@ -606,15 +645,14 @@
     )
     shift = 2 * reach
 
-    overlap = tuple(STEP * t for t in range(tiles))
-    alone = tuple(hz + LANES * t for t in range(own))
+    mats = {overlap: (forward, back, ends), alone: (forward, back_own)}
 
     def inner(est, data_off, starts, rows, need):
         plan = dict(data_off=data_off, starts=starts, need=need)
         rows = ceil_to(rows, 8)
         return call(
             functools.partial(inner_kernel, plan), [shape(len(starts), cx - shift, rows, LANES)],
-            (est, ext, weight, tx, ty, forward, back), [(tiles, cx - shift, rows + 16, LANES)], 24, 1,
+            (est, ext, weight, tx, ty, *mats[starts]), [(tiles, cx - shift, rows + 16, LANES)], 24, 1,
         )[0]
 
     def outer(est, halos, extra, inner_part, last, plan, outs):
@@ -622,10 +660,10 @@
         lateral = (tx_own, ty_own) if last else (tx, ty)
         starts = alone if last else overlap
         args = (place, est) + tuple(h for _, pair in halos for h in pair) + extra
-        args += (inner_part, inv, tx, ty) + lateral + (forward, back)
+        args += (inner_part, inv, tx, ty) + lateral + mats[starts]
         plan = dict(
             plan, hx=hx, packed=packed, halos=[rng for rng, _ in halos], make_data=not last, pay=not last,
-            starts=starts, data_off=shift if last else 0,
+            starts=starts, mats=len(mats[starts]), data_off=shift if last else 0,
         )
         scratch = [(tiles, cx, rows + 16, LANES), (len(starts), 2 * hx, rows, LANES)]
         return call(functools.partial(outer_kernel, plan), outs, args, scratch, 16, 1, scalars=1)

time: 109 us -> 105 us (0.963)
  Pallas kernels: 56.7 us -> 51.2 us
  local copies, waits for them, and re-layouts: 4.61 us -> 8.6 us
  waiting for transfers between devices: 24 us -> 21.2 us
    pallas_call x10, Pallas kernels: 56.7 us -> 51.2 us  [call(): pl.pallas_call(kernel, out_shape=out_shape, in_specs=[pl.BlockSpec(memory...]
    unnamed x13 -> x18, local copies, waits for them, and re-layouts: 0.3 us -> 3.52 us
    ppermute x2, waiting for transfers between devices: 8.71 us -> 6.18 us  [body(): parts.append(lax.ppermute(value, ('sy', 'gz'), both_ways(cross)))]
    reshape x1 -> x0, local copies, waits for them, and re-layouts: 1.99 us -> none  [body(): volume = observed.reshape(-1, LANES, cx, cy).transpose(0, 2, 3, 1)]
  transfers between devices with their start and end apart: 13 -> 13, of which waited for: 4 -> 5; matrix products, arithmetic and copies ran while one was open for 1% -> 4% of each run, Pallas kernels for 36% -> 36%
where the time goes in v7:
time: 105 us; the launch traced here: 104 us
  Pallas kernels  51.2 us (49%)
  starting transfers between devices  21.5 us (20%)
  waiting for transfers between devices  21.2 us (20%)
  local copies, waits for them, and re-layouts  8.6 us (8%)
    pallas_call x10, Pallas kernels, call(): pl.pallas_call(kernel, out_shape=out_shape, in_specs=[pl.BlockSpec(memory...  51.2 us
    ppermute x8, waiting for transfers between devices, swap(): got.append(lax.ppermute(pays[n], 'sx', rounds_x[n]))  15 us
    ppermute x8, starting transfers between devices, swap(): got.append(lax.ppermute(pays[n], 'sx', rounds_x[n]))  14.4 us
    ppermute x2, waiting for transfers between devices, body(): parts.append(lax.ppermute(value, ('sy', 'gz'), both_ways(cross)))  6.18 us
    unnamed x18, local copies, waits for them, and re-layouts  3.52 us
    ppermute x2, starting transfers between devices, body(): parts.append(lax.ppermute(value, ('sy', 'gz'), both_ways(cross)))  3.02 us
    ppermute x1, starting transfers between devices, body(): lax.ppermute(second, 'sy', both_ways(rounds_y[1]))  2.54 us
  transfers between devices with their start and end apart: 13, of which 5 were waited for; matrix products, arithmetic and copies ran while one was open for 4% of the time, Pallas kernels for 36%

profile of v7, /device:TPU:10, one launch (start us, length us, event | category | flops | bytes accessed | tf_op | source)
XLA Modules:
  0.0 103.6 jit_solution(10671302150768366881)
XLA Ops:
  0.0 1.9 %copy.26 = f32[256,16,128]{0,2,1:T(8,128)S(1)} copy(f32[256,16,128]{2,1,0:T(8,128)} %param.6) | data formatting | bytes 4194304 | tf_op args[0]
  3.3 2.5 %shard_map.64 = (f32[3,192,128]{2,1,0:T(8,128)}, f32[3,192,128]{2,1,0:T(8,128)}, f32[192,128]{1,0:T(8,128)}, f32[192,128]{1,0:T(8,128)}, f32[1032,128]{1,0:T(8,128)}) custom-call(s32[2]{0:T(128)S(1)} %pad_add_fusion.place_ref, f32[3,16,128,128]{3,2,1,0:T(8,128)S(1)} %maximum_bitcast_fusion.vol_ref.refs_0_, f32[8,128]{1,0:T(8,128)S(1)} %pad.9.refs_0_), custom_call_target="tpu_custom_call" | custom-call | flops 1 | bytes 4464648 | tf_op jit(solution)/shard_map/pallas_call | solution.py:542
  5.8 1.5 %collective-permute-start.2 = (f32[1032,128]{1,0:T(8,128)}, f32[1032,128]{1,0:T(8,128)}, u32[]{:S(2)}, u32[]{:S(2)}) collective-permute-start(f32[1032,128]{1,0:T(8,128)} %get-tuple-element.31), channel_id=1, source_target_pairs={{0,1},{1,0},{2,3},{3,2},{4,5},{5,4},{6,7},{7,6},{8,9},{9,8},{10,11... | collective-permute-start | bytes 1585160 | tf_op jit(solution)/shard_map/ppermute | solution.py:565
  7.3 2.5 %collective-permute-start.1 = (f32[3,192,128]{2,1,0:T(8,128)}, f32[3,192,128]{2,1,0:T(8,128)}, u32[]{:S(2)}, u32[]{:S(2)}) collective-permute-start(f32[3,192,128]{2,1,0:T(8,128)} %get-tuple-element.30), channel_id=1, source_target_pairs={{2,4},{4,2},{3,5},{5,3},{10,12},{12,10},{11,13},{13,11},{18,20},{2... | collective-permute-start | bytes 884744 | tf_op jit(solution)/shard_map/ppermute | solution.py:566
  9.9 3.0 %collective-permute-start.4 = (f32[192,128]{1,0:T(8,128)}, f32[192,128]{1,0:T(8,128)}, u32[]{:S(2)}, u32[]{:S(2)}) collective-permute-start(f32[192,128]{1,0:T(8,128)} %get-tuple-element.33), channel_id=1, source_target_pairs={{2,5},{3,4},{5,2},{4,3},{10,13},{11,12},{13,10},{12,11},{18,21},{1... | collective-permute-start | bytes 294920 | tf_op jit(solution)/shard_map/ppermute | solution.py:570
  15.9 6.2 %collective-permute-done.3.refs_4_ = f32[192,128]{1,0:T(8,128)S(1)} collective-permute-done((f32[192,128]{1,0:T(8,128)}, f32[192,128]{1,0:T(8,128)S(1)}, u32[]{:S(2)}, u32[]{:S(2)}) %collective-permute-start.3) | collective-permute-done | bytes 98336 | tf_op jit(solution)/shard_map/ppermute | solution.py:570
  22.1 4.6 %shard_map.65 = (f32[3,16,160,128]{3,2,1,0:T(8,128)S(1)}, f32[15,96,128]{2,1,0:T(8,128)S(1)}, f32[15,96,128]{2,1,0:T(8,128)S(1)}, f32[15,56,128]{2,1,0:T(8,128)S(1)}, f32[15,56,128]{2,1,0:T(8,128)S(1)}) custom-call(s32[2]{0:T(128)S(1)} %pad_add_fusion.place_ref, f32[3,16,128,128]{3,2,1,0:T(8,128)S(1)} %maximum_bitcast_fusion.vol_ref.refs_0_, ...), custom_call_target="tpu_custom_call" | custom-call | flops 1 | bytes 10727432 | tf_op jit(solution)/shard_map/pallas_call | solution.py:542
  26.7 3.5 %collective-permute-start.8 = (f32[15,56,128]{2,1,0:T(8,128)S(1)}, f32[15,56,128]{2,1,0:T(8,128)S(1)}, u32[]{:S(2)}, u32[]{:S(2)}) collective-permute-start(f32[15,56,128]{2,1,0:T(8,128)S(1)} %get-tuple-element.38._), channel_id=1, source_target_pairs={{8,16},{16,8},{9,17},{17,9},{10,18},{18,10},{11,19},{19,11},{12,20... | collective-permute-start | bytes 1290248 | tf_op jit(solution)/shard_map/ppermute | solution.py:620
  30.2 1.2 %shard_map.67 = (bf16[256,256]{1,0:T(8,128)(2,1)S(1)}, bf16[256,256]{1,0:T(8,128)(2,1)S(1)}, bf16[256,256]{1,0:T(8,128)(2,1)S(1)}, bf16[4,256,256]{2,1,0:T(8,128)(2,1)S(1)}) custom-call(f32[17]{0:T(128)S(1)} %copy-done, f32[15,56,128]{2,1,0:T(8,128)S(1)} %get-tuple-element.38._), custom_call_target="tpu_custom_call" | custom-call | flops 1 | bytes 2265156 | tf_op jit(solution)/shard_map/pallas_call | solution.py:542
  31.5 2.4 %collective-permute-start.6 = (f32[15,96,128]{2,1,0:T(8,128)S(1)}, f32[15,96,128]{2,1,0:T(8,128)S(1)}, u32[]{:S(2)}, u32[]{:S(2)}) collective-permute-start(f32[15,96,128]{2,1,0:T(8,128)S(1)} %get-tuple-element.36), channel_id=1, source_target_pairs={{8,16},{16,8},{9,17},{17,9},{10,18},{18,10},{11,19},{19,11},{12,20... | collective-permute-start | bytes 2211848 | tf_op jit(solution)/shard_map/ppermute | solution.py:620
  35.3 4.9 %shard_map.66 = (f32[22,160,128]{2,1,0:T(8,128)S(1)}, f32[3,16,144,128]{3,2,1,0:T(8,128)S(1)}) custom-call(s32[2]{0:T(128)S(1)} %pad_add_fusion.place_ref, s32[32]{0:T(128)S(1)} %reshape.62.bands_ref, f32[15,56,128]{2,1,0:T(8,128)S(1)} %get-tuple-element.38._, f32[3,7,8,128]{3,2,1,0:T(8,128)S(1)} %broadcast_in_dim.17.tx_ref.refs_6_.refs_8_.refs_9_.refs_11_, ...), custom_call_target="tpu_custom_call" | custom-call | flops 1 | bytes 5943432 | tf_op jit(solution)/shard_map/pallas_call | solution.py:542
  40.1 4.6 %shard_map.68.refs_4_.refs_7_ = f32[3,10,152,128]{3,2,1,0:T(8,128)S(1)} custom-call(f32[3,16,160,128]{3,2,1,0:T(8,128)S(1)} %get-tuple-element.34.est_ref.obs_ref.refs_0_, f32[3,16,160,128]{3,2,1,0:T(8,128)S(1)} %get-tuple-element.34.est_ref.obs_ref.refs_0_, f32[22,160,128]{2,1,0:T(8,128)S(1)} %get-tuple-element.39.w_ref.refs_3_.refs_5_, ...), custom_call_target="tpu_custom_call" | custom-call | flops 1 | bytes 12959744 | tf_op jit(solution)/shard_map/pallas_call | solution.py:542
  44.8 6.0 %collective-permute-done.5.refs_1_ = f32[15,96,128]{2,1,0:T(8,128)S(1)} collective-permute-done((f32[15,96,128]{2,1,0:T(8,128)S(1)}, f32[15,96,128]{2,1,0:T(8,128)S(1)}, u32[]{:S(2)}, u32[]{:S(2)}) %collective-permute-start.5) | collective-permute-done | bytes 737312 | tf_op jit(solution)/shard_map/ppermute | solution.py:620
  50.8 6.0 %collective-permute-done.6.refs_2_ = f32[15,96,128]{2,1,0:T(8,128)S(1)} collective-permute-done((f32[15,96,128]{2,1,0:T(8,128)S(1)}, f32[15,96,128]{2,1,0:T(8,128)S(1)}, u32[]{:S(2)}, u32[]{:S(2)}) %collective-permute-start.6) | collective-permute-done | bytes 737312 | tf_op jit(solution)/shard_map/ppermute | solution.py:620
  56.8 8.4 %shard_map.69 = (f32[3,16,80,128]{3,2,1,0:T(8,128)S(1)}, f32[3,12,96,128]{3,2,1,0:T(8,128)S(1)}, f32[15,80,128]{2,1,0:T(8,128)S(1)}, f32[15,80,128]{2,1,0:T(8,128)S(1)}) custom-call(s32[2]{0:T(128)S(1)} %pad_add_fusion.place_ref, f32[3,16,160,128]{3,2,1,0:T(8,128)S(1)} %get-tuple-element.34.est_ref.obs_ref.refs_0_, ...), custom_call_target="tpu_custom_call" | custom-call | flops 1 | bytes 19177480 | tf_op jit(solution)/shard_map/pallas_call | solution.py:542
  65.3 3.5 %collective-permute-start.10 = (f32[15,80,128]{2,1,0:T(8,128)S(1)}, f32[15,80,128]{2,1,0:T(8,128)S(1)}, u32[]{:S(2)}, u32[]{:S(2)}) collective-permute-start(f32[15,80,128]{2,1,0:T(8,128)S(1)} %get-tuple-element.47), channel_id=1, source_target_pairs={{8,16},{16,8},{9,17},{17,9},{10,18},{18,10},{11,19},{19,11},{12,20... | collective-permute-start | bytes 1843208 | tf_op jit(solution)/shard_map/ppermute | solution.py:620
  68.9 7.3 %shard_map.70 = (f32[3,16,144,128]{3,2,1,0:T(8,128)S(1)}, f32[3,12,88,128]{3,2,1,0:T(8,128)S(1)}, f32[15,64,128]{2,1,0:T(8,128)S(1)}, f32[15,64,128]{2,1,0:T(8,128)S(1)}) custom-call(s32[2]{0:T(128)S(1)} %pad_add_fusion.place_ref, f32[3,16,160,128]{3,2,1,0:T(8,128)S(1)} %get-tuple-element.34.est_ref.obs_ref.refs_0_, ...), custom_call_target="tpu_custom_call" | custom-call | flops 1 | bytes 23183368 | tf_op jit(solution)/shard_map/pallas_call | solution.py:542
  76.2 2.0 %collective-permute-start.11 = (f32[15,64,128]{2,1,0:T(8,128)S(1)}, f32[15,64,128]{2,1,0:T(8,128)S(1)}, u32[]{:S(2)}, u32[]{:S(2)}) collective-permute-start(f32[15,64,128]{2,1,0:T(8,128)S(1)} %get-tuple-element.50), channel_id=1, source_target_pairs={{0,8},{16,24},{8,0},{24,16},{1,9},{17,25},{9,1},{25,17},{2,10},{18... | collective-permute-start | bytes 1474568 | tf_op jit(solution)/shard_map/ppermute | solution.py:620
  78.2 2.5 %collective-permute-start.12 = (f32[15,64,128]{2,1,0:T(8,128)S(1)}, f32[15,64,128]{2,1,0:T(8,128)S(1)}, u32[]{:S(2)}, u32[]{:S(2)}) collective-permute-start(f32[15,64,128]{2,1,0:T(8,128)S(1)} %get-tuple-element.51), channel_id=1, source_target_pairs={{8,16},{16,8},{9,17},{17,9},{10,18},{18,10},{11,19},{19,11},{12,20... | collective-permute-start | bytes 1474568 | tf_op jit(solution)/shard_map/ppermute | solution.py:620
  80.9 4.1 %shard_map.71.refs_4_.refs_6_ = f32[2,10,136,128]{3,2,1,0:T(8,128)S(1)} custom-call(f32[3,16,144,128]{3,2,1,0:T(8,128)S(1)} %get-tuple-element.45.est_ref.refs_0_, f32[3,16,160,128]{3,2,1,0:T(8,128)S(1)} %get-tuple-element.34.est_ref.obs_ref.refs_0_, f32[22,160,128]{2,1,0:T(8,128)S(1)} %get-tuple-element.39.w_ref.refs_3_.refs_5_, ...), custom_call_target="tpu_custom_call" | custom-call | flops 1 | bytes 12148736 | tf_op jit(solution)/shard_map/pallas_call | solution.py:542
  85.6 6.8 %shard_map.72 = f32[2,16,64,128]{3,2,1,0:T(8,128)S(1)} custom-call(s32[2]{0:T(128)S(1)} %pad_add_fusion.place_ref, f32[3,16,144,128]{3,2,1,0:T(8,128)S(1)} %get-tuple-element.45.est_ref.refs_0_, f32[15,80,128]{2,1,0:T(8,128)S(1)} %collective-permute-done.9.refs_1_, f32[15,80,128]{2,1,0:T(8,128)S(1)} %collective-permute-done.10.refs_2_, ...), custom_call_target="tpu_custom_call" | custom-call | flops 1 | bytes 14114824 | tf_op jit(solution)/shard_map/pallas_call | solution.py:542
  92.4 2.3 %collective-permute-done.11.refs_3_ = f32[15,64,128]{2,1,0:T(8,128)S(1)} collective-permute-done((f32[15,64,128]{2,1,0:T(8,128)S(1)}, f32[15,64,128]{2,1,0:T(8,128)S(1)}, u32[]{:S(2)}, u32[]{:S(2)}) %collective-permute-start.11) | collective-permute-done | bytes 491552 | tf_op jit(solution)/shard_map/ppermute | solution.py:620
  94.7 6.8 %shard_map.73 = f32[2,16,64,128]{3,2,1,0:T(8,128)S(1)} custom-call(s32[2]{0:T(128)S(1)} %pad_add_fusion.place_ref, f32[3,16,144,128]{3,2,1,0:T(8,128)S(1)} %get-tuple-element.45.est_ref.refs_0_, f32[15,80,128]{2,1,0:T(8,128)S(1)} %collective-permute-done.9.refs_1_, f32[15,80,128]{2,1,0:T(8,128)S(1)} %collective-permute-done.10.refs_2_, ...), custom_call_target="tpu_custom_call" | custom-call | flops 1 | bytes 14950408 | tf_op jit(solution)/shard_map/pallas_call | solution.py:542
  101.7 2.0 %copy.35 = f32[2,128,16,128]{3,2,1,0:T(8,128)} copy(f32[2,128,16,128]{1,3,2,0:T(8,128)S(1)} %maximum_bitcast_fusion.1) | data formatting | bytes 4194304 | tf_op jit(solution)/shard_map/transpose | solution.py:695
  (53 shorter events, 6.8 us)
Async XLA Ops:
  1.9 0.9 copy-start.5
  2.8 10.1 %copy-start.1 = (f32[256]{0:T(256)}, f32[256]{0:T(256)S(1)}, u32[]{:S(2)}) copy-start(f32[256]{0:T(256)S(1)} %get-tuple-element.64) | copy-start | bytes 3076
  3.3 10.2 %copy-start.4 = (f32[8,7]{1,0:T(8,128)S(1)}, f32[8,7]{1,0:T(8,128)}, u32[]{:S(2)}) copy-start(f32[8,7]{1,0:T(8,128)} %param.8) | copy-start | bytes 676
  3.3 11.1 %copy-start.3 = (s32[4,4,2]{1,2,0:T(2,128)S(1)}, s32[4,4,2]{1,2,0:T(2,128)}, u32[]{:S(2)}) copy-start(s32[4,4,2]{1,2,0:T(2,128)} %param.11) | copy-start | bytes 388
  5.8 16.3 %collective-permute-start.2 = (f32[1032,128]{1,0:T(8,128)}, f32[1032,128]{1,0:T(8,128)}, u32[]{:S(2)}, u32[]{:S(2)}) collective-permute-start(f32[1032,128]{1,0:T(8,128)} %get-tuple-element.31), channel_id=1, source_target_pairs={{0,1},{1,0},{2,3},{3,2},{4,5},{5,4},{6,7},{7,6},{8,9},{9,8},{10,11... | collective-permute-start | bytes 1585160 | tf_op jit(solution)/shard_map/ppermute | solution.py:565
  7.3 14.8 %collective-permute-start = (f32[3,192,128]{2,1,0:T(8,128)}, f32[3,192,128]{2,1,0:T(8,128)S(1)}, u32[]{:S(2)}, u32[]{:S(2)}) collective-permute-start(f32[3,192,128]{2,1,0:T(8,128)} %get-tuple-element.29), channel_id=1, source_target_pairs={{0,2},{4,6},{2,0},{6,4},{1,3},{5,7},{3,1},{7,5},{8,10},{12,14},{10... | collective-permute-start | bytes 884744 | tf_op jit(solution)/shard_map/ppermute | solution.py:566
  7.3 14.8 %collective-permute-start.1 = (f32[3,192,128]{2,1,0:T(8,128)}, f32[3,192,128]{2,1,0:T(8,128)}, u32[]{:S(2)}, u32[]{:S(2)}) collective-permute-start(f32[3,192,128]{2,1,0:T(8,128)} %get-tuple-element.30), channel_id=1, source_target_pairs={{2,4},{4,2},{3,5},{5,3},{10,12},{12,10},{11,13},{13,11},{18,20},{2... | collective-permute-start | bytes 884744 | tf_op jit(solution)/shard_map/ppermute | solution.py:566
  9.9 12.2 %collective-permute-start.3 = (f32[192,128]{1,0:T(8,128)}, f32[192,128]{1,0:T(8,128)S(1)}, u32[]{:S(2)}, u32[]{:S(2)}) collective-permute-start(f32[192,128]{1,0:T(8,128)} %get-tuple-element.32), channel_id=1, source_target_pairs={{0,3},{1,2},{4,7},{5,6},{3,0},{2,1},{7,4},{6,5},{8,11},{9,10},{12,... | collective-permute-start | bytes 294920 | tf_op jit(solution)/shard_map/ppermute | solution.py:570
  9.9 12.1 %collective-permute-start.4 = (f32[192,128]{1,0:T(8,128)}, f32[192,128]{1,0:T(8,128)}, u32[]{:S(2)}, u32[]{:S(2)}) collective-permute-start(f32[192,128]{1,0:T(8,128)} %get-tuple-element.33), channel_id=1, source_target_pairs={{2,5},{3,4},{5,2},{4,3},{10,13},{11,12},{13,10},{12,11},{18,21},{1... | collective-permute-start | bytes 294920 | tf_op jit(solution)/shard_map/ppermute | solution.py:570
  15.8 14.3 %copy-start = (f32[17]{0:T(128)S(1)}, f32[17]{0:T(128)}, u32[]{:S(2)}) copy-start(f32[17]{0:T(128)} %psf_ref.1) | copy-start | bytes 208
  15.8 18.7 %copy-start.2 = (f32[256]{0:T(256)S(1)}, f32[256]{0:T(256)}, u32[]{:S(2)}) copy-start(f32[256]{0:T(256)} %copy-done.1) | copy-start | bytes 3076
  15.9 19.2 %copy-start.6 = (f32[128]{0:T(128)S(1)}, f32[128]{0:T(128)}, u32[]{:S(2)}) copy-start(f32[128]{0:T(128)} %slice.42) | copy-start | bytes 1540
  26.7 42.2 %collective-permute-start.8 = (f32[15,56,128]{2,1,0:T(8,128)S(1)}, f32[15,56,128]{2,1,0:T(8,128)S(1)}, u32[]{:S(2)}, u32[]{:S(2)}) collective-permute-start(f32[15,56,128]{2,1,0:T(8,128)S(1)} %get-tuple-element.38._), channel_id=1, source_target_pairs={{8,16},{16,8},{9,17},{17,9},{10,18},{18,10},{11,19},{19,11},{12,20... | collective-permute-start | bytes 1290248 | tf_op jit(solution)/shard_map/ppermute | solution.py:620
  31.4 19.4 %collective-permute-start.5 = (f32[15,96,128]{2,1,0:T(8,128)S(1)}, f32[15,96,128]{2,1,0:T(8,128)S(1)}, u32[]{:S(2)}, u32[]{:S(2)}) collective-permute-start(f32[15,96,128]{2,1,0:T(8,128)S(1)} %get-tuple-element.35), channel_id=1, source_target_pairs={{0,8},{16,24},{8,0},{24,16},{1,9},{17,25},{9,1},{25,17},{2,10},{18... | collective-permute-start | bytes 2211848 | tf_op jit(solution)/shard_map/ppermute | solution.py:620
  31.5 25.4 %collective-permute-start.6 = (f32[15,96,128]{2,1,0:T(8,128)S(1)}, f32[15,96,128]{2,1,0:T(8,128)S(1)}, u32[]{:S(2)}, u32[]{:S(2)}) collective-permute-start(f32[15,96,128]{2,1,0:T(8,128)S(1)} %get-tuple-element.36), channel_id=1, source_target_pairs={{8,16},{16,8},{9,17},{17,9},{10,18},{18,10},{11,19},{19,11},{12,20... | collective-permute-start | bytes 2211848 | tf_op jit(solution)/shard_map/ppermute | solution.py:620
  34.7 34.1 %collective-permute-start.7 = (f32[15,56,128]{2,1,0:T(8,128)S(1)}, f32[15,56,128]{2,1,0:T(8,128)S(1)}, u32[]{:S(2)}, u32[]{:S(2)}) collective-permute-start(f32[15,56,128]{2,1,0:T(8,128)S(1)} %get-tuple-element.37), channel_id=1, source_target_pairs={{0,8},{16,24},{8,0},{24,16},{1,9},{17,25},{9,1},{25,17},{2,10},{18... | collective-permute-start | bytes 1290248 | tf_op jit(solution)/shard_map/ppermute | solution.py:620
  65.3 19.7 %collective-permute-start.10 = (f32[15,80,128]{2,1,0:T(8,128)S(1)}, f32[15,80,128]{2,1,0:T(8,128)S(1)}, u32[]{:S(2)}, u32[]{:S(2)}) collective-permute-start(f32[15,80,128]{2,1,0:T(8,128)S(1)} %get-tuple-element.47), channel_id=1, source_target_pairs={{8,16},{16,8},{9,17},{17,9},{10,18},{18,10},{11,19},{19,11},{12,20... | collective-permute-start | bytes 1843208 | tf_op jit(solution)/shard_map/ppermute | solution.py:620
  68.8 16.8 %collective-permute-start.9 = (f32[15,80,128]{2,1,0:T(8,128)S(1)}, f32[15,80,128]{2,1,0:T(8,128)S(1)}, u32[]{:S(2)}, u32[]{:S(2)}) collective-permute-start(f32[15,80,128]{2,1,0:T(8,128)S(1)} %get-tuple-element.46), channel_id=1, source_target_pairs={{0,8},{16,24},{8,0},{24,16},{1,9},{17,25},{9,1},{25,17},{2,10},{18... | collective-permute-start | bytes 1843208 | tf_op jit(solution)/shard_map/ppermute | solution.py:620
  76.2 18.5 %collective-permute-start.11 = (f32[15,64,128]{2,1,0:T(8,128)S(1)}, f32[15,64,128]{2,1,0:T(8,128)S(1)}, u32[]{:S(2)}, u32[]{:S(2)}) collective-permute-start(f32[15,64,128]{2,1,0:T(8,128)S(1)} %get-tuple-element.50), channel_id=1, source_target_pairs={{0,8},{16,24},{8,0},{24,16},{1,9},{17,25},{9,1},{25,17},{2,10},{18... | collective-permute-start | bytes 1474568 | tf_op jit(solution)/shard_map/ppermute | solution.py:620
  78.2 16.5 %collective-permute-start.12 = (f32[15,64,128]{2,1,0:T(8,128)S(1)}, f32[15,64,128]{2,1,0:T(8,128)S(1)}, u32[]{:S(2)}, u32[]{:S(2)}) collective-permute-start(f32[15,64,128]{2,1,0:T(8,128)S(1)} %get-tuple-element.51), channel_id=1, source_target_pairs={{8,16},{16,8},{9,17},{17,9},{10,18},{18,10},{11,19},{19,11},{12,20... | collective-permute-start | bytes 1474568 | tf_op jit(solution)/shard_map/ppermute | solution.py:620

commit v8 on v7

--- a/solution.py
+++ b/solution.py
@@ -238,7 +238,7 @@
         seen = obs_ref[t, pl.ds(x + reach, group), first : first + rows, :]
         return (seen * w_ref[pl.ds(x + 2 * reach, group), first : first + rows, :]).reshape(group * rows, LANES)
 
-    correct(mid_ref, ty_ref, mats, plan["starts"], 2, count, rows, data_of, spread_ref)
+    correct(mid_ref, ty_ref, mats, plan["starts"], 10, count, rows, data_of, spread_ref)
 
 
 def norm_kernel(plan, place_ref, bands_ref, _, tx_ref, ty_ref, w_ref, out_ref, mid_ref):
@@ -347,6 +347,7 @@
     else:
         first_ref, second_ref = refs
     lane = lax.broadcasted_iota(jnp.int32, (hy, LANES), 1)
+    kept = []
     for x in range(cx):
         to = slice(hy * x, hy * x + hy)
         both = []
@@ -355,8 +356,11 @@
             both.append((jnp.where(odd == 1, low, high), jnp.where(odd == 1, high, low)))
             first_ref[t, to, :], second_ref[t, to, :] = both[-1]
         if direct:
-            for n, ref in enumerate((first_z, second_z)):
-                ref[to, :] = outmost(both[0][n], both[-1][n], lane)
+            kept.append([outmost(both[0][n], both[-1][n], lane) for n in range(2)])
+            if x >= half:
+                to = slice(hy * (x - half), hy * (x - half) + hy)
+                for n, ref in enumerate((first_z, second_z)):
+                    ref[to, :] = jnp.where(lane < LANES // 2, kept[x - half][n], spin(kept[x][n], LANES // 2))
 
 
 def assemble_kernel(packed, hx, cut, shift, refs_in, place_ref, *refs):
@@ -375,9 +379,10 @@
         low, high = zip(*[by_side(odd, first_ref[t, edge, :], second_ref[t, edge, :]) for t in range(main)])
         mids = [vol_ref[t, x] for t in range(main)]
         if depth_ref is not None:
-            low_z, high_z = by_side(odd, first_z[edge, :], second_z[edge, :])
-            low = with_halo(low, low_z, spin(low_z, LANES // 2), shift)
-            high = with_halo(high, high_z, spin(high_z, LANES // 2), shift)
+            edge_z = slice(hy * (x % half), hy * (x % half) + hy)
+            low_z, high_z = [(z, spin(z, LANES // 2)) for z in by_side(odd, first_z[edge_z, :], second_z[edge_z, :])]
+            low = with_halo(low, *(low_z if x < half else low_z[::-1]), shift)
+            high = with_halo(high, *(high_z if x < half else high_z[::-1]), shift)
             halo = depth_ref[cy * (x % half) : cy * (x % half) + cy, :]
             pair = (halo, spin(halo, LANES // 2))
             mids = with_halo(mids, *(pair if x < half else pair[::-1]), shift)
@@ -386,10 +391,11 @@
             ext_ref[t, x, hy : hy + cy, :] = mids[t]
             ext_ref[t, x, hy + cy : end, :] = high[t]
             ext_ref[t, x, end:, :] = jnp.zeros((ext_ref.shape[2] - end, LANES), jnp.float32)
-    odd_x = place_ref[0] % 2
-    for n in range(2):
-        start, stop = (0, cut) if n == 0 else (cut, end)
-        pack_both(ext_ref, pays[2 * n : 2 * n + 2], odd_x, packed, hx, -(-(stop - start) // 8), start // 8)
+    pack_both(ext_ref, pays, place_ref[0] % 2, packed, hx, -(-cut // 8), 0)
+
+
+def pack_kernel(packed, hx, first, stop, place_ref, ext_ref, *pays):
+    pack_both(ext_ref, pays, place_ref[0] % 2, packed, hx, -(-(stop - first) // 8), first // 8)
 
 
 def outer_kernel(plan, place_ref, *refs):
@@ -466,7 +472,7 @@
     def data_of(t, x, group):
         return data_ref[t, pl.ds(x, group), spot0 : spot0 + rows, :].reshape(group * rows, LANES)
 
-    correct(mid_ref, ty_ref, mats, starts, 6, 2 * hx, rows, data_of, edge_ref)
+    correct(mid_ref, ty_ref, mats, starts, 12, 2 * hx, rows, data_of, edge_ref)
 
     blocks = -(-(high - low) // 8)
 
@@ -557,7 +563,7 @@
     if direct:
         volume = lanes_first(jnp.pad(observed, ((hz, hz), (0, 0), (0, 0))))
         zone_rows = jnp.pad(zones.reshape(-1, LANES), ((0, 8 - nz // LANES), (0, 0)))
-        edge, edge_z = shape(volume.shape[0], cx * hy, LANES), shape(cx * hy, LANES)
+        edge, edge_z = shape(volume.shape[0], cx * hy, LANES), shape(cx // 2 * hy, LANES)
         first, second, first_z, second_z, borders = call(
             functools.partial(edges_kernel, hy, hz, nz - STEP * (tiles - 1)), [edge, edge, edge_z, edge_z, shape(cx // 2 * cy + 8, LANES)],
             (place, volume, zone_rows), [], 8, 1, scalars=1,
@@ -622,11 +628,13 @@
 
     ext, *pays = call(
         functools.partial(assemble_kernel, packed, hx, cut, hz, len(parts)),
-        [shape(tiles, cx, full, LANES)] + pay_shapes(cut) + pay_shapes(end0 - cut),
+        [shape(tiles, cx, full, LANES)] + pay_shapes(cut),
         (place, *parts), [], 8, 1, scalars=1,
     )
-    halo_a = swap(pays[:2])
-    halo_b = swap(pays[2:])
+    halo_a = swap(pays)
+    pack = functools.partial(pack_kernel, packed, hx, cut, end0)
+    rest = call(pack, pay_shapes(end0 - cut), (place, ext), [], 8, 1, scalars=1)
+    halo_b = swap(rest)
 
     overlap = tuple(STEP * t for t in range(tiles))
     alone = tuple(hz + LANES * t for t in range(own))
@@ -635,13 +643,13 @@
         functools.partial(band_kernel, pairs, alone),
         [jax.ShapeDtypeStruct((2 * LANES, 2 * LANES), jnp.bfloat16)] * 3
         + [jax.ShapeDtypeStruct((len(pairs), 2 * LANES, 2 * LANES), jnp.bfloat16)],
-        (depth_psf, pays[-1]), [], 8, 1, scalars=1, unread=(1,),
+        (depth_psf, rest[-1]), [], 8, 1, scalars=1, unread=(1,),
     )
     stacks_x, stacks_y = stitch_width.shape[:2]
     weight, inv = call(
         functools.partial(norm_kernel, (cx, cy, hy, stacks_x, stacks_y)),
         [shape(wide, full, LANES), shape(tiles, cx, ceil_to(end1, 8), LANES)],
-        (place, stitch_width.reshape(-1), pays[-1], tx, ty), [(tiles, cx, full, LANES)], 10, 1, scalars=2, unread=(2,),
+        (place, stitch_width.reshape(-1), rest[-1], tx, ty), [(tiles, cx, full, LANES)], 10, 1, scalars=2, unread=(2,),
     )
     shift = 2 * reach
 

time: 105 us -> 104 us (level)
  Pallas kernels: 51.2 us -> 49.5 us
    pallas_call x10 -> x11, Pallas kernels: 51.2 us -> 49.5 us  [call(): pl.pallas_call(kernel, out_shape=out_shape, in_specs=[pl.BlockSpec(memory...]
    ppermute x2, waiting for transfers between devices: 6.18 us -> 4.68 us  [body(): parts.append(lax.ppermute(value, ('sy', 'gz'), both_ways(cross)))]
    ppermute x8, waiting for transfers between devices: 15 us -> 16.1 us  [swap(): got.append(lax.ppermute(pays[n], 'sx', rounds_x[n]))]
  transfers between devices with their start and end apart: 13 -> 13, of which waited for: 5 -> 6; matrix products, arithmetic and copies ran while one was open for 4% -> 4% of each run, Pallas kernels for 36% -> 35%
where the time goes in v8:
time: 104 us; the launch traced here: 102 us
  Pallas kernels  49.5 us (48%)
  starting transfers between devices  21.5 us (21%)
  waiting for transfers between devices  21.2 us (20%)
  local copies, waits for them, and re-layouts  8.55 us (8%)
    pallas_call x11, Pallas kernels, call(): pl.pallas_call(kernel, out_shape=out_shape, in_specs=[pl.BlockSpec(memory...  49.5 us
    ppermute x8, waiting for transfers between devices, swap(): got.append(lax.ppermute(pays[n], 'sx', rounds_x[n]))  16.1 us
    ppermute x8, starting transfers between devices, swap(): got.append(lax.ppermute(pays[n], 'sx', rounds_x[n]))  14.4 us
    ppermute x2, waiting for transfers between devices, body(): parts.append(lax.ppermute(value, ('sy', 'gz'), both_ways(cross)))  4.68 us
    unnamed x18, local copies, waits for them, and re-layouts  3.51 us
    ppermute x2, starting transfers between devices, body(): parts.append(lax.ppermute(value, ('sy', 'gz'), both_ways(cross)))  3.02 us
    ppermute x1, starting transfers between devices, body(): lax.ppermute(second, 'sy', both_ways(rounds_y[1]))  2.54 us
  transfers between devices with their start and end apart: 13, of which 6 were waited for; matrix products, arithmetic and copies ran while one was open for 4% of the time, Pallas kernels for 35%

profile of v8, /device:TPU:10, one launch (start us, length us, event | category | flops | bytes accessed | tf_op | source)
XLA Modules:
  0.0 101.8 jit_solution(3126362582345563023)
XLA Ops:
  0.0 1.9 %copy.26 = f32[256,16,128]{0,2,1:T(8,128)S(1)} copy(f32[256,16,128]{2,1,0:T(8,128)} %param.6) | data formatting | bytes 4194304 | tf_op args[0]
  3.2 2.5 %shard_map.64 = (f32[3,192,128]{2,1,0:T(8,128)}, f32[3,192,128]{2,1,0:T(8,128)}, f32[96,128]{1,0:T(8,128)}, f32[96,128]{1,0:T(8,128)}, f32[1032,128]{1,0:T(8,128)}) custom-call(s32[2]{0:T(128)S(1)} %pad_add_fusion.place_ref, f32[3,16,128,128]{3,2,1,0:T(8,128)S(1)} %maximum_bitcast_fusion.vol_ref.refs_0_, f32[8,128]{1,0:T(8,128)S(1)} %pad.9.refs_0_), custom_call_target="tpu_custom_call" | custom-call | flops 1 | bytes 4366344 | tf_op jit(solution)/shard_map/pallas_call | solution.py:548
  7.2 2.5 %collective-permute-start.1 = (f32[3,192,128]{2,1,0:T(8,128)}, f32[3,192,128]{2,1,0:T(8,128)}, u32[]{:S(2)}, u32[]{:S(2)}) collective-permute-start(f32[3,192,128]{2,1,0:T(8,128)} %get-tuple-element.30), channel_id=1, source_target_pairs={{2,4},{4,2},{3,5},{5,3},{10,12},{12,10},{11,13},{13,11},{18,20},{2... | collective-permute-start | bytes 884744 | tf_op jit(solution)/shard_map/ppermute | solution.py:572
  9.8 3.0 %collective-permute-start.4 = (f32[96,128]{1,0:T(8,128)}, f32[96,128]{1,0:T(8,128)S(1)}, u32[]{:S(2)}, u32[]{:S(2)}) collective-permute-start(f32[96,128]{1,0:T(8,128)} %get-tuple-element.33), channel_id=1, source_target_pairs={{2,5},{3,4},{5,2},{4,3},{10,13},{11,12},{13,10},{12,11},{18,21},{1... | collective-permute-start | bytes 147464 | tf_op jit(solution)/shard_map/ppermute | solution.py:576
  15.7 4.7 %collective-permute-done.3.refs_4_ = f32[96,128]{1,0:T(8,128)S(1)} collective-permute-done((f32[96,128]{1,0:T(8,128)}, f32[96,128]{1,0:T(8,128)S(1)}, u32[]{:S(2)}, u32[]{:S(2)}) %collective-permute-start.3) | collective-permute-done | bytes 49184 | tf_op jit(solution)/shard_map/ppermute | solution.py:576
  20.8 3.5 %shard_map.65 = (f32[3,16,160,128]{3,2,1,0:T(8,128)S(1)}, f32[15,96,128]{2,1,0:T(8,128)S(1)}, f32[15,96,128]{2,1,0:T(8,128)S(1)}) custom-call(s32[2]{0:T(128)S(1)} %pad_add_fusion.place_ref, f32[3,16,128,128]{3,2,1,0:T(8,128)S(1)} %maximum_bitcast_fusion.vol_ref.refs_0_, f32[3,192,128]{2,1,0:T(8,128)S(1)} %collective-permute-done.refs_1_, ...), custom_call_target="tpu_custom_call" | custom-call | flops 1 | bytes 9768968 | tf_op jit(solution)/shard_map/pallas_call | solution.py:548
  24.3 1.7 %shard_map.66 = (f32[15,56,128]{2,1,0:T(8,128)S(1)}, f32[15,56,128]{2,1,0:T(8,128)S(1)}) custom-call(s32[2]{0:T(128)S(1)} %pad_add_fusion.place_ref, f32[3,16,160,128]{3,2,1,0:T(8,128)S(1)} %get-tuple-element.34.ext_ref.est_ref.obs_ref.refs_0_), custom_call_target="tpu_custom_call" | custom-call | flops 1 | bytes 4792328 | tf_op jit(solution)/shard_map/pallas_call | solution.py:548
  26.0 3.5 %collective-permute-start.8 = (f32[15,56,128]{2,1,0:T(8,128)S(1)}, f32[15,56,128]{2,1,0:T(8,128)S(1)}, u32[]{:S(2)}, u32[]{:S(2)}) collective-permute-start(f32[15,56,128]{2,1,0:T(8,128)S(1)} %get-tuple-element.38._), channel_id=1, source_target_pairs={{8,16},{16,8},{9,17},{17,9},{10,18},{18,10},{11,19},{19,11},{12,20... | collective-permute-start | bytes 1290248 | tf_op jit(solution)/shard_map/ppermute | solution.py:626
  30.8 2.4 %collective-permute-start.6 = (f32[15,96,128]{2,1,0:T(8,128)S(1)}, f32[15,96,128]{2,1,0:T(8,128)S(1)}, u32[]{:S(2)}, u32[]{:S(2)}) collective-permute-start(f32[15,96,128]{2,1,0:T(8,128)S(1)} %get-tuple-element.36), channel_id=1, source_target_pairs={{8,16},{16,8},{9,17},{17,9},{10,18},{18,10},{11,19},{19,11},{12,20... | collective-permute-start | bytes 2211848 | tf_op jit(solution)/shard_map/ppermute | solution.py:626
  34.6 4.9 %shard_map.67 = (f32[22,160,128]{2,1,0:T(8,128)S(1)}, f32[3,16,144,128]{3,2,1,0:T(8,128)S(1)}) custom-call(s32[2]{0:T(128)S(1)} %pad_add_fusion.place_ref, s32[32]{0:T(128)S(1)} %reshape.62.bands_ref, f32[15,56,128]{2,1,0:T(8,128)S(1)} %get-tuple-element.38._, f32[3,7,8,128]{3,2,1,0:T(8,128)S(1)} %broadcast_in_dim.17.tx_ref.refs_6_.refs_8_.refs_9_.refs_11_, ...), custom_call_target="tpu_custom_call" | custom-call | flops 1 | bytes 5943432 | tf_op jit(solution)/shard_map/pallas_call | solution.py:548
  39.5 4.0 %shard_map.69.refs_4_.refs_7_ = f32[3,10,152,128]{3,2,1,0:T(8,128)S(1)} custom-call(f32[3,16,160,128]{3,2,1,0:T(8,128)S(1)} %get-tuple-element.34.ext_ref.est_ref.obs_ref.refs_0_, f32[3,16,160,128]{3,2,1,0:T(8,128)S(1)} %get-tuple-element.34.ext_ref.est_ref.obs_ref.refs_0_, f32[22,160,128]{2,1,0:T(8,128)S(1)} %get-tuple-element.39.w_ref.refs_3_.refs_5_, ...), custom_call_target="tpu_custom_call" | custom-call | flops 1 | bytes 12959744 | tf_op jit(solution)/shard_map/pallas_call | solution.py:548
  43.5 6.6 %collective-permute-done.5.refs_1_ = f32[15,96,128]{2,1,0:T(8,128)S(1)} collective-permute-done((f32[15,96,128]{2,1,0:T(8,128)S(1)}, f32[15,96,128]{2,1,0:T(8,128)S(1)}, u32[]{:S(2)}, u32[]{:S(2)}) %collective-permute-start.5) | collective-permute-done | bytes 737312 | tf_op jit(solution)/shard_map/ppermute | solution.py:626
  50.1 5.6 %collective-permute-done.6.refs_2_ = f32[15,96,128]{2,1,0:T(8,128)S(1)} collective-permute-done((f32[15,96,128]{2,1,0:T(8,128)S(1)}, f32[15,96,128]{2,1,0:T(8,128)S(1)}, u32[]{:S(2)}, u32[]{:S(2)}) %collective-permute-start.6) | collective-permute-done | bytes 737312 | tf_op jit(solution)/shard_map/ppermute | solution.py:626
  55.8 8.1 %shard_map.70 = (f32[3,16,80,128]{3,2,1,0:T(8,128)S(1)}, f32[3,12,96,128]{3,2,1,0:T(8,128)S(1)}, f32[15,80,128]{2,1,0:T(8,128)S(1)}, f32[15,80,128]{2,1,0:T(8,128)S(1)}) custom-call(s32[2]{0:T(128)S(1)} %pad_add_fusion.place_ref, f32[3,16,160,128]{3,2,1,0:T(8,128)S(1)} %get-tuple-element.34.ext_ref.est_ref.obs_ref.refs_0_, ...), custom_call_target="tpu_custom_call" | custom-call | flops 1 | bytes 19177480 | tf_op jit(solution)/shard_map/pallas_call | solution.py:548
  63.9 3.7 %collective-permute-start.10 = (f32[15,80,128]{2,1,0:T(8,128)S(1)}, f32[15,80,128]{2,1,0:T(8,128)S(1)}, u32[]{:S(2)}, u32[]{:S(2)}) collective-permute-start(f32[15,80,128]{2,1,0:T(8,128)S(1)} %get-tuple-element.47), channel_id=1, source_target_pairs={{8,16},{16,8},{9,17},{17,9},{10,18},{18,10},{11,19},{19,11},{12,20... | collective-permute-start | bytes 1843208 | tf_op jit(solution)/shard_map/ppermute | solution.py:626
  67.7 7.1 %shard_map.71 = (f32[3,16,144,128]{3,2,1,0:T(8,128)S(1)}, f32[3,12,88,128]{3,2,1,0:T(8,128)S(1)}, f32[15,64,128]{2,1,0:T(8,128)S(1)}, f32[15,64,128]{2,1,0:T(8,128)S(1)}) custom-call(s32[2]{0:T(128)S(1)} %pad_add_fusion.place_ref, f32[3,16,160,128]{3,2,1,0:T(8,128)S(1)} %get-tuple-element.34.ext_ref.est_ref.obs_ref.refs_0_, ...), custom_call_target="tpu_custom_call" | custom-call | flops 1 | bytes 23183368 | tf_op jit(solution)/shard_map/pallas_call | solution.py:548
  74.7 2.0 %collective-permute-start.11 = (f32[15,64,128]{2,1,0:T(8,128)S(1)}, f32[15,64,128]{2,1,0:T(8,128)S(1)}, u32[]{:S(2)}, u32[]{:S(2)}) collective-permute-start(f32[15,64,128]{2,1,0:T(8,128)S(1)} %get-tuple-element.50), channel_id=1, source_target_pairs={{0,8},{16,24},{8,0},{24,16},{1,9},{17,25},{9,1},{25,17},{2,10},{18... | collective-permute-start | bytes 1474568 | tf_op jit(solution)/shard_map/ppermute | solution.py:626
  76.8 2.3 %collective-permute-start.12 = (f32[15,64,128]{2,1,0:T(8,128)S(1)}, f32[15,64,128]{2,1,0:T(8,128)S(1)}, u32[]{:S(2)}, u32[]{:S(2)}) collective-permute-start(f32[15,64,128]{2,1,0:T(8,128)S(1)} %get-tuple-element.51), channel_id=1, source_target_pairs={{8,16},{16,8},{9,17},{17,9},{10,18},{18,10},{11,19},{19,11},{12,20... | collective-permute-start | bytes 1474568 | tf_op jit(solution)/shard_map/ppermute | solution.py:626
  79.2 3.5 %shard_map.72.refs_4_.refs_6_ = f32[2,10,136,128]{3,2,1,0:T(8,128)S(1)} custom-call(f32[3,16,144,128]{3,2,1,0:T(8,128)S(1)} %get-tuple-element.45.est_ref.refs_0_, f32[3,16,160,128]{3,2,1,0:T(8,128)S(1)} %get-tuple-element.34.ext_ref.est_ref.obs_ref.refs_0_, f32[22,160,128]{2,1,0:T(8,128)S(1)} %get-tuple-element.39.w_ref.refs_3_.refs_5_, ...), custom_call_target="tpu_custom_call" | custom-call | flops 1 | bytes 12148736 | tf_op jit(solution)/shard_map/pallas_call | solution.py:548
  82.7 1.7 %collective-permute-done.9.refs_1_ = f32[15,80,128]{2,1,0:T(8,128)S(1)} collective-permute-done((f32[15,80,128]{2,1,0:T(8,128)S(1)}, f32[15,80,128]{2,1,0:T(8,128)S(1)}, u32[]{:S(2)}, u32[]{:S(2)}) %collective-permute-start.9) | collective-permute-done | bytes 614432 | tf_op jit(solution)/shard_map/ppermute | solution.py:626
  84.4 6.5 %shard_map.73 = f32[2,16,64,128]{3,2,1,0:T(8,128)S(1)} custom-call(s32[2]{0:T(128)S(1)} %pad_add_fusion.place_ref, f32[3,16,144,128]{3,2,1,0:T(8,128)S(1)} %get-tuple-element.45.est_ref.refs_0_, f32[15,80,128]{2,1,0:T(8,128)S(1)} %collective-permute-done.9.refs_1_, f32[15,80,128]{2,1,0:T(8,128)S(1)} %collective-permute-done.10.refs_2_, ...), custom_call_target="tpu_custom_call" | custom-call | flops 1 | bytes 14114824 | tf_op jit(solution)/shard_map/pallas_call | solution.py:548
  90.9 2.1 %collective-permute-done.11.refs_3_ = f32[15,64,128]{2,1,0:T(8,128)S(1)} collective-permute-done((f32[15,64,128]{2,1,0:T(8,128)S(1)}, f32[15,64,128]{2,1,0:T(8,128)S(1)}, u32[]{:S(2)}, u32[]{:S(2)}) %collective-permute-start.11) | collective-permute-done | bytes 491552 | tf_op jit(solution)/shard_map/ppermute | solution.py:626
  93.1 6.6 %shard_map.74 = f32[2,16,64,128]{3,2,1,0:T(8,128)S(1)} custom-call(s32[2]{0:T(128)S(1)} %pad_add_fusion.place_ref, f32[3,16,144,128]{3,2,1,0:T(8,128)S(1)} %get-tuple-element.45.est_ref.refs_0_, f32[15,80,128]{2,1,0:T(8,128)S(1)} %collective-permute-done.9.refs_1_, f32[15,80,128]{2,1,0:T(8,128)S(1)} %collective-permute-done.10.refs_2_, ...), custom_call_target="tpu_custom_call" | custom-call | flops 1 | bytes 14950408 | tf_op jit(solution)/shard_map/pallas_call | solution.py:548
  99.9 2.0 %copy.35 = f32[2,128,16,128]{3,2,1,0:T(8,128)} copy(f32[2,128,16,128]{1,3,2,0:T(8,128)S(1)} %maximum_bitcast_fusion.1) | data formatting | bytes 4194304 | tf_op jit(solution)/shard_map/transpose | solution.py:703
  (54 shorter events, 9.2 us)
Async XLA Ops:
  1.9 0.9 copy-start.5
  2.8 9.9 %copy-start.1 = (f32[256]{0:T(256)}, f32[256]{0:T(256)S(1)}, u32[]{:S(2)}) copy-start(f32[256]{0:T(256)S(1)} %get-tuple-element.64) | copy-start | bytes 3076
  3.1 10.2 %copy-start.4 = (f32[8,7]{1,0:T(8,128)S(1)}, f32[8,7]{1,0:T(8,128)}, u32[]{:S(2)}) copy-start(f32[8,7]{1,0:T(8,128)} %param.8) | copy-start | bytes 676
  3.2 11.0 %copy-start.3 = (s32[4,4,2]{1,2,0:T(2,128)S(1)}, s32[4,4,2]{1,2,0:T(2,128)}, u32[]{:S(2)}) copy-start(s32[4,4,2]{1,2,0:T(2,128)} %param.11) | copy-start | bytes 388
  5.7 15.1 %collective-permute-start.2 = (f32[1032,128]{1,0:T(8,128)}, f32[1032,128]{1,0:T(8,128)}, u32[]{:S(2)}, u32[]{:S(2)}) collective-permute-start(f32[1032,128]{1,0:T(8,128)} %get-tuple-element.31), channel_id=1, source_target_pairs={{0,1},{1,0},{2,3},{3,2},{4,5},{5,4},{6,7},{7,6},{8,9},{9,8},{10,11... | collective-permute-start | bytes 1585160 | tf_op jit(solution)/shard_map/ppermute | solution.py:571
  7.2 13.2 %collective-permute-start = (f32[3,192,128]{2,1,0:T(8,128)}, f32[3,192,128]{2,1,0:T(8,128)S(1)}, u32[]{:S(2)}, u32[]{:S(2)}) collective-permute-start(f32[3,192,128]{2,1,0:T(8,128)} %get-tuple-element.29), channel_id=1, source_target_pairs={{0,2},{4,6},{2,0},{6,4},{1,3},{5,7},{3,1},{7,5},{8,10},{12,14},{10... | collective-permute-start | bytes 884744 | tf_op jit(solution)/shard_map/ppermute | solution.py:572
  7.2 13.2 %collective-permute-start.1 = (f32[3,192,128]{2,1,0:T(8,128)}, f32[3,192,128]{2,1,0:T(8,128)}, u32[]{:S(2)}, u32[]{:S(2)}) collective-permute-start(f32[3,192,128]{2,1,0:T(8,128)} %get-tuple-element.30), channel_id=1, source_target_pairs={{2,4},{4,2},{3,5},{5,3},{10,12},{12,10},{11,13},{13,11},{18,20},{2... | collective-permute-start | bytes 884744 | tf_op jit(solution)/shard_map/ppermute | solution.py:572
  9.7 10.6 %collective-permute-start.3 = (f32[96,128]{1,0:T(8,128)}, f32[96,128]{1,0:T(8,128)S(1)}, u32[]{:S(2)}, u32[]{:S(2)}) collective-permute-start(f32[96,128]{1,0:T(8,128)} %get-tuple-element.32), channel_id=1, source_target_pairs={{0,3},{1,2},{4,7},{5,6},{3,0},{2,1},{7,4},{6,5},{8,11},{9,10},{12,... | collective-permute-start | bytes 147464 | tf_op jit(solution)/shard_map/ppermute | solution.py:576
  9.8 10.5 %collective-permute-start.4 = (f32[96,128]{1,0:T(8,128)}, f32[96,128]{1,0:T(8,128)S(1)}, u32[]{:S(2)}, u32[]{:S(2)}) collective-permute-start(f32[96,128]{1,0:T(8,128)} %get-tuple-element.33), channel_id=1, source_target_pairs={{2,5},{3,4},{5,2},{4,3},{10,13},{11,12},{13,10},{12,11},{18,21},{1... | collective-permute-start | bytes 147464 | tf_op jit(solution)/shard_map/ppermute | solution.py:576
  24.3 5.2 %copy-start = (f32[17]{0:T(128)S(1)}, f32[17]{0:T(128)}, u32[]{:S(2)}) copy-start(f32[17]{0:T(128)} %psf_ref.1) | copy-start | bytes 208
  24.3 9.6 %copy-start.2 = (f32[256]{0:T(256)S(1)}, f32[256]{0:T(256)}, u32[]{:S(2)}) copy-start(f32[256]{0:T(256)} %copy-done.1) | copy-start | bytes 3076
  24.3 10.1 %copy-start.6 = (f32[128]{0:T(128)S(1)}, f32[128]{0:T(128)}, u32[]{:S(2)}) copy-start(f32[128]{0:T(128)} %slice.42) | copy-start | bytes 1540
  26.0 41.7 %collective-permute-start.8 = (f32[15,56,128]{2,1,0:T(8,128)S(1)}, f32[15,56,128]{2,1,0:T(8,128)S(1)}, u32[]{:S(2)}, u32[]{:S(2)}) collective-permute-start(f32[15,56,128]{2,1,0:T(8,128)S(1)} %get-tuple-element.38._), channel_id=1, source_target_pairs={{8,16},{16,8},{9,17},{17,9},{10,18},{18,10},{11,19},{19,11},{12,20... | collective-permute-start | bytes 1290248 | tf_op jit(solution)/shard_map/ppermute | solution.py:626
  30.7 19.4 %collective-permute-start.5 = (f32[15,96,128]{2,1,0:T(8,128)S(1)}, f32[15,96,128]{2,1,0:T(8,128)S(1)}, u32[]{:S(2)}, u32[]{:S(2)}) collective-permute-start(f32[15,96,128]{2,1,0:T(8,128)S(1)} %get-tuple-element.35), channel_id=1, source_target_pairs={{0,8},{16,24},{8,0},{24,16},{1,9},{17,25},{9,1},{25,17},{2,10},{18... | collective-permute-start | bytes 2211848 | tf_op jit(solution)/shard_map/ppermute | solution.py:626
  30.8 25.0 %collective-permute-start.6 = (f32[15,96,128]{2,1,0:T(8,128)S(1)}, f32[15,96,128]{2,1,0:T(8,128)S(1)}, u32[]{:S(2)}, u32[]{:S(2)}) collective-permute-start(f32[15,96,128]{2,1,0:T(8,128)S(1)} %get-tuple-element.36), channel_id=1, source_target_pairs={{8,16},{16,8},{9,17},{17,9},{10,18},{18,10},{11,19},{19,11},{12,20... | collective-permute-start | bytes 2211848 | tf_op jit(solution)/shard_map/ppermute | solution.py:626
  34.0 33.6 %collective-permute-start.7 = (f32[15,56,128]{2,1,0:T(8,128)S(1)}, f32[15,56,128]{2,1,0:T(8,128)S(1)}, u32[]{:S(2)}, u32[]{:S(2)}) collective-permute-start(f32[15,56,128]{2,1,0:T(8,128)S(1)} %get-tuple-element.37), channel_id=1, source_target_pairs={{0,8},{16,24},{8,0},{24,16},{1,9},{17,25},{9,1},{25,17},{2,10},{18... | collective-permute-start | bytes 1290248 | tf_op jit(solution)/shard_map/ppermute | solution.py:626
  63.9 18.8 %collective-permute-start.10 = (f32[15,80,128]{2,1,0:T(8,128)S(1)}, f32[15,80,128]{2,1,0:T(8,128)S(1)}, u32[]{:S(2)}, u32[]{:S(2)}) collective-permute-start(f32[15,80,128]{2,1,0:T(8,128)S(1)} %get-tuple-element.47), channel_id=1, source_target_pairs={{8,16},{16,8},{9,17},{17,9},{10,18},{18,10},{11,19},{19,11},{12,20... | collective-permute-start | bytes 1843208 | tf_op jit(solution)/shard_map/ppermute | solution.py:626
  67.6 16.8 %collective-permute-start.9 = (f32[15,80,128]{2,1,0:T(8,128)S(1)}, f32[15,80,128]{2,1,0:T(8,128)S(1)}, u32[]{:S(2)}, u32[]{:S(2)}) collective-permute-start(f32[15,80,128]{2,1,0:T(8,128)S(1)} %get-tuple-element.46), channel_id=1, source_target_pairs={{0,8},{16,24},{8,0},{24,16},{1,9},{17,25},{9,1},{25,17},{2,10},{18... | collective-permute-start | bytes 1843208 | tf_op jit(solution)/shard_map/ppermute | solution.py:626
  74.7 18.3 %collective-permute-start.11 = (f32[15,64,128]{2,1,0:T(8,128)S(1)}, f32[15,64,128]{2,1,0:T(8,128)S(1)}, u32[]{:S(2)}, u32[]{:S(2)}) collective-permute-start(f32[15,64,128]{2,1,0:T(8,128)S(1)} %get-tuple-element.50), channel_id=1, source_target_pairs={{0,8},{16,24},{8,0},{24,16},{1,9},{17,25},{9,1},{25,17},{2,10},{18... | collective-permute-start | bytes 1474568 | tf_op jit(solution)/shard_map/ppermute | solution.py:626
  76.8 16.3 %collective-permute-start.12 = (f32[15,64,128]{2,1,0:T(8,128)S(1)}, f32[15,64,128]{2,1,0:T(8,128)S(1)}, u32[]{:S(2)}, u32[]{:S(2)}) collective-permute-start(f32[15,64,128]{2,1,0:T(8,128)S(1)} %get-tuple-element.51), channel_id=1, source_target_pairs={{8,16},{16,8},{9,17},{17,9},{10,18},{18,10},{11,19},{19,11},{12,20... | collective-permute-start | bytes 1474568 | tf_op jit(solution)/shard_map/ppermute | solution.py:626
